TPU v7x, 32 devices: a whole 2x2x4 slice. The times are simulated.
32 devices in a mesh: grp: 2 (over y), row: 4 (over x, core), col: 4 (over z).
Axes of the slice: x: 2, y: 2, z: 4, core: 2. Of those that a mesh axis runs over, the one named last changes fastest.
Arguments:
- features: bfloat16 [32, 1024, 1024], P(None, ('grp', 'row'), 'col'), parts along dimension 1, may hold values from -6 to 6
- conv_weight: bfloat16 [32, 3, 3], replicated, may hold values from -0.375 to 0.375
- row_taps: float32 [8, 2, 33], replicated, may hold values from -1 to 1
- col_taps: float32 [8, 2, 33], replicated, may hold values from -1 to 1
- kernel_weight: float32 [8], replicated, may hold values from 0.1 to 1
- target: float32 [1024, 1024], P(('grp', 'row'), 'col'), parts along dimension 0, may hold values from 0 to 1
- block_list: int32 [8, 4, 8], P(('grp', 'row'), 'col'), parts along dimension 0, may hold values from 0 to 8, as said below
Outputs:
- grad_weight: float32 [64, 3, 3], P('grp'), parts along dimension 0
- grad_features: bfloat16 [32, 1024, 1024], P(None, ('grp', 'row'), 'col'), parts along dimension 1
There are 2 independent parts, one for each index of `grp`. A program takes and returns all parts, laid end to end along the dimension named above; an argument that names none is the same for every part. Nothing has to cross between parts.
Inputs may be any that keep to these rules, and one draw needn't show every extreme that they name: `block_list`: each tile's entry lists its occupied blocks in increasing order, then entries equal to 8; every tile has at least one occupied block, and in every draw some tile has all 8 occupied.
All inputs are finite; a program needn't handle non-finite values.
Results may differ from a plain program's by a relative error of at most 0.0004.
Values may be sent and summed in bfloat16 or wider, within the bound.
No kernel may reach another device: no remote copies, remote signals or barrier semaphores. Data moves between devices by JAX's collectives and lax.ppermute only.
A program may use at most 128 MiB of HBM per device.

v0:
```python
import functools
import math

import jax
import jax.numpy as jnp
from jax import lax
from jax.experimental import pallas as pl
from jax.experimental.pallas import tpu as pltpu
from jax.sharding import PartitionSpec as P

BLOCK = 64
ROWS = 16
WIN = 32
MIB = 1 << 20
F32 = jnp.float32
BF16 = jnp.bfloat16


def up(value, multiple):
    return -(-value // multiple) * multiple


def iota(shape, dim):
    return lax.broadcasted_iota(jnp.int32, shape, dim)


def split(value):
    high = value.astype(BF16)
    return high, (value - high.astype(F32)).astype(BF16)


def dot(left, right, dims=((1,), (0,)), precision=None):
    return lax.dot_general(
        left, right, (dims, ((), ())), precision=precision, preferred_element_type=F32
    )


NT = ((1,), (1,))


class Sizes:
    def __init__(self, channels, tile_rows, tile_cols, taps, filters):
        self.channels, self.rows, self.cols = channels, tile_rows, tile_cols
        self.taps, self.filters = taps, filters
        self.half = (taps - 1) // 2
        self.mask_halo = 2 * self.half + 1
        self.field_halo = self.half + 1
        self.strip = self.mask_halo + 1
        self.base = self.mask_halo - 1
        self.width = up(tile_cols + 2 * self.mask_halo, 128)
        self.field_rows = tile_rows + 2 * self.field_halo
        self.field_cols = tile_cols + 2 * self.field_halo
        self.field_pad = up(self.field_rows, 16)
        self.grad_pad = tile_rows + ROWS
        mask_rows = tile_rows + 2 * self.mask_halo
        self.depth = up(max(mask_rows, self.field_pad + taps), 128)
        self.steps = tile_rows // ROWS
        self.strip_rows = up(self.strip + 1 + self.field_halo, 8)
        self.fold = self.grad_pad // 2


def band_kernel(s, row_taps, col_taps, kernel_weight, row_high, row_low, col_fwd, col_adj, adj_high, adj_low, flipped):
    for f in range(s.filters):
        k, p = f // 2, f % 2
        pad = jnp.zeros((1, s.depth - s.taps), F32)
        row = jnp.concatenate([row_taps[k, p : p + 1, :], pad], 1)
        col = jnp.concatenate([col_taps[k, p : p + 1, :], pad], 1)
        band = pltpu.roll(
            jnp.broadcast_to(row, (s.field_pad, s.depth)), 0, 1, stride=1, stride_axis=0
        )
        row_high[f], row_low[f] = split(band)
        turned = pltpu.roll(
            jnp.broadcast_to(row * (2.0 * kernel_weight[k]), (s.field_pad, s.depth)),
            s.depth - (s.taps - 1),
            1,
            stride=1,
            stride_axis=0,
        )
        flipped[f * s.field_pad : (f + 1) * s.field_pad, :] = turned
        wide = col[:, :256]
        band = pltpu.roll(jnp.broadcast_to(wide, (128, 256)), 0, 1, stride=1, stride_axis=0)
        col_fwd[f, :128, :], col_fwd[f, 128:, :] = split(band)
        band = pltpu.roll(
            jnp.broadcast_to(wide, (256, 256)), 256 - (s.taps - 1), 1, stride=1, stride_axis=0
        )
        col_adj[f, :, :128], col_adj[f, :, 128:] = split(band[:, :128])
    turned = flipped[...].T[: s.grad_pad, :]
    adj_high[...], adj_low[...] = split(turned)


def edge_kernel(s, listed, features, conv_weight, target, table, partial, left_out, right_out, acc):
    lanes = 6 * WIN
    u, lane = iota((ROWS, 256), 0), iota((ROWS, 256), 1)
    h, b = lane % WIN, (lane // WIN) % 3
    taps = conv_weight[...].astype(F32)
    total = jnp.zeros((s.channels, ROWS, 256), F32)
    for row_shift in range(3):
        for col_shift in range(3):
            hit = (h == u - row_shift + 2) & (b == col_shift) & (lane < lanes)
            total += taps[:, row_shift : row_shift + 1, col_shift : col_shift + 1] * jnp.where(
                hit, 1.0, 0.0
            )
    flat = total.reshape(s.channels * ROWS, 256)
    table[...] = flat.astype(BF16)
    left = flat[:, :128].T[: 3 * WIN].astype(BF16)
    acc[...] = jnp.zeros_like(acc)
    for k in range(s.steps):
        block = features[:, k * ROWS : (k + 1) * ROWS, :].reshape(s.channels * ROWS, s.cols)
        sums = dot(left, block)
        for b in range(3):
            acc[b, k * ROWS : k * ROWS + WIN, :] += sums[b * WIN : (b + 1) * WIN]
    whole = jnp.zeros((s.grad_pad, s.width), F32)
    blank = jnp.zeros((s.grad_pad, s.width - s.cols), F32)
    for b in range(3):
        part = jnp.concatenate([acc[b, : s.grad_pad], blank], 1)
        whole += pltpu.roll(part, s.base + 2 - b, 1)
    partial[...] = whole

    place, row = iota((s.grad_pad, 128), 1), iota((s.grad_pad, 128), 0)
    aim = jnp.concatenate([target[...], jnp.zeros((s.grad_pad - s.rows, s.cols), F32)], 0)
    aim = jnp.concatenate([aim, jnp.zeros((s.grad_pad, s.width - s.cols), F32)], 1)
    across = s.cols // BLOCK
    for out, first, first_aim, block_col in (
        (left_out, s.base, 0, 0),
        (right_out, s.cols, s.cols - s.field_halo, across - 1),
    ):
        logits = pltpu.roll(whole, (s.width - first) % s.width, 1)[:, :128]
        wanted = pltpu.roll(aim, (s.width - first_aim + s.strip) % s.width, 1)[:, :128]
        number = (row // BLOCK) * across + block_col
        used = jnp.zeros((s.grad_pad, 128), F32)
        for n in range(listed.shape[2]):
            used = jnp.where(number == listed[0, 0, n], 1.0, used)
        used = jnp.where(row < s.rows, used, 0.0)
        value = jnp.where(place < s.strip, logits, wanted)
        value = jnp.where(place < s.strip + s.field_halo, value, used)
        value = jnp.where(place < s.strip + s.field_halo + 1, value, 0.0)
        out[...] = jnp.where(
            iota((s.fold, 128), 1) < 64, value[: s.fold], pltpu.roll(value[s.fold :], 64, 1)
        )


def unfolded(s, ref):
    value = ref[...]
    low = iota((s.fold, 128), 1) < 64
    return jnp.concatenate(
        [jnp.where(low, value, 0.0), jnp.where(low, pltpu.roll(value, 64, 1), 0.0)], 0
    )


def middle_kernel(s, sides, listed, partial, target, from_left, from_right, logits, aim, occupied, up_out, down_out):
    extra = jnp.zeros((s.grad_pad, s.width - 128), F32)
    lane = iota((s.grad_pad, 128), 1)
    has_left, has_right = sides[0], sides[1]
    west = jnp.where(has_left > 0, unfolded(s, from_left), 0.0)
    east = jnp.where(has_right > 0, unfolded(s, from_right), 0.0)

    def placed(value, keep_from, keep, offset):
        kept = jnp.where((lane >= keep_from) & (lane < keep_from + keep), value, 0.0)
        wide = jnp.concatenate([kept, extra], 1)
        return pltpu.roll(wide, (offset - keep_from) % s.width, 1)

    whole = partial[...] + placed(west, 0, s.strip, 0)
    whole += placed(east, 0, s.strip, s.cols + s.base)
    logits[...] = whole
    own = jnp.concatenate([target[...], jnp.zeros((s.rows, s.width - s.cols), F32)], 1)
    aims = pltpu.roll(own, s.field_halo, 1)
    aims += placed(west, s.strip, s.field_halo, 0)[: s.rows]
    aims += placed(east, s.strip, s.field_halo, s.cols + s.field_halo)[: s.rows]
    aim[...] = aims

    across, down = s.cols // BLOCK, s.rows // BLOCK
    row, col = iota((8, s.width), 0), iota((8, s.width), 1) - s.mask_halo
    inside = (col >= 0) & (col < s.cols) & (row < down)
    number = jnp.where(inside, row * across + (col + BLOCK) // BLOCK - 1, -1)
    used = jnp.zeros((8, s.width), F32)
    for n in range(listed.shape[2]):
        used = jnp.where(number == listed[0, 0, n], 1.0, used)
    flag = s.strip + s.field_halo
    for r in range(down):
        here = row == r
        used = jnp.where(here & (col < 0), west[r * BLOCK : r * BLOCK + 1, flag : flag + 1], used)
        beyond = here & (col >= s.cols) & (col < s.cols + s.mask_halo)
        used = jnp.where(beyond, east[r * BLOCK : r * BLOCK + 1, flag : flag + 1], used)
    occupied[...] = used

    for out, first, first_aim, block_row in (
        (up_out, 0, 0, 0),
        (down_out, s.rows + 2 - s.strip, s.rows - s.field_halo, down - 1),
    ):
        out[...] = jnp.zeros_like(out)
        out[: s.strip, :] = whole[first : first + s.strip]
        out[s.strip : s.strip + 1, :] = used[block_row : block_row + 1]
        out[s.strip + 1 : s.strip + 1 + s.field_halo, :] = aims[first_aim : first_aim + s.field_halo]


def optics_kernel(
    s, sides, weights, logits, aim, occupied, from_up, from_down, row_high, row_low, col_fwd, col_adj,
    adj_high, adj_low, features, shifted, terms,
    ext, aims, mask_high, mask_low, row_field, field, pulled_high, pulled_low, total,
    v_row_high, v_row_low, v_fwd, v_adj, v_adj_high, v_adj_low, v_features, sems,
):
    pairs = (
        (row_high, v_row_high), (row_low, v_row_low), (col_fwd, v_fwd), (col_adj, v_adj),
        (adj_high, v_adj_high), (adj_low, v_adj_low), (features, v_features),
    )
    copies = [pltpu.make_async_copy(a, b, sems.at[i]) for i, (a, b) in enumerate(pairs)]
    for copy in copies:
        copy.start()

    north = jnp.where(sides[2] > 0, from_up[...], 0.0)
    south = jnp.where(sides[3] > 0, from_down[...], 0.0)
    edge = up(s.strip, 8)
    lane_row = iota((edge, s.width), 0)
    ext[...] = jnp.zeros_like(ext)
    ext[s.base : s.base + s.grad_pad, :] = logits[...]
    ext[:edge, :] += jnp.where(lane_row < s.strip, north[:edge], 0.0)
    low = s.rows + s.base
    ext[low : low + edge, :] += jnp.where(lane_row < s.strip, south[:edge], 0.0)
    aims[...] = jnp.zeros_like(aims)
    aims[: s.field_halo, :] = north[s.strip + 1 : s.strip + 1 + s.field_halo]
    aims[s.field_halo : s.field_halo + s.rows, :] = aim[...]
    aims[s.field_halo + s.rows : s.field_rows, :] = south[s.strip + 1 : s.strip + 1 + s.field_halo]

    place = iota((s.depth, s.width), 0) - s.mask_halo
    used = jnp.where(place < 0, north[s.strip : s.strip + 1], 0.0)
    for r in range(s.rows // BLOCK):
        used = jnp.where((place >= r * BLOCK) & (place < (r + 1) * BLOCK), occupied[r : r + 1, :], used)
    below = (place >= s.rows) & (place < s.rows + s.mask_halo)
    used = jnp.where(below, south[s.strip : s.strip + 1], used)
    sigma = jax.nn.sigmoid(ext[...])
    mask = used * sigma
    mask_high[...], mask_low[...] = split(mask)
    slope = (mask * (1.0 - sigma))[s.base : s.base + s.grad_pad]
    slope = pltpu.roll(slope, s.width - s.base, 1)

    blocks = -(-s.field_cols // 128)
    total[...] = jnp.zeros_like(total)
    for copy in copies[:3]:
        copy.wait()

    def forward(f, carry):
        high, low = v_row_high[f], v_row_low[f]
        rowed = dot(high, mask_high[...]) + dot(high, mask_low[...]) + dot(low, mask_high[...])
        rowed_high, rowed_low = split(rowed)
        weight = weights[f // 2]
        for n in range(blocks):
            end = min(128 * n + 256, s.width)
            band = v_fwd[f][:, : end - 128 * n]
            both = dot(rowed_high[:, 128 * n : end], band, NT) + dot(rowed_low[:, 128 * n : end], band, NT)
            value = both[:, :128] + both[:, 128:]
            field[f, :, 128 * n : 128 * (n + 1)] = value
            total[:, 128 * n : 128 * (n + 1)] += weight * (value * value)
        return carry

    lax.fori_loop(0, s.filters, forward, 0)

    row, col = iota((s.field_pad, s.width), 0) - s.field_halo, iota((s.field_pad, s.width), 1) - s.field_halo
    inside = ((row >= 0) | (sides[2] > 0)) & ((row < s.rows) | (sides[3] > 0)) & (row < s.rows + s.field_halo)
    inside &= ((col >= 0) | (sides[0] > 0)) & ((col < s.cols) | (sides[1] > 0)) & (col < s.cols + s.field_halo)
    total[...] = jnp.where(inside, total[...] - aims[...], 0.0)
    copies[3].wait()
    out_blocks = -(-(s.cols + 2) // 128)
    if blocks * 128 < s.width:
        field[:, :, blocks * 128 :] = jnp.zeros_like(field[:, :, blocks * 128 :])

    def backward(f, carry):
        high, low = split(total[...] * field[f])
        start = pl.multiple_of(f * s.field_pad, 16)
        for n in range(out_blocks):
            end = min(128 * n + 256, s.width)
            band = v_adj[f][: end - 128 * n, :]
            both = dot(high[:, 128 * n : end], band) + dot(low[:, 128 * n : end], band)
            value = both[:, :128] + both[:, 128:]
            a, b = split(value)
            pulled_high[pl.ds(start, s.field_pad), 128 * n : 128 * (n + 1)] = a
            pulled_low[pl.ds(start, s.field_pad), 128 * n : 128 * (n + 1)] = b
        return carry

    lax.fori_loop(0, s.filters, backward, 0)
    if out_blocks * 128 < s.width:
        pulled_high[:, out_blocks * 128 :] = jnp.zeros_like(pulled_high[:, out_blocks * 128 :])
        pulled_low[:, out_blocks * 128 :] = jnp.zeros_like(pulled_low[:, out_blocks * 128 :])
    for copy in copies[4:6]:
        copy.wait()
    grad = dot(v_adj_high[...], pulled_high[...]) + dot(v_adj_high[...], pulled_low[...])
    grad = (grad + dot(v_adj_low[...], pulled_high[...])) * slope

    for b in range(3):
        moved = grad if b == 2 else pltpu.roll(grad, s.width - (2 - b), 1)
        shifted[b], shifted[3 + b] = split(moved[:, : s.cols])
    copies[6].wait()
    sums = jnp.zeros((s.channels * ROWS, 6 * WIN), F32)
    for k in range(s.steps):
        block = v_features[:, k * ROWS : (k + 1) * ROWS, :].reshape(s.channels * ROWS, s.cols)
        window = jnp.concatenate([shifted[q, k * ROWS : k * ROWS + WIN, :] for q in range(6)], 0)
        sums += dot(block, window, NT)
    cube = sums.reshape(s.channels, ROWS, 6 * WIN)
    u, lane = iota((ROWS, 6 * WIN), 0), iota((ROWS, 6 * WIN), 1)
    number, group = iota((16, 6 * WIN), 0), (iota((16, 6 * WIN), 1) // WIN) % 3
    result = jnp.zeros((16, s.channels), F32)
    for a in range(3):
        hit = jnp.where(lane % WIN == u - a + 2, 1.0, 0.0)
        line = (cube * hit[None]).sum(1)
        pick = jnp.where(number == a * 3 + group, 1.0, 0.0)
        result += dot(pick, line, NT, lax.Precision.HIGHEST)
    terms[...] = result


def feature_kernel(s, table, shifted, out):
    k = pl.program_id(0)
    start = pl.multiple_of(k * ROWS, ROWS)
    window = jnp.concatenate([shifted[q, pl.ds(start, WIN), :] for q in range(6)], 0)
    value = dot(table[:, : 6 * WIN], window)
    out[...] = value.astype(BF16).reshape(s.channels, ROWS, s.cols)


def spec(space=pltpu.VMEM):
    return pl.BlockSpec(memory_space=space)


def ring(value, axis, step):
    size = lax.axis_size(axis)
    return lax.ppermute(value, axis, [(i, (i + step) % size) for i in range(size)])


def summed(value, axis):
    size = lax.axis_size(axis)
    parts = [ring(value, axis, step) for step in range(1, size)]
    return functools.reduce(jnp.add, parts, value)


def on_device(features, conv_weight, row_taps, col_taps, kernel_weight, target, block_list):
    channels, tile_rows, tile_cols = features.shape
    s = Sizes(channels, tile_rows, tile_cols, row_taps.shape[2], row_taps.shape[0] * 2)
    shape = jax.ShapeDtypeStruct
    smem, hbm = spec(pltpu.SMEM), spec(pl.ANY)

    def call(body, outs, ins, scratch=(), limit=32):
        return pl.pallas_call(
            functools.partial(body, s),
            out_shape=outs,
            in_specs=ins,
            out_specs=jax.tree.map(lambda _: spec(), outs),
            scratch_shapes=list(scratch),
            compiler_params=pltpu.CompilerParams(vmem_limit_bytes=limit * MIB),
        )

    here_row, here_col = lax.axis_index("row"), lax.axis_index("col")
    sides = jnp.stack(
        [
            here_col > 0,
            here_col < lax.axis_size("col") - 1,
            here_row > 0,
            here_row < lax.axis_size("row") - 1,
        ]
    ).astype(jnp.int32)

    half_strip = shape((s.fold, 128), F32)
    table, partial, to_left, to_right = call(
        edge_kernel,
        (
            shape((channels * ROWS, 256), BF16),
            shape((s.grad_pad, s.width), F32),
            half_strip,
            half_strip,
        ),
        [smem, spec(), spec(), spec()],
        [pltpu.VMEM((3, s.rows + WIN, s.cols), F32)],
    )(block_list, features, conv_weight, target)
    from_right = ring(to_left, "col", -1)
    from_left = ring(to_right, "col", 1)

    filters = s.filters
    bands = call(
        band_kernel,
        (
            shape((filters, s.field_pad, s.depth), BF16),
            shape((filters, s.field_pad, s.depth), BF16),
            shape((filters, 256, 256), BF16),
            shape((filters, 256, 256), BF16),
            shape((s.grad_pad, filters * s.field_pad), BF16),
            shape((s.grad_pad, filters * s.field_pad), BF16),
        ),
        [spec(), spec(), smem],
        [pltpu.VMEM((filters * s.field_pad, s.depth), F32)],
    )(row_taps, col_taps, kernel_weight)

    row_strip = shape((s.strip_rows, s.width), F32)
    logits, aim, occupied, to_up, to_down = call(
        middle_kernel,
        (
            shape((s.grad_pad, s.width), F32),
            shape((s.rows, s.width), F32),
            shape((8, s.width), F32),
            row_strip,
            row_strip,
        ),
        [smem, smem, spec(), spec(), spec(), spec()],
    )(sides, block_list, partial, target, from_left, from_right)
    from_down = ring(to_up, "row", -1)
    from_up = ring(to_down, "row", 1)

    shifted, terms = call(
        optics_kernel,
        (shape((6, s.grad_pad, s.cols), BF16), shape((16, channels), F32)),
        [smem, smem] + [spec()] * 5 + [hbm] * 7,
        [
            pltpu.VMEM((s.depth, s.width), F32),
            pltpu.VMEM((s.field_pad, s.width), F32),
            pltpu.VMEM((s.depth, s.width), BF16),
            pltpu.VMEM((s.depth, s.width), BF16),
            pltpu.VMEM((8, 128), F32),
            pltpu.VMEM((filters, s.field_pad, s.width), F32),
            pltpu.VMEM((filters * s.field_pad, s.width), BF16),
            pltpu.VMEM((filters * s.field_pad, s.width), BF16),
            pltpu.VMEM((s.field_pad, s.width), F32),
        ]
        + [pltpu.VMEM(b.shape, BF16) for b in bands]
        + [pltpu.VMEM(features.shape, BF16), pltpu.SemaphoreType.DMA((7,))],
        48,
    )(sides, kernel_weight, logits, aim, occupied, from_up, from_down, *bands, features)

    by_row = summed(terms, "row")
    grad_features = pl.pallas_call(
        functools.partial(feature_kernel, s),
        out_shape=shape(features.shape, BF16),
        grid=(s.steps,),
        in_specs=[
            pl.BlockSpec((channels * ROWS, 256), lambda k: (0, 0)),
            pl.BlockSpec((6, s.grad_pad, s.cols), lambda k: (0, 0, 0)),
        ],
        out_specs=pl.BlockSpec((channels, ROWS, s.cols), lambda k: (0, k, 0)),
    )(table, shifted)
    whole = summed(by_row, "col")
    height = tile_rows * lax.axis_size("row")
    width = tile_cols * lax.axis_size("col")
    grad_weight = (whole[:9].T / math.sqrt(height * width)).reshape(channels, 3, 3)
    return (grad_weight, grad_features)


def solution(mesh):
    placed = (
        P(None, ("grp", "row"), "col"),
        P(),
        P(),
        P(),
        P(),
        P(("grp", "row"), "col"),
        P(("grp", "row"), "col", None),
    )
    return jax.shard_map(
        on_device,
        mesh=mesh,
        in_specs=placed,
        out_specs=(P("grp", None, None), P(None, ("grp", "row"), "col")),
        check_vma=False,
    )
```

profile of v0, /device:TPU:0, one launch (start us, length us, event | category | flops | bytes accessed | tf_op | source)
XLA Modules:
  0.0 57.8 jit_solution(12794866755964564289)
XLA Ops:
  0.7 0.8 %copy.9.conv_weight = bf16[32,3,3]{2,1,0:T(4,128)(2,1)S(1)} copy(bf16[32,3,3]{0,2,1:T(4,128)(2,1)} %param.8) | data formatting | bytes 1152 | tf_op args[1]
  1.5 1.6 %copy-done = bf16[32,128,256]{2,1,0:T(8,128)(2,1)S(1)} copy-done((bf16[32,128,256]{2,1,0:T(8,128)(2,1)S(1)}, bf16[32,128,256]{2,1,0:T(8,128)(2,1)}, u32[]{:S(2)}) %copy-start) | copy-done | bytes 2097176
  3.1 0.9 %copy-done.3 = f32[128,256]{1,0:T(8,128)S(1)} copy-done((f32[128,256]{1,0:T(8,128)S(1)}, f32[128,256]{1,0:T(8,128)}, u32[]{:S(2)}) %copy-start.3) | copy-done | bytes 131096
  4.0 0.7 %copy-done.9 = s32[1,1,8]{2,1,0:T(1,128)S(1)} copy-done((s32[1,1,8]{2,1,0:T(1,128)S(1)}, s32[1,1,8]{2,1,0:T(1,128)}, u32[]{:S(2)}) %copy-start.9) | copy-done | bytes 56
  4.7 1.8 %shard_map.86 = (bf16[512,256]{1,0:T(8,128)(2,1)S(1)}, f32[144,384]{1,0:T(8,128)S(1)}, f32[72,128]{1,0:T(8,128)S(1)}, f32[72,128]{1,0:T(8,128)S(1)}) custom-call(s32[1,1,8]{2,1,0:T(1,128)S(1)} %copy-done.9, bf16[32,128,256]{2,1,0:T(8,128)(2,1)S(1)} %copy-done, bf16[32,3,3]{2,1,0:T(4,128)(2,1)S(1)} %copy.9.conv_weight, f32[128,256]{1,0:T(8,128)S(1)} %copy-done.3), custom_call_target="tpu_custom_call" | custom-call | tf_op jit(solution)/shard_map/pallas_call | solution.py:359
  6.4 0.7 %copy-done.6 = bf16[512,256]{1,0:T(8,128)(2,1)} copy-done((bf16[512,256]{1,0:T(8,128)(2,1)}, bf16[512,256]{1,0:T(8,128)(2,1)S(1)}, u32[]{:S(2)}) %copy-start.6) | copy-done | bytes 262168
  7.1 3.0 %collective-permute-start = (f32[72,128]{1,0:T(8,128)S(1)}, f32[72,128]{1,0:T(8,128)S(1)}, u32[]{:S(2)}, u32[]{:S(2)}) collective-permute-start(f32[72,128]{1,0:T(8,128)S(1)} %get-tuple-element.20), channel_id=1, source_target_pairs={{0,1},{1,2},{2,3},{3,0},{4,5},{5,6},{6,7},{7,4},{8,9},{9,10},{10,1... | collective-permute-start | bytes 110600 | tf_op jit(solution)/shard_map/ppermute | solution.py:323
  10.2 2.0 %collective-permute-start.1 = (f32[72,128]{1,0:T(8,128)S(1)}, f32[72,128]{1,0:T(8,128)S(1)}, u32[]{:S(2)}, u32[]{:S(2)}) collective-permute-start(f32[72,128]{1,0:T(8,128)S(1)} %get-tuple-element.21), channel_id=1, source_target_pairs={{0,3},{1,0},{2,1},{3,2},{4,7},{5,4},{6,5},{7,6},{8,11},{9,8},{10,9... | collective-permute-start | bytes 110600 | tf_op jit(solution)/shard_map/ppermute | solution.py:323
  12.3 2.0 %collective-permute-done.from_left = f32[72,128]{1,0:T(8,128)S(1)} collective-permute-done((f32[72,128]{1,0:T(8,128)S(1)}, f32[72,128]{1,0:T(8,128)S(1)}, u32[]{:S(2)}, u32[]{:S(2)}) %collective-permute-start) | collective-permute-done | bytes 36896 | tf_op jit(solution)/shard_map/ppermute | solution.py:323
  14.2 0.3 collective-permute-done.1.from_right
  14.5 0.7 %shard_map.87 = (f32[144,384]{1,0:T(8,128)S(1)}, f32[128,384]{1,0:T(8,128)S(1)}, f32[8,384]{1,0:T(8,128)S(1)}, f32[56,384]{1,0:T(8,128)S(1)}, f32[56,384]{1,0:T(8,128)S(1)}) custom-call(s32[4]{0:T(128)S(1)} %add_convert_fusion.sides, s32[1,1,8]{2,1,0:T(1,128)S(1)} %copy-done.10, f32[144,384]{1,0:T(8,128)S(1)} %get-tuple-element.19.partial, ...), custom_call_target="tpu_custom_call" | custom-call | tf_op jit(solution)/shard_map/pallas_call | solution.py:389
  15.3 1.7 %collective-permute-start.3 = (f32[56,384]{1,0:T(8,128)S(1)}, f32[56,384]{1,0:T(8,128)S(1)}, u32[]{:S(2)}, u32[]{:S(2)}) collective-permute-start(f32[56,384]{1,0:T(8,128)S(1)} %get-tuple-element.26), channel_id=1, source_target_pairs={{0,12},{4,0},{8,4},{12,8},{1,13},{5,1},{9,5},{13,9},{2,14},{6,2},{... | collective-permute-start | bytes 258056 | tf_op jit(solution)/shard_map/ppermute | solution.py:323
  17.1 2.5 %shard_map.88 = (bf16[16,176,256]{2,1,0:T(8,128)(2,1)S(1)}, bf16[16,176,256]{2,1,0:T(8,128)(2,1)S(1)}, bf16[16,256,256]{2,1,0:T(8,128)(2,1)S(1)}, bf16[16,256,25...) custom-call(f32[8,2,33]{2,1,0:T(2,128)S(1)} %copy-done.7, ...), custom_call_target="tpu_custom_call" | custom-call | tf_op jit(solution)/shard_map/pallas_call | solution.py:374
  19.6 1.3 %copy-done.1 = bf16[16,256,256]{2,1,0:T(8,128)(2,1)} copy-done((bf16[16,256,256]{2,1,0:T(8,128)(2,1)}, bf16[16,256,256]{2,1,0:T(8,128)(2,1)S(1)}, u32[]{:S(2)}) %copy-start.1) | copy-done | bytes 2097176
  20.9 1.3 %copy-done.2 = bf16[16,256,256]{2,1,0:T(8,128)(2,1)} copy-done((bf16[16,256,256]{2,1,0:T(8,128)(2,1)}, bf16[16,256,256]{2,1,0:T(8,128)(2,1)S(1)}, u32[]{:S(2)}) %copy-start.2) | copy-done | bytes 2097176
  22.3 20.2 %shard_map.89 = (bf16[6,144,256]{2,1,0:T(8,128)(2,1)S(1)}, f32[16,32]{1,0:T(8,128)S(1)}) custom-call(s32[4]{0:T(128)S(1)} %add_convert_fusion.sides, f32[8]{0:T(128)S(1)} %copy-done.11, f32[144,384]{1,0:T(8,128)S(1)} %get-tuple-element.22.logits, f32[128,384]{1,0:T(8,128)S(1)} %get-tuple-element.23.aim, f32[8,384]{1,0:T(8,128)S(1)} %get-tuple-element.24.occupied, ...), custom_call_target="tpu_custom_call" | custom-call | tf_op jit(solution)/shard_map/pallas_call | solution.py:403
  42.5 0.8 %copy-done.5 = bf16[6,144,256]{2,1,0:T(8,128)(2,1)} copy-done((bf16[6,144,256]{2,1,0:T(8,128)(2,1)}, bf16[6,144,256]{2,1,0:T(8,128)(2,1)S(1)}, u32[]{:S(2)}) %copy-start.5) | copy-done | bytes 442392
  43.3 1.5 %collective-permute-start.5 = (f32[16,32]{1,0:T(8,128)S(1)}, f32[16,32]{1,0:T(8,128)S(1)}, u32[]{:S(2)}, u32[]{:S(2)}) collective-permute-start(f32[16,32]{1,0:T(8,128)S(1)} %get-tuple-element.33), channel_id=1, source_target_pairs={{0,8},{4,12},{8,0},{12,4},{1,9},{5,13},{9,1},{13,5},{2,10},{6,14},... | collective-permute-start | bytes 6152 | tf_op jit(solution)/shard_map/ppermute | solution.py:323
  45.0 1.9 %collective-permute-done.5 = f32[16,32]{1,0:T(8,128)S(1)} collective-permute-done((f32[16,32]{1,0:T(8,128)S(1)}, f32[16,32]{1,0:T(8,128)S(1)}, u32[]{:S(2)}, u32[]{:S(2)}) %collective-permute-start.5) | collective-permute-done | bytes 2080 | tf_op jit(solution)/shard_map/ppermute | solution.py:323
  46.9 0.9 %collective-permute-done.4 = f32[16,32]{1,0:T(8,128)S(1)} collective-permute-done((f32[16,32]{1,0:T(8,128)S(1)}, f32[16,32]{1,0:T(8,128)S(1)}, u32[]{:S(2)}, u32[]{:S(2)}) %collective-permute-start.4) | collective-permute-done | bytes 2080 | tf_op jit(solution)/shard_map/ppermute | solution.py:323
  47.9 3.7 %collective-permute-start.9 = (f32[16,32]{1,0:T(8,128)S(1)}, f32[16,32]{1,0:T(8,128)S(1)}, u32[]{:S(2)}, u32[]{:S(2)}) collective-permute-start(f32[16,32]{1,0:T(8,128)S(1)} %add_add_fusion), channel_id=1, source_target_pairs={{0,3},{1,0},{2,1},{3,2},{4,7},{5,4},{6,5},{7,6},{8,11},{9,8},{10,9... | collective-permute-start | bytes 6152 | tf_op jit(solution)/shard_map/ppermute | solution.py:323
  51.5 0.6 %collective-permute-start.7 = (f32[16,32]{1,0:T(8,128)S(1)}, f32[16,32]{1,0:T(8,128)S(1)}, u32[]{:S(2)}, u32[]{:S(2)}) collective-permute-start(f32[16,32]{1,0:T(8,128)S(1)} %add_add_fusion), channel_id=1, source_target_pairs={{0,1},{1,2},{2,3},{3,0},{4,5},{5,6},{6,7},{7,4},{8,9},{9,10},{10,1... | collective-permute-start | bytes 6152 | tf_op jit(solution)/shard_map/ppermute | solution.py:323
  52.2 5.0 %shard_map.90 = bf16[32,128,256]{2,1,0:T(8,128)(2,1)} custom-call(bf16[512,256]{1,0:T(8,128)(2,1)} %copy-done.6, bf16[6,144,256]{2,1,0:T(8,128)(2,1)} %copy-done.5), custom_call_target="tpu_custom_call" | custom-call | tf_op jit(solution)/shard_map/pallas_call | solution.py:424
  57.2 0.6 %reshape.7 = f32[32,3,3]{0,2,1:T(4,128)} reshape(f32[32,9]{0,1:T(8,128)S(1)} %fusion.1) | data formatting | bytes 2304 | tf_op jit(solution)/shard_map/reshape | solution.py:437
  (30 shorter events, 0.4 us)
Async XLA Ops:
  0.6 13.9 %copy-start.10 = (s32[1,1,8]{2,1,0:T(1,128)S(1)}, s32[1,1,8]{2,1,0:T(1,128)}, u32[]{:S(2)}) copy-start(s32[1,1,8]{2,1,0:T(1,128)} %listed.3) | copy-start | bytes 100
  0.6 16.4 %copy-start.11 = (f32[8]{0:T(128)S(1)}, f32[8]{0:T(128)}, u32[]{:S(2)}) copy-start(f32[8]{0:T(128)} %weights.1) | copy-start | bytes 100
  0.7 16.4 %copy-start.8 = (f32[8,2,33]{2,1,0:T(2,128)S(1)}, f32[8,2,33]{2,1,0:T(2,128)}, u32[]{:S(2)}) copy-start(f32[8,2,33]{2,1,0:T(2,128)} %col_taps.1) | copy-start | bytes 6340
  0.7 16.4 %copy-start.7 = (f32[8,2,33]{2,1,0:T(2,128)S(1)}, f32[8,2,33]{2,1,0:T(2,128)}, u32[]{:S(2)}) copy-start(f32[8,2,33]{2,1,0:T(2,128)} %row_taps.1) | copy-start | bytes 6340
  1.5 1.6 %copy-start = (bf16[32,128,256]{2,1,0:T(8,128)(2,1)S(1)}, bf16[32,128,256]{2,1,0:T(8,128)(2,1)}, u32[]{:S(2)}) copy-start(bf16[32,128,256]{2,1,0:T(8,128)(2,1)} %features.3) | copy-start | bytes 6291460
  3.1 0.9 %copy-start.3 = (f32[128,256]{1,0:T(8,128)S(1)}, f32[128,256]{1,0:T(8,128)}, u32[]{:S(2)}) copy-start(f32[128,256]{1,0:T(8,128)} %target.3) | copy-start | bytes 393220
  4.0 0.7 %copy-start.9 = (s32[1,1,8]{2,1,0:T(1,128)S(1)}, s32[1,1,8]{2,1,0:T(1,128)}, u32[]{:S(2)}) copy-start(s32[1,1,8]{2,1,0:T(1,128)} %listed.3) | copy-start | bytes 100
  4.7 9.9 %copy-start.4 = (f32[128,256]{1,0:T(8,128)S(1)}, f32[128,256]{1,0:T(8,128)}, u32[]{:S(2)}) copy-start(f32[128,256]{1,0:T(8,128)} %target.3) | copy-start | bytes 393220
  6.4 0.7 %copy-start.6 = (bf16[512,256]{1,0:T(8,128)(2,1)}, bf16[512,256]{1,0:T(8,128)(2,1)S(1)}, u32[]{:S(2)}) copy-start(bf16[512,256]{1,0:T(8,128)(2,1)S(1)} %get-tuple-element.34.table) | copy-start | bytes 786436
  7.1 7.1 %collective-permute-start = (f32[72,128]{1,0:T(8,128)S(1)}, f32[72,128]{1,0:T(8,128)S(1)}, u32[]{:S(2)}, u32[]{:S(2)}) collective-permute-start(f32[72,128]{1,0:T(8,128)S(1)} %get-tuple-element.20), channel_id=1, source_target_pairs={{0,1},{1,2},{2,3},{3,0},{4,5},{5,6},{6,7},{7,4},{8,9},{9,10},{10,1... | collective-permute-start | bytes 110600 | tf_op jit(solution)/shard_map/ppermute | solution.py:323
  10.2 4.4 %collective-permute-start.1 = (f32[72,128]{1,0:T(8,128)S(1)}, f32[72,128]{1,0:T(8,128)S(1)}, u32[]{:S(2)}, u32[]{:S(2)}) collective-permute-start(f32[72,128]{1,0:T(8,128)S(1)} %get-tuple-element.21), channel_id=1, source_target_pairs={{0,3},{1,0},{2,1},{3,2},{4,7},{5,4},{6,5},{7,6},{8,11},{9,8},{10,9... | collective-permute-start | bytes 110600 | tf_op jit(solution)/shard_map/ppermute | solution.py:323
  15.3 7.0 %collective-permute-start.2 = (f32[56,384]{1,0:T(8,128)S(1)}, f32[56,384]{1,0:T(8,128)S(1)}, u32[]{:S(2)}, u32[]{:S(2)}) collective-permute-start(f32[56,384]{1,0:T(8,128)S(1)} %get-tuple-element.25), channel_id=1, source_target_pairs={{0,4},{4,8},{8,12},{12,0},{1,5},{5,9},{9,13},{13,1},{2,6},{6,10},{... | collective-permute-start | bytes 258056 | tf_op jit(solution)/shard_map/ppermute | solution.py:323
  15.3 6.9 %collective-permute-start.3 = (f32[56,384]{1,0:T(8,128)S(1)}, f32[56,384]{1,0:T(8,128)S(1)}, u32[]{:S(2)}, u32[]{:S(2)}) collective-permute-start(f32[56,384]{1,0:T(8,128)S(1)} %get-tuple-element.26), channel_id=1, source_target_pairs={{0,12},{4,0},{8,4},{12,8},{1,13},{5,1},{9,5},{13,9},{2,14},{6,2},{... | collective-permute-start | bytes 258056 | tf_op jit(solution)/shard_map/ppermute | solution.py:323
  19.6 1.3 %copy-start.1 = (bf16[16,256,256]{2,1,0:T(8,128)(2,1)}, bf16[16,256,256]{2,1,0:T(8,128)(2,1)S(1)}, u32[]{:S(2)}) copy-start(bf16[16,256,256]{2,1,0:T(8,128)(2,1)S(1)} %get-tuple-element.29.col_fwd) | copy-start | bytes 6291460
  20.9 1.3 %copy-start.2 = (bf16[16,256,256]{2,1,0:T(8,128)(2,1)}, bf16[16,256,256]{2,1,0:T(8,128)(2,1)S(1)}, u32[]{:S(2)}) copy-start(bf16[16,256,256]{2,1,0:T(8,128)(2,1)S(1)} %get-tuple-element.30.col_adj) | copy-start | bytes 6291460
  42.5 0.8 %copy-start.5 = (bf16[6,144,256]{2,1,0:T(8,128)(2,1)}, bf16[6,144,256]{2,1,0:T(8,128)(2,1)S(1)}, u32[]{:S(2)}) copy-start(bf16[6,144,256]{2,1,0:T(8,128)(2,1)S(1)} %get-tuple-element.35.shifted) | copy-start | bytes 1327108
  43.3 1.7 %collective-permute-start.6 = (f32[16,32]{1,0:T(8,128)S(1)}, f32[16,32]{1,0:T(8,128)S(1)}, u32[]{:S(2)}, u32[]{:S(2)}) collective-permute-start(f32[16,32]{1,0:T(8,128)S(1)} %get-tuple-element.33), channel_id=1, source_target_pairs={{0,12},{4,0},{8,4},{12,8},{1,13},{5,1},{9,5},{13,9},{2,14},{6,2},{... | collective-permute-start | bytes 6152 | tf_op jit(solution)/shard_map/ppermute | solution.py:323
  43.3 3.7 %collective-permute-start.5 = (f32[16,32]{1,0:T(8,128)S(1)}, f32[16,32]{1,0:T(8,128)S(1)}, u32[]{:S(2)}, u32[]{:S(2)}) collective-permute-start(f32[16,32]{1,0:T(8,128)S(1)} %get-tuple-element.33), channel_id=1, source_target_pairs={{0,8},{4,12},{8,0},{12,4},{1,9},{5,13},{9,1},{13,5},{2,10},{6,14},... | collective-permute-start | bytes 6152 | tf_op jit(solution)/shard_map/ppermute | solution.py:323
  44.8 3.1 %collective-permute-start.4 = (f32[16,32]{1,0:T(8,128)S(1)}, f32[16,32]{1,0:T(8,128)S(1)}, u32[]{:S(2)}, u32[]{:S(2)}) collective-permute-start(f32[16,32]{1,0:T(8,128)S(1)} %get-tuple-element.33), channel_id=1, source_target_pairs={{0,4},{4,8},{8,12},{12,0},{1,5},{5,9},{9,13},{13,1},{2,6},{6,10},{... | collective-permute-start | bytes 6152 | tf_op jit(solution)/shard_map/ppermute | solution.py:323
  47.9 9.3 %collective-permute-start.9 = (f32[16,32]{1,0:T(8,128)S(1)}, f32[16,32]{1,0:T(8,128)S(1)}, u32[]{:S(2)}, u32[]{:S(2)}) collective-permute-start(f32[16,32]{1,0:T(8,128)S(1)} %add_add_fusion), channel_id=1, source_target_pairs={{0,3},{1,0},{2,1},{3,2},{4,7},{5,4},{6,5},{7,6},{8,11},{9,8},{10,9... | collective-permute-start | bytes 6152 | tf_op jit(solution)/shard_map/ppermute | solution.py:323
  51.5 5.7 %collective-permute-start.8 = (f32[16,32]{1,0:T(8,128)S(1)}, f32[16,32]{1,0:T(8,128)S(1)}, u32[]{:S(2)}, u32[]{:S(2)}) collective-permute-start(f32[16,32]{1,0:T(8,128)S(1)} %add_add_fusion), channel_id=1, source_target_pairs={{0,2},{1,3},{2,0},{3,1},{4,6},{5,7},{6,4},{7,5},{8,10},{9,11},{10,... | collective-permute-start | bytes 6152 | tf_op jit(solution)/shard_map/ppermute | solution.py:323
  51.5 5.7 %collective-permute-start.7 = (f32[16,32]{1,0:T(8,128)S(1)}, f32[16,32]{1,0:T(8,128)S(1)}, u32[]{:S(2)}, u32[]{:S(2)}) collective-permute-start(f32[16,32]{1,0:T(8,128)S(1)} %add_add_fusion), channel_id=1, source_target_pairs={{0,1},{1,2},{2,3},{3,0},{4,5},{5,6},{6,7},{7,4},{8,9},{9,10},{10,1... | collective-permute-start | bytes 6152 | tf_op jit(solution)/shard_map/ppermute | solution.py:323
where the time goes:
time: 58.1 us; the launch traced here: 57.8 us
  Pallas kernels  30.3 us (52%)
  starting transfers between devices  12.9 us (22%)
  local copies, waits for them, and re-layouts  8.69 us (15%)
  waiting for transfers between devices  5.12 us (9%)
  between operations  0.75 us (1%)
    pallas_call x1, Pallas kernels, on_device(): call(optics_kernel, (shape((6, s.grad_pad, s.cols), BF16), shape((16, cha...  20.2 us
    ppermute x10, starting transfers between devices, ring(): lax.ppermute(value, axis, [(i, (i + step) % size) for i in range(size)])  12.9 us
    unnamed x25, local copies, waits for them, and re-layouts  8.09 us
    ppermute x10, waiting for transfers between devices, ring(): lax.ppermute(value, axis, [(i, (i + step) % size) for i in range(size)])  5.12 us
    pallas_call x1, Pallas kernels, on_device(): pl.pallas_call(functools.partial(feature_kernel, s), out_shape=shape(feat...  5.03 us
    pallas_call x1, Pallas kernels, on_device(): call(band_kernel, (shape((filters, s.field_pad, s.depth), BF16), shape((f...  2.53 us
    pallas_call x1, Pallas kernels, on_device(): call(edge_kernel, (shape((channels * ROWS, 256), BF16), shape((s.grad_pad...  1.78 us
  transfers between devices with their start and end apart: 10, of which 4 were waited for; matrix products, arithmetic and copies ran while one was open for 0% of the time, Pallas kernels for 13%

commit v1 on v0

v1 whole, which is shorter than its diff:
```python
import functools
import math

import jax
import jax.numpy as jnp
from jax import lax
from jax.experimental import pallas as pl
from jax.experimental.pallas import tpu as pltpu
from jax.sharding import PartitionSpec as P

BLOCK = 64
ROWS = 16
WIN = 32
MIB = 1 << 20
F32 = jnp.float32
BF16 = jnp.bfloat16


def up(value, multiple):
    return -(-value // multiple) * multiple


def iota(shape, dim):
    return lax.broadcasted_iota(jnp.int32, shape, dim)


def split(value):
    high = value.astype(BF16)
    return high, (value - high.astype(F32)).astype(BF16)


def dot(left, right, dims=((1,), (0,)), precision=None):
    return lax.dot_general(
        left, right, (dims, ((), ())), precision=precision, preferred_element_type=F32
    )


NT = ((1,), (1,))


def neighbours(axis):
    here = lax.axis_index(axis)
    return here > 0, here < lax.axis_size(axis) - 1, here % 2 == 1


class Sizes:
    def __init__(self, channels, tile_rows, tile_cols, taps, filters):
        self.channels, self.rows, self.cols = channels, tile_rows, tile_cols
        self.taps, self.filters = taps, filters
        self.half = (taps - 1) // 2
        self.mask_halo = 2 * self.half + 1
        self.field_halo = self.half + 1
        self.strip = self.mask_halo + 1
        self.base = self.mask_halo - 1
        self.width = up(tile_cols + 2 * self.mask_halo, 128)
        self.field_rows = tile_rows + 2 * self.field_halo
        self.field_cols = tile_cols + 2 * self.field_halo
        self.field_pad = up(self.field_rows, 16)
        self.grad_pad = tile_rows + ROWS
        mask_rows = tile_rows + 2 * self.mask_halo
        self.depth = up(max(mask_rows, self.field_pad + taps), 128)
        self.steps = tile_rows // ROWS
        self.strip_rows = up(self.strip + 1 + self.field_halo, 8)
        self.fold = self.grad_pad // 2


def row_band_kernel(s, row_taps, kernel_weight, row_band, adj_high, adj_low, flipped):
    for f in range(s.filters):
        k, p = f // 2, f % 2
        pad = jnp.zeros((1, s.depth - s.taps), F32)
        row = jnp.concatenate([row_taps[k, p : p + 1, :], pad], 1)
        band = pltpu.roll(
            jnp.broadcast_to(row, (s.field_pad, s.depth)), 0, 1, stride=1, stride_axis=0
        )
        here = slice(f * s.field_pad, (f + 1) * s.field_pad)
        row_band[here, : s.depth], row_band[here, s.depth :] = split(band)
        flipped[here, :] = pltpu.roll(
            jnp.broadcast_to(row * (2.0 * kernel_weight[k]), (s.field_pad, s.depth)),
            s.depth - (s.taps - 1),
            1,
            stride=1,
            stride_axis=0,
        )
    turned = flipped[...].T[: s.grad_pad, :]
    adj_high[...], adj_low[...] = split(turned)


def col_band_kernel(s, col_taps, col_fwd, col_adj):
    for f in range(s.filters):
        k, p = f // 2, f % 2
        pad = jnp.zeros((1, 256 - s.taps), F32)
        wide = jnp.concatenate([col_taps[k, p : p + 1, :], pad], 1)
        band = pltpu.roll(jnp.broadcast_to(wide, (128, 256)), 0, 1, stride=1, stride_axis=0).T
        col_fwd[f, :, :128], col_fwd[f, :, 128:] = split(band)
        band = pltpu.roll(
            jnp.broadcast_to(wide, (256, 256)), 256 - (s.taps - 1), 1, stride=1, stride_axis=0
        )
        col_adj[f, :, :128], col_adj[f, :, 128:] = split(band[:, :128])


def edge_kernel(
    s, listed_hbm, features_hbm, conv_weight_hbm, target_hbm, table, partial, first_out, second_out,
    acc, listed, features, conv_weight, target, sems,
):
    fetch = [
        pltpu.make_async_copy(conv_weight_hbm, conv_weight, sems.at[0]),
        pltpu.make_async_copy(listed_hbm, listed, sems.at[1]),
        pltpu.make_async_copy(target_hbm, target, sems.at[2]),
    ]
    parts = 4
    rows = s.rows // parts
    for q in range(parts):
        here = pl.ds(q * rows, rows)
        fetch.append(
            pltpu.make_async_copy(features_hbm.at[:, here, :], features.at[:, here, :], sems.at[3 + q])
        )
    for copy in fetch:
        copy.start()
    acc[...] = jnp.zeros_like(acc)
    lanes = 3 * WIN
    u, lane = iota((s.channels * ROWS, lanes), 0) % ROWS, iota((s.channels * ROWS, lanes), 1)
    h = lane % WIN
    owner = jnp.where(
        iota((s.channels * ROWS, s.channels), 0) // ROWS == iota((s.channels * ROWS, s.channels), 1), 1.0, 0.0
    ).astype(BF16)
    pick = jnp.where(iota((3, lanes), 1) // WIN == iota((3, lanes), 0), 1.0, 0.0)
    fetch[0].wait()
    flat = jnp.zeros((s.channels * ROWS, lanes), F32)
    for row_shift in range(3):
        spread = dot(conv_weight[row_shift].astype(F32), pick, ((0,), (0,))).astype(BF16)
        flat = jnp.where(h == u - row_shift + 2, dot(owner, spread), flat)
    table[...] = jnp.concatenate([flat.astype(BF16)] * 3, 1)
    left = flat.T.astype(BF16)
    for k in range(s.steps):
        if k % (s.steps // parts) == 0:
            fetch[3 + k // (s.steps // parts)].wait()
        block = features[:, k * ROWS : (k + 1) * ROWS, :].reshape(s.channels * ROWS, s.cols)
        sums = dot(left, block)
        for b in range(3):
            acc[b, k * ROWS : k * ROWS + WIN, :] += sums[b * WIN : (b + 1) * WIN]
    fetch[1].wait()
    fetch[2].wait()
    whole = jnp.zeros((s.grad_pad, s.width), F32)
    blank = jnp.zeros((s.grad_pad, s.width - s.cols), F32)
    for b in range(3):
        part = jnp.concatenate([acc[b, : s.grad_pad], blank], 1)
        whole += pltpu.roll(part, s.base + 2 - b, 1)
    partial[...] = whole

    place, row = iota((s.grad_pad, 128), 1), iota((s.grad_pad, 128), 0)
    aim = jnp.concatenate([target[...], jnp.zeros((s.grad_pad - s.rows, s.cols), F32)], 0)
    aim = jnp.concatenate([aim, jnp.zeros((s.grad_pad, s.width - s.cols), F32)], 1)
    across = s.cols // BLOCK
    strips = []
    for first, first_aim, block_col in (
        (s.base, 0, 0),
        (s.cols, s.cols - s.field_halo, across - 1),
    ):
        logits = pltpu.roll(whole, (s.width - first) % s.width, 1)[:, :128]
        wanted = pltpu.roll(aim, (s.width - first_aim + s.strip) % s.width, 1)[:, :128]
        number = (row // BLOCK) * across + block_col
        used = jnp.zeros((s.grad_pad, 128), F32)
        for n in range(listed.shape[2]):
            used = jnp.where(number == listed[0, 0, n], 1.0, used)
        used = jnp.where(row < s.rows, used, 0.0)
        value = jnp.where(place < s.strip, logits, wanted)
        value = jnp.where(place < s.strip + s.field_halo, value, used)
        value = jnp.where(place < s.strip + s.field_halo + 1, value, 0.0)
        strips.append(
            jnp.where(iota((s.fold, 128), 1) < 64, value[: s.fold], pltpu.roll(value[s.fold :], 64, 1))
        )
    odd = neighbours("col")[2]
    first_out[...] = jnp.where(odd, strips[0], strips[1])
    second_out[...] = jnp.where(odd, strips[1], strips[0])


def unfolded(s, value):
    low = iota((s.fold, 128), 1) < 64
    return jnp.concatenate(
        [jnp.where(low, value, 0.0), jnp.where(low, pltpu.roll(value, 64, 1), 0.0)], 0
    )


def middle_kernel(s, listed, partial, target, first, second, band, logits, aim, occupied, first_out, second_out):
    extra = jnp.zeros((s.grad_pad, s.width - 128), F32)
    lane = iota((s.grad_pad, 128), 1)
    has_left, has_right, odd = neighbours("col")
    one, two = first[...], second[...]
    west = unfolded(s, jnp.where(has_left, jnp.where(odd, one, two), 0.0))
    east = unfolded(s, jnp.where(has_right, jnp.where(odd, two, one), 0.0))

    def placed(value, keep_from, keep, offset):
        kept = jnp.where((lane >= keep_from) & (lane < keep_from + keep), value, 0.0)
        wide = jnp.concatenate([kept, extra], 1)
        return pltpu.roll(wide, (offset - keep_from) % s.width, 1)

    whole = partial[...] + placed(west, 0, s.strip, 0)
    whole += placed(east, 0, s.strip, s.cols + s.base)
    logits[...] = whole
    own = jnp.concatenate([target[...], jnp.zeros((s.rows, s.width - s.cols), F32)], 1)
    aims = pltpu.roll(own, s.field_halo, 1)
    aims += placed(west, s.strip, s.field_halo, 0)[: s.rows]
    aims += placed(east, s.strip, s.field_halo, s.cols + s.field_halo)[: s.rows]
    aim[...] = aims

    across, down = s.cols // BLOCK, s.rows // BLOCK
    row, col = iota((8, s.width), 0), iota((8, s.width), 1) - s.mask_halo
    inside = (col >= 0) & (col < s.cols) & (row < down)
    number = jnp.where(inside, row * across + (col + BLOCK) // BLOCK - 1, -1)
    used = jnp.zeros((8, s.width), F32)
    for n in range(listed.shape[2]):
        used = jnp.where(number == listed[0, 0, n], 1.0, used)
    flag = s.strip + s.field_halo
    for r in range(down):
        here = row == r
        used = jnp.where(here & (col < 0), west[r * BLOCK : r * BLOCK + 1, flag : flag + 1], used)
        beyond = here & (col >= s.cols) & (col < s.cols + s.mask_halo)
        used = jnp.where(beyond, east[r * BLOCK : r * BLOCK + 1, flag : flag + 1], used)
    occupied[...] = used

    odd = neighbours("row")[2]

    def fill(out, low):
        start = s.rows + 2 - s.strip if low else 0
        start_aim = s.rows - s.field_halo if low else 0
        block_row = down - 1 if low else 0
        out[...] = jnp.zeros_like(out)
        out[: s.strip, :] = whole[start : start + s.strip]
        out[s.strip : s.strip + 1, :] = used[block_row : block_row + 1]
        out[s.strip + 1 : s.strip + 1 + s.field_halo, :] = aims[start_aim : start_aim + s.field_halo]

    @pl.when(odd)
    def _():
        fill(first_out, False)
        fill(second_out, True)

    @pl.when(jnp.logical_not(odd))
    def _():
        fill(first_out, True)
        fill(second_out, False)


def optics_kernel(
    s, weights, logits, aim, occupied, first, second, row_band, col_fwd, col_adj, adj_high, adj_low,
    features, shifted, terms,
    ext, aims, masks, field, pulled_high, pulled_low, total,
):

    has_left, has_right, _ = neighbours("col")
    has_up, has_down, odd = neighbours("row")
    one, two = first[...], second[...]
    north = jnp.where(has_up, jnp.where(odd, one, two), 0.0)
    south = jnp.where(has_down, jnp.where(odd, two, one), 0.0)
    edge = up(s.strip, 8)
    lane_row = iota((edge, s.width), 0)
    ext[...] = jnp.zeros_like(ext)
    ext[s.base : s.base + s.grad_pad, :] = logits[...]
    ext[:edge, :] += jnp.where(lane_row < s.strip, north[:edge], 0.0)
    low = s.rows + s.base
    ext[low : low + edge, :] += jnp.where(lane_row < s.strip, south[:edge], 0.0)
    aims[...] = jnp.zeros_like(aims)
    aims[: s.field_halo, :] = north[s.strip + 1 : s.strip + 1 + s.field_halo]
    aims[s.field_halo : s.field_halo + s.rows, :] = aim[...]
    aims[s.field_halo + s.rows : s.field_rows, :] = south[s.strip + 1 : s.strip + 1 + s.field_halo]

    place = iota((s.depth, s.width), 0) - s.mask_halo
    used = jnp.where(place < 0, north[s.strip : s.strip + 1], 0.0)
    for r in range(s.rows // BLOCK):
        used = jnp.where((place >= r * BLOCK) & (place < (r + 1) * BLOCK), occupied[r : r + 1, :], used)
    below = (place >= s.rows) & (place < s.rows + s.mask_halo)
    used = jnp.where(below, south[s.strip : s.strip + 1], used)
    sigma = jax.nn.sigmoid(ext[...])
    mask = used * sigma
    high, low = split(mask)
    masks[: s.depth, :] = high
    masks[s.depth : 2 * s.depth, :] = low
    masks[2 * s.depth :, :] = high
    slope = (mask * (1.0 - sigma))[s.base : s.base + s.grad_pad]
    slope = pltpu.roll(slope, s.width - s.base, 1)

    blocks = -(-s.field_cols // 128)
    total[...] = jnp.zeros_like(total)
    group = 4
    tall = group * s.field_pad
    gap = jnp.zeros((s.field_pad, 128), BF16)

    def windows(high, low, count):
        rows = []
        for n in range(count):
            line = []
            for part in (high, low):
                line.append(part[:, 128 * n : min(128 * n + 256, s.width)])
                if 128 * n + 256 > s.width:
                    line.append(gap)
            rows.append(jnp.concatenate(line, 1))
        return jnp.concatenate(rows, 0)

    def doubled(band):
        return jnp.concatenate([band, band], 0)

    def forward(g, carry):
        start = pl.multiple_of(g * tall, 16)
        band = row_band[pl.ds(start, tall), :]
        stack = jnp.concatenate([band[:, : s.depth], band[:, : s.depth], band[:, s.depth :]], 1)
        rowed = dot(stack, masks[...])
        for i in range(0, group, 2):
            squares = 0.0
            for f in (i, i + 1):
                high, low = split(rowed[f * s.field_pad : (f + 1) * s.field_pad])
                both = dot(windows(high, low, blocks), doubled(col_fwd[g * group + f]))
                value = both[:, :128] + both[:, 128:]
                for n in range(blocks):
                    here = slice(n * s.field_pad, (n + 1) * s.field_pad)
                    field[g * group + f, :, 128 * n : 128 * (n + 1)] = value[here]
                squares += value * value
            squares *= weights[(g * group + i) // 2]
            for n in range(blocks):
                total[:, 128 * n : 128 * (n + 1)] += squares[n * s.field_pad : (n + 1) * s.field_pad]
        return carry

    lax.fori_loop(0, s.filters // group, forward, 0)

    row, col = iota((s.field_pad, s.width), 0) - s.field_halo, iota((s.field_pad, s.width), 1) - s.field_halo
    inside = ((row >= 0) | has_up) & ((row < s.rows) | has_down) & (row < s.rows + s.field_halo)
    inside &= ((col >= 0) | has_left) & ((col < s.cols) | has_right) & (col < s.cols + s.field_halo)
    total[...] = jnp.where(inside, total[...] - aims[...], 0.0)
    out_blocks = -(-(s.cols + 2) // 128)
    if blocks * 128 < s.width:
        field[:, :, blocks * 128 :] = jnp.zeros_like(field[:, :, blocks * 128 :])

    def backward(g, carry):
        for i in range(group):
            f = g * group + i
            high, low = split(total[...] * field[f])
            start = pl.multiple_of(f * s.field_pad, 16)
            both = dot(windows(high, low, out_blocks), doubled(col_adj[f]))
            high, low = split(both[:, :128] + both[:, 128:])
            for n in range(out_blocks):
                here = slice(n * s.field_pad, (n + 1) * s.field_pad)
                pulled_high[pl.ds(start, s.field_pad), 128 * n : 128 * (n + 1)] = high[here]
                pulled_low[pl.ds(start, s.field_pad), 128 * n : 128 * (n + 1)] = low[here]
        return carry

    lax.fori_loop(0, s.filters // group, backward, 0)
    if out_blocks * 128 < s.width:
        pulled_high[:, out_blocks * 128 :] = jnp.zeros_like(pulled_high[:, out_blocks * 128 :])
        pulled_low[:, out_blocks * 128 :] = jnp.zeros_like(pulled_low[:, out_blocks * 128 :])
    both = dot(jnp.concatenate([adj_high[...], adj_low[...]], 0), pulled_high[...])
    grad = both[: s.grad_pad] + both[s.grad_pad :] + dot(adj_high[...], pulled_low[...])
    grad = grad * slope

    for b in range(3):
        moved = grad if b == 2 else pltpu.roll(grad, s.width - (2 - b), 1)
        moved = moved[:, : s.cols]
        shifted[b], shifted[3 + b] = split(moved)
        rest = moved - shifted[b].astype(F32) - shifted[3 + b].astype(F32)
        shifted[6 + b] = rest.astype(BF16)
    sums = jnp.zeros((s.channels * ROWS, 6 * WIN), F32)
    for k in range(s.steps):
        block = features[:, k * ROWS : (k + 1) * ROWS, :].reshape(s.channels * ROWS, s.cols)
        window = jnp.concatenate([shifted[q, k * ROWS : k * ROWS + WIN, :] for q in range(6)], 0)
        sums += dot(block, window, NT)
    cube = sums.reshape(s.channels, ROWS, 6 * WIN)
    u, lane = iota((ROWS, 6 * WIN), 0), iota((ROWS, 6 * WIN), 1)
    number, group = iota((16, 6 * WIN), 0), (iota((16, 6 * WIN), 1) // WIN) % 3
    result = jnp.zeros((16, s.channels), F32)
    for a in range(3):
        hit = jnp.where(lane % WIN == u - a + 2, 1.0, 0.0)
        line = (cube * hit[None]).sum(1)
        pick = jnp.where(number == a * 3 + group, 1.0, 0.0)
        result += dot(pick, line, NT, lax.Precision.HIGHEST)
    terms[...] = result


def feature_kernel(s, table, shifted, out, blocks, sems):
    copies = []
    for k in range(s.steps):
        window = jnp.concatenate([shifted[q, k * ROWS : k * ROWS + WIN, :] for q in range(9)], 0)
        value = dot(table[...], window)
        here = pl.ds(k * ROWS, ROWS)
        blocks[:, here, :] = value.astype(BF16).reshape(s.channels, ROWS, s.cols)
        copies.append(pltpu.make_async_copy(blocks.at[:, here, :], out.at[:, here, :], sems.at[k]))
        copies[-1].start()
    for copy in copies:
        copy.wait()


def spec(space=pltpu.VMEM):
    return pl.BlockSpec(memory_space=space)


def exchanged(first, second, axis):
    size, parts = lax.axis_size(axis), lax.axis_size("grp")
    one = lax.ppermute(first, axis, [(i, i ^ 1) for i in range(size)])
    pairs = []
    for g in range(parts):
        for i in range(size):
            j = i + 1 if i % 2 else i - 1
            if 0 <= j < size:
                pairs.append((g * size + i, g * size + j))
            elif parts % 2:
                pairs.append((g * size + i, g * size + (j % size)))
            else:
                pairs.append((g * size + i, (g ^ 1) * size + i))
    return one, lax.ppermute(second, ("grp", axis), pairs)


def summed(value, axis):
    size = lax.axis_size(axis)
    parts = [
        lax.ppermute(value, axis, [(i, i ^ step) for i in range(size)]) for step in range(1, size)
    ]
    return functools.reduce(jnp.add, parts, value)


def on_device(features, conv_weight, row_taps, col_taps, kernel_weight, target, block_list):
    channels, tile_rows, tile_cols = features.shape
    s = Sizes(channels, tile_rows, tile_cols, row_taps.shape[2], row_taps.shape[0] * 2)
    shape = jax.ShapeDtypeStruct
    smem, hbm = spec(pltpu.SMEM), spec(pltpu.HBM)

    def call(body, outs, ins, scratch=(), limit=24, out_space=pltpu.VMEM):
        return pl.pallas_call(
            functools.partial(body, s),
            out_shape=outs,
            in_specs=ins,
            out_specs=jax.tree.map(lambda _: spec(out_space), outs),
            scratch_shapes=list(scratch),
            compiler_params=pltpu.CompilerParams(vmem_limit_bytes=limit * MIB),
        )

    half_strip = shape((s.fold, 128), F32)
    table, partial, first, second = call(
        edge_kernel,
        (
            shape((channels * ROWS, 9 * WIN), BF16),
            shape((s.grad_pad, s.width), F32),
            half_strip,
            half_strip,
        ),
        [hbm] * 4,
        [
            pltpu.VMEM((3, s.rows + WIN, s.cols), F32),
            pltpu.SMEM(block_list.shape, jnp.int32),
            pltpu.VMEM(features.shape, BF16),
            pltpu.VMEM((3, 3, channels), BF16),
            pltpu.VMEM(target.shape, F32),
            pltpu.SemaphoreType.DMA((7,)),
        ],
    )(*(pltpu.with_memory_space_constraint(x, pltpu.HBM) for x in (block_list, features, conv_weight.transpose(1, 2, 0), target)))
    first, second = exchanged(first, second, "col")

    filters = s.filters
    col_bands = call(
        col_band_kernel,
        (shape((filters, 256, 256), BF16), shape((filters, 256, 256), BF16)),
        [spec()],
    )(col_taps)
    row_bands = call(
        row_band_kernel,
        (
            shape((filters * s.field_pad, 2 * s.depth), BF16),
            shape((s.grad_pad, filters * s.field_pad), BF16),
            shape((s.grad_pad, filters * s.field_pad), BF16),
        ),
        [spec(), smem],
        [pltpu.VMEM((filters * s.field_pad, s.depth), F32)],
    )(row_taps, kernel_weight)

    row_strip = shape((s.strip_rows, s.width), F32)
    logits, aim, occupied, first, second = call(
        middle_kernel,
        (
            shape((s.grad_pad, s.width), F32),
            shape((s.rows, s.width), F32),
            shape((8, s.width), F32),
            row_strip,
            row_strip,
        ),
        [smem, spec(), spec(), spec(), spec(), spec()],
    )(block_list, partial, target, first, second, col_bands[0])
    first, second = exchanged(first, second, "row")

    shifted, terms = call(
        optics_kernel,
        (shape((9, s.grad_pad, s.cols), BF16), shape((16, channels), F32)),
        [smem] + [spec()] * 11,
        [
            pltpu.VMEM((s.depth, s.width), F32),
            pltpu.VMEM((s.field_pad, s.width), F32),
            pltpu.VMEM((3 * s.depth, s.width), BF16),
            pltpu.VMEM((filters, s.field_pad, s.width), F32),
            pltpu.VMEM((filters * s.field_pad, s.width), BF16),
            pltpu.VMEM((filters * s.field_pad, s.width), BF16),
            pltpu.VMEM((s.field_pad, s.width), F32),
        ],
        32,
    )(kernel_weight, logits, aim, occupied, first, second, *row_bands[:1], *col_bands, *row_bands[1:], features)

    by_row = summed(terms, "row")
    grad_features = call(
        feature_kernel,
        shape(features.shape, BF16),
        [spec(), spec()],
        [pltpu.VMEM(features.shape, BF16), pltpu.SemaphoreType.DMA((s.steps,))],
        out_space=pltpu.HBM,
    )(table, shifted)
    whole = summed(by_row, "col")
    height = tile_rows * lax.axis_size("row")
    width = tile_cols * lax.axis_size("col")
    grad_weight = (whole[:9].T / math.sqrt(height * width)).reshape(channels, 3, 3)
    return (grad_weight, grad_features)


def solution(mesh):
    placed = (
        P(None, ("grp", "row"), "col"),
        P(),
        P(),
        P(),
        P(),
        P(("grp", "row"), "col"),
        P(("grp", "row"), "col", None),
    )
    return jax.shard_map(
        on_device,
        mesh=mesh,
        in_specs=placed,
        out_specs=(P("grp", None, None), P(None, ("grp", "row"), "col")),
        check_vma=False,
    )
```

time: 58.1 us -> 40.4 us (0.70)
  Pallas kernels: 30.3 us -> 21.3 us
  local copies, waits for them, and re-layouts: 8.69 us -> 0.63 us
    pallas_call x4 -> x5, Pallas kernels: 29.6 us -> 20.5 us  [the longest x1 12 us: on_device(): call(optics_kernel, (shape((9, s.grad_pad, s.cols), BF16), shape((16, cha...]
    unnamed x25 -> x12, local copies, waits for them, and re-layouts: 8.09 us -> 0.03 us
  transfers between devices with their start and end apart: 10 -> 10, of which waited for: 4 -> 5; matrix products, arithmetic and copies ran while one was open for 0% -> 0% of each run, Pallas kernels for 13% -> 13%
where the time goes in v1:
time: 40.4 us; the launch traced here: 40.3 us
  Pallas kernels  21.3 us (53%)
  starting transfers between devices  12.6 us (31%)
  waiting for transfers between devices  4.99 us (12%)
  between operations  0.76 us (2%)
  local copies, waits for them, and re-layouts  0.63 us (2%)
    pallas_call x1, Pallas kernels, on_device(): call(optics_kernel, (shape((9, s.grad_pad, s.cols), BF16), shape((16, cha...  12 us
    ppermute x6, starting transfers between devices, summed(): lax.ppermute(value, axis, [(i, i ^ step) for i in range(size)])  6.37 us
    ppermute x2, starting transfers between devices, exchanged(): one = lax.ppermute(first, axis, [(i, i ^ 1) for i in range(size)])  3.16 us
    pallas_call x1, Pallas kernels, on_device(): call(edge_kernel, (shape((channels * ROWS, 9 * WIN), BF16), shape((s.grad...  3.11 us
    ppermute x2, starting transfers between devices, exchanged(): return (one, lax.ppermute(second, ('grp', axis), pairs))  3.11 us
    ppermute x6, waiting for transfers between devices, summed(): lax.ppermute(value, axis, [(i, i ^ step) for i in range(size)])  2.84 us
    pallas_call x1, Pallas kernels, on_device(): call(row_band_kernel, (shape((filters * s.field_pad, 2 * s.depth), BF16),...  2.2 us
    pallas_call x1, Pallas kernels, on_device(): call(feature_kernel, shape(features.shape, BF16), [spec(), spec()], [pltp...  2.18 us
  transfers between devices with their start and end apart: 10, of which 5 were waited for; matrix products, arithmetic and copies ran while one was open for 0% of the time, Pallas kernels for 13%

profile of v1, /device:TPU:0, one launch (start us, length us, event | category | flops | bytes accessed | tf_op | source)
XLA Modules:
  0.0 40.3 jit_solution(2698351755400585913)
XLA Ops:
  0.7 3.1 %shard_map.86 = (bf16[512,288]{1,0:T(8,128)(2,1)S(1)}, f32[144,384]{1,0:T(8,128)S(1)}, f32[72,128]{1,0:T(8,128)S(1)}, f32[72,128]{1,0:T(8,128)S(1)}) custom-call(s32[1,1,8]{2,1,0:T(1,128)} %listed.1, bf16[32,128,256]{2,1,0:T(8,128)(2,1)} %features.1, bf16[3,3,32]{2,1,0:T(4,128)(2,1)} %bitcast.5, f32[128,256]{1,0:T(8,128)} %target.1), custom_call_target="tpu_custom_call" | custom-call | tf_op jit(solution)/shard_map/pallas_call | solution.py:433
  3.8 3.1 %collective-permute-start = (f32[72,128]{1,0:T(8,128)S(1)}, f32[72,128]{1,0:T(8,128)S(1)}, u32[]{:S(2)}, u32[]{:S(2)}) collective-permute-start(f32[72,128]{1,0:T(8,128)S(1)} %get-tuple-element.19), channel_id=1, source_target_pairs={{0,1},{1,0},{2,3},{3,2},{4,5},{5,4},{6,7},{7,6},{8,9},{9,8},{10,11... | collective-permute-start | bytes 110600 | tf_op jit(solution)/shard_map/ppermute | solution.py:394
  6.9 1.5 %collective-permute-start.1 = (f32[72,128]{1,0:T(8,128)S(1)}, f32[72,128]{1,0:T(8,128)S(1)}, u32[]{:S(2)}, u32[]{:S(2)}) collective-permute-start(f32[72,128]{1,0:T(8,128)S(1)} %get-tuple-element.20), channel_id=1, source_target_pairs={{0,16},{1,2},{2,1},{3,19},{16,0},{17,18},{18,17},{19,3},{4,20},{5,... | collective-permute-start | bytes 110600 | tf_op jit(solution)/shard_map/ppermute | solution.py:405
  8.4 1.0 %shard_map.87 = (bf16[16,256,256]{2,1,0:T(8,128)(2,1)S(1)}, bf16[16,256,256]{2,1,0:T(8,128)(2,1)S(1)}) custom-call(f32[8,2,33]{2,1,0:T(2,128)S(1)} %copy-done.2), custom_call_target="tpu_custom_call" | custom-call | tf_op jit(solution)/shard_map/pallas_call | solution.py:454
  9.4 0.0 collective-permute-done.first
  9.5 1.4 %collective-permute-done.1.second = f32[72,128]{1,0:T(8,128)S(1)} collective-permute-done((f32[72,128]{1,0:T(8,128)S(1)}, f32[72,128]{1,0:T(8,128)S(1)}, u32[]{:S(2)}, u32[]{:S(2)}) %collective-permute-start.1) | collective-permute-done | bytes 36896 | tf_op jit(solution)/shard_map/ppermute | solution.py:405
  10.9 0.8 %shard_map.88 = (f32[144,384]{1,0:T(8,128)S(1)}, f32[128,384]{1,0:T(8,128)S(1)}, f32[8,384]{1,0:T(8,128)S(1)}, f32[56,384]{1,0:T(8,128)S(1)}, f32[56,384]{1,0:T(8,128)S(1)}) custom-call(s32[1,1,8]{2,1,0:T(1,128)S(1)} %copy-done.5, f32[144,384]{1,0:T(8,128)S(1)} %get-tuple-element.18.partial, f32[128,256]{1,0:T(8,128)S(1)} %copy-done.1, ...), custom_call_target="tpu_custom_call" | custom-call | tf_op jit(solution)/shard_map/pallas_call | solution.py:471
  11.7 0.1 collective-permute-start.2
  11.7 1.6 %collective-permute-start.3 = (f32[56,384]{1,0:T(8,128)S(1)}, f32[56,384]{1,0:T(8,128)S(1)}, u32[]{:S(2)}, u32[]{:S(2)}) collective-permute-start(f32[56,384]{1,0:T(8,128)S(1)} %get-tuple-element.26), channel_id=1, source_target_pairs={{0,16},{4,8},{8,4},{12,28},{16,0},{20,24},{24,20},{28,12},{1,17},{... | collective-permute-start | bytes 258056 | tf_op jit(solution)/shard_map/ppermute | solution.py:405
  13.3 2.2 %shard_map.89 = (bf16[2816,512]{1,0:T(8,128)(2,1)S(1)}, bf16[144,2816]{1,0:T(8,128)(2,1)S(1)}, bf16[144,2816]{1,0:T(8,128)(2,1)S(1)}) custom-call(f32[8,2,33]{2,1,0:T(2,128)S(1)} %copy-done.3, f32[8]{0:T(128)S(1)} %copy-done.4), custom_call_target="tpu_custom_call" | custom-call | tf_op jit(solution)/shard_map/pallas_call | solution.py:459
  15.5 0.0 collective-permute-done.2.first
  15.5 0.7 %collective-permute-done.3.second = f32[56,384]{1,0:T(8,128)S(1)} collective-permute-done((f32[56,384]{1,0:T(8,128)S(1)}, f32[56,384]{1,0:T(8,128)S(1)}, u32[]{:S(2)}, u32[]{:S(2)}) %collective-permute-start.3) | collective-permute-done | bytes 86048 | tf_op jit(solution)/shard_map/ppermute | solution.py:405
  16.3 12.0 %shard_map.90 = (bf16[9,144,256]{2,1,0:T(8,128)(2,1)S(1)}, f32[16,32]{1,0:T(8,128)S(1)}) custom-call(f32[8]{0:T(128)S(1)} %copy-done.4, f32[144,384]{1,0:T(8,128)S(1)} %get-tuple-element.22.logits, f32[128,384]{1,0:T(8,128)S(1)} %get-tuple-element.23.aim, f32[8,384]{1,0:T(8,128)S(1)} %get-tuple-element.24.occupied, ...), custom_call_target="tpu_custom_call" | custom-call | tf_op jit(solution)/shard_map/pallas_call | solution.py:484
  28.3 0.7 %collective-permute-start.6 = (f32[16,32]{1,0:T(8,128)S(1)}, f32[16,32]{1,0:T(8,128)S(1)}, u32[]{:S(2)}, u32[]{:S(2)}) collective-permute-start(f32[16,32]{1,0:T(8,128)S(1)} %get-tuple-element.31), channel_id=1, source_target_pairs={{0,12},{4,8},{8,4},{12,0},{1,13},{5,9},{9,5},{13,1},{2,14},{6,10},... | collective-permute-start | bytes 6152 | tf_op jit(solution)/shard_map/ppermute | solution.py:411
  28.9 1.1 %collective-permute-start.5 = (f32[16,32]{1,0:T(8,128)S(1)}, f32[16,32]{1,0:T(8,128)S(1)}, u32[]{:S(2)}, u32[]{:S(2)}) collective-permute-start(f32[16,32]{1,0:T(8,128)S(1)} %get-tuple-element.31), channel_id=1, source_target_pairs={{0,8},{4,12},{8,0},{12,4},{1,9},{5,13},{9,1},{13,5},{2,10},{6,14},... | collective-permute-start | bytes 6152 | tf_op jit(solution)/shard_map/ppermute | solution.py:411
  30.0 0.1 collective-permute-start.4
  30.2 1.2 %collective-permute-done.6 = f32[16,32]{1,0:T(8,128)S(1)} collective-permute-done((f32[16,32]{1,0:T(8,128)S(1)}, f32[16,32]{1,0:T(8,128)S(1)}, u32[]{:S(2)}, u32[]{:S(2)}) %collective-permute-start.6) | collective-permute-done | bytes 2080 | tf_op jit(solution)/shard_map/ppermute | solution.py:411
  31.4 1.2 %collective-permute-done.5 = f32[16,32]{1,0:T(8,128)S(1)} collective-permute-done((f32[16,32]{1,0:T(8,128)S(1)}, f32[16,32]{1,0:T(8,128)S(1)}, u32[]{:S(2)}, u32[]{:S(2)}) %collective-permute-start.5) | collective-permute-done | bytes 2080 | tf_op jit(solution)/shard_map/ppermute | solution.py:411
  32.6 2.5 %collective-permute-start.9 = (f32[16,32]{1,0:T(8,128)S(1)}, f32[16,32]{1,0:T(8,128)S(1)}, u32[]{:S(2)}, u32[]{:S(2)}) collective-permute-start(f32[16,32]{1,0:T(8,128)S(1)} %add_add_fusion), channel_id=1, source_target_pairs={{0,3},{1,2},{2,1},{3,0},{4,7},{5,6},{6,5},{7,4},{8,11},{9,10},{10,... | collective-permute-start | bytes 6152 | tf_op jit(solution)/shard_map/ppermute | solution.py:411
  35.1 0.2 collective-permute-start.8
  35.3 1.7 %collective-permute-start.7 = (f32[16,32]{1,0:T(8,128)S(1)}, f32[16,32]{1,0:T(8,128)S(1)}, u32[]{:S(2)}, u32[]{:S(2)}) collective-permute-start(f32[16,32]{1,0:T(8,128)S(1)} %add_add_fusion), channel_id=1, source_target_pairs={{0,1},{1,0},{2,3},{3,2},{4,5},{5,4},{6,7},{7,6},{8,9},{9,8},{10,11... | collective-permute-start | bytes 6152 | tf_op jit(solution)/shard_map/ppermute | solution.py:411
  37.0 2.2 %shard_map.91 = bf16[32,128,256]{2,1,0:T(8,128)(2,1)} custom-call(bf16[512,288]{1,0:T(8,128)(2,1)S(1)} %get-tuple-element.32.table, bf16[9,144,256]{2,1,0:T(8,128)(2,1)S(1)} %get-tuple-element.33.shifted), custom_call_target="tpu_custom_call" | custom-call | tf_op jit(solution)/shard_map/pallas_call | solution.py:501
  39.2 0.4 %collective-permute-done.8 = f32[16,32]{1,0:T(8,128)S(1)} collective-permute-done((f32[16,32]{1,0:T(8,128)S(1)}, f32[16,32]{1,0:T(8,128)S(1)}, u32[]{:S(2)}, u32[]{:S(2)}) %collective-permute-start.8) | collective-permute-done | bytes 2080 | tf_op jit(solution)/shard_map/ppermute | solution.py:411
  39.7 0.6 %reshape.7 = f32[32,3,3]{0,2,1:T(4,128)} reshape(f32[32,9]{0,1:T(8,128)S(1)} %fusion.1) | data formatting | bytes 2304 | tf_op jit(solution)/shard_map/reshape | solution.py:511
  (17 shorter events, 0.0 us)
Async XLA Ops:
  0.6 10.2 %copy-start.5 = (s32[1,1,8]{2,1,0:T(1,128)S(1)}, s32[1,1,8]{2,1,0:T(1,128)}, u32[]{:S(2)}) copy-start(s32[1,1,8]{2,1,0:T(1,128)} %listed.1) | copy-start | bytes 100
  0.6 10.2 %copy-start.1 = (f32[128,256]{1,0:T(8,128)S(1)}, f32[128,256]{1,0:T(8,128)}, u32[]{:S(2)}) copy-start(f32[128,256]{1,0:T(8,128)} %target.1) | copy-start | bytes 393220
  0.7 7.8 %copy-start.2 = (f32[8,2,33]{2,1,0:T(2,128)S(1)}, f32[8,2,33]{2,1,0:T(2,128)}, u32[]{:S(2)}) copy-start(f32[8,2,33]{2,1,0:T(2,128)} %col_taps.1) | copy-start | bytes 6340
  0.7 12.7 %copy-start.3 = (f32[8,2,33]{2,1,0:T(2,128)S(1)}, f32[8,2,33]{2,1,0:T(2,128)}, u32[]{:S(2)}) copy-start(f32[8,2,33]{2,1,0:T(2,128)} %row_taps.1) | copy-start | bytes 6340
  0.7 12.7 %copy-start.4 = (f32[8]{0:T(128)S(1)}, f32[8]{0:T(128)}, u32[]{:S(2)}) copy-start(f32[8]{0:T(128)} %weights.1) | copy-start | bytes 100
  0.7 15.6 %copy-start = (bf16[32,128,256]{2,1,0:T(8,128)(2,1)S(1)}, bf16[32,128,256]{2,1,0:T(8,128)(2,1)}, u32[]{:S(2)}) copy-start(bf16[32,128,256]{2,1,0:T(8,128)(2,1)} %features.1) | copy-start | bytes 6291460
  3.8 5.6 %collective-permute-start = (f32[72,128]{1,0:T(8,128)S(1)}, f32[72,128]{1,0:T(8,128)S(1)}, u32[]{:S(2)}, u32[]{:S(2)}) collective-permute-start(f32[72,128]{1,0:T(8,128)S(1)} %get-tuple-element.19), channel_id=1, source_target_pairs={{0,1},{1,0},{2,3},{3,2},{4,5},{5,4},{6,7},{7,6},{8,9},{9,8},{10,11... | collective-permute-start | bytes 110600 | tf_op jit(solution)/shard_map/ppermute | solution.py:394
  6.9 4.0 %collective-permute-start.1 = (f32[72,128]{1,0:T(8,128)S(1)}, f32[72,128]{1,0:T(8,128)S(1)}, u32[]{:S(2)}, u32[]{:S(2)}) collective-permute-start(f32[72,128]{1,0:T(8,128)S(1)} %get-tuple-element.20), channel_id=1, source_target_pairs={{0,16},{1,2},{2,1},{3,19},{16,0},{17,18},{18,17},{19,3},{4,20},{5,... | collective-permute-start | bytes 110600 | tf_op jit(solution)/shard_map/ppermute | solution.py:405
  11.7 3.9 %collective-permute-start.2 = (f32[56,384]{1,0:T(8,128)S(1)}, f32[56,384]{1,0:T(8,128)S(1)}, u32[]{:S(2)}, u32[]{:S(2)}) collective-permute-start(f32[56,384]{1,0:T(8,128)S(1)} %get-tuple-element.25), channel_id=1, source_target_pairs={{0,4},{4,0},{8,12},{12,8},{1,5},{5,1},{9,13},{13,9},{2,6},{6,2},{1... | collective-permute-start | bytes 258056 | tf_op jit(solution)/shard_map/ppermute | solution.py:394
  11.7 4.6 %collective-permute-start.3 = (f32[56,384]{1,0:T(8,128)S(1)}, f32[56,384]{1,0:T(8,128)S(1)}, u32[]{:S(2)}, u32[]{:S(2)}) collective-permute-start(f32[56,384]{1,0:T(8,128)S(1)} %get-tuple-element.26), channel_id=1, source_target_pairs={{0,16},{4,8},{8,4},{12,28},{16,0},{20,24},{24,20},{28,12},{1,17},{... | collective-permute-start | bytes 258056 | tf_op jit(solution)/shard_map/ppermute | solution.py:405
  28.3 3.1 %collective-permute-start.6 = (f32[16,32]{1,0:T(8,128)S(1)}, f32[16,32]{1,0:T(8,128)S(1)}, u32[]{:S(2)}, u32[]{:S(2)}) collective-permute-start(f32[16,32]{1,0:T(8,128)S(1)} %get-tuple-element.31), channel_id=1, source_target_pairs={{0,12},{4,8},{8,4},{12,0},{1,13},{5,9},{9,5},{13,1},{2,14},{6,10},... | collective-permute-start | bytes 6152 | tf_op jit(solution)/shard_map/ppermute | solution.py:411
  28.9 3.7 %collective-permute-start.5 = (f32[16,32]{1,0:T(8,128)S(1)}, f32[16,32]{1,0:T(8,128)S(1)}, u32[]{:S(2)}, u32[]{:S(2)}) collective-permute-start(f32[16,32]{1,0:T(8,128)S(1)} %get-tuple-element.31), channel_id=1, source_target_pairs={{0,8},{4,12},{8,0},{12,4},{1,9},{5,13},{9,1},{13,5},{2,10},{6,14},... | collective-permute-start | bytes 6152 | tf_op jit(solution)/shard_map/ppermute | solution.py:411
  30.0 2.5 %collective-permute-start.4 = (f32[16,32]{1,0:T(8,128)S(1)}, f32[16,32]{1,0:T(8,128)S(1)}, u32[]{:S(2)}, u32[]{:S(2)}) collective-permute-start(f32[16,32]{1,0:T(8,128)S(1)} %get-tuple-element.31), channel_id=1, source_target_pairs={{0,4},{4,0},{8,12},{12,8},{1,5},{5,1},{9,13},{13,9},{2,6},{6,2},{1... | collective-permute-start | bytes 6152 | tf_op jit(solution)/shard_map/ppermute | solution.py:411
  32.6 6.6 %collective-permute-start.9 = (f32[16,32]{1,0:T(8,128)S(1)}, f32[16,32]{1,0:T(8,128)S(1)}, u32[]{:S(2)}, u32[]{:S(2)}) collective-permute-start(f32[16,32]{1,0:T(8,128)S(1)} %add_add_fusion), channel_id=1, source_target_pairs={{0,3},{1,2},{2,1},{3,0},{4,7},{5,6},{6,5},{7,4},{8,11},{9,10},{10,... | collective-permute-start | bytes 6152 | tf_op jit(solution)/shard_map/ppermute | solution.py:411
  35.1 4.5 %collective-permute-start.8 = (f32[16,32]{1,0:T(8,128)S(1)}, f32[16,32]{1,0:T(8,128)S(1)}, u32[]{:S(2)}, u32[]{:S(2)}) collective-permute-start(f32[16,32]{1,0:T(8,128)S(1)} %add_add_fusion), channel_id=1, source_target_pairs={{0,2},{1,3},{2,0},{3,1},{4,6},{5,7},{6,4},{7,5},{8,10},{9,11},{10,... | collective-permute-start | bytes 6152 | tf_op jit(solution)/shard_map/ppermute | solution.py:411
  35.3 4.3 %collective-permute-start.7 = (f32[16,32]{1,0:T(8,128)S(1)}, f32[16,32]{1,0:T(8,128)S(1)}, u32[]{:S(2)}, u32[]{:S(2)}) collective-permute-start(f32[16,32]{1,0:T(8,128)S(1)} %add_add_fusion), channel_id=1, source_target_pairs={{0,1},{1,0},{2,3},{3,2},{4,5},{5,4},{6,7},{7,6},{8,9},{9,8},{10,11... | collective-permute-start | bytes 6152 | tf_op jit(solution)/shard_map/ppermute | solution.py:411

commit v2 on v1

--- a/solution.py
+++ b/solution.py
@@ -60,11 +60,13 @@
         mask_rows = tile_rows + 2 * self.mask_halo
         self.depth = up(max(mask_rows, self.field_pad + taps), 128)
         self.steps = tile_rows // ROWS
+        self.reach = taps - 1
+        self.main = self.width - 128
         self.strip_rows = up(self.strip + 1 + self.field_halo, 8)
         self.fold = self.grad_pad // 2
 
 
-def row_band_kernel(s, row_taps, kernel_weight, row_band, adj_high, adj_low, flipped):
+def row_band_kernel(s, row_taps, weights, row_band, adj_high, adj_low, flipped):
     for f in range(s.filters):
         k, p = f // 2, f % 2
         pad = jnp.zeros((1, s.depth - s.taps), F32)
@@ -75,8 +77,8 @@
         here = slice(f * s.field_pad, (f + 1) * s.field_pad)
         row_band[here, : s.depth], row_band[here, s.depth :] = split(band)
         flipped[here, :] = pltpu.roll(
-            jnp.broadcast_to(row * (2.0 * kernel_weight[k]), (s.field_pad, s.depth)),
-            s.depth - (s.taps - 1),
+            jnp.broadcast_to(row * (2.0 * weights[k : k + 1, :1]), (s.field_pad, s.depth)),
+            s.depth - s.reach,
             1,
             stride=1,
             stride_axis=0,
@@ -85,28 +87,57 @@
     adj_high[...], adj_low[...] = split(turned)
 
 
-def col_band_kernel(s, col_taps, col_fwd, col_adj):
+def col_band_kernel(s, col_taps, fwd_main, fwd_last, adj_main, adj_last):
+    early = iota((128, 128), 1) < 128 - s.reach
+    blocks = s.main // 128
+    blank = jnp.zeros((128, 128), BF16)
+
+    def fill(out, f, same, below):
+        ends = split(jnp.where(early, same, 0.0))
+        same, below = split(same), split(below)
+        for part in range(2):
+            for i in range(blocks):
+                for j in range(blocks):
+                    piece = blank
+                    if i == j:
+                        piece = ends[part] if j == blocks - 1 else same[part]
+                    elif i == j + 1:
+                        piece = below[part]
+                    out[f, part, 128 * i : 128 * (i + 1), 128 * j : 128 * (j + 1)] = piece
+
     for f in range(s.filters):
         k, p = f // 2, f % 2
         pad = jnp.zeros((1, 256 - s.taps), F32)
         wide = jnp.concatenate([col_taps[k, p : p + 1, :], pad], 1)
-        band = pltpu.roll(jnp.broadcast_to(wide, (128, 256)), 0, 1, stride=1, stride_axis=0).T
-        col_fwd[f, :, :128], col_fwd[f, :, 128:] = split(band)
+        band = pltpu.roll(jnp.broadcast_to(wide, (128, 256)), 0, 1, stride=1, stride_axis=0)
+        turned = band.T
+        fill(fwd_main, f, turned[:128], turned[128:])
+        corner = jnp.concatenate([band[: 128 - s.reach, :128], band[: s.reach, :128]], 0).T
+        fwd_last[f, :, :128], fwd_last[f, :, 128:] = split(corner)
         band = pltpu.roll(
-            jnp.broadcast_to(wide, (256, 256)), 256 - (s.taps - 1), 1, stride=1, stride_axis=0
-        )
-        col_adj[f, :, :128], col_adj[f, :, 128:] = split(band[:, :128])
+            jnp.broadcast_to(wide, (256, 256)), 256 - s.reach, 1, stride=1, stride_axis=0
+        )[:, :128]
+        fill(adj_main, f, band[:128], band[128:])
+        corner = pltpu.roll(
+            jnp.broadcast_to(wide[:, :128], (128, 128)), 128 - 2 * s.reach, 1, stride=1, stride_axis=0
+        )
+        adj_last[f, :, :128], adj_last[f, :, 128:] = split(corner)
 
 
 def edge_kernel(
-    s, listed_hbm, features_hbm, conv_weight_hbm, target_hbm, table, partial, first_out, second_out,
-    acc, listed, features, conv_weight, target, sems,
+    s, listed_hbm, features_hbm, conv_weight_hbm, target_hbm, row_taps_hbm, col_taps_hbm, weights_hbm,
+    table, partial, first_out, second_out, features, target, row_taps, col_taps, weights_out, own,
+    acc, listed, conv_weight, weights, sems,
 ):
     fetch = [
         pltpu.make_async_copy(conv_weight_hbm, conv_weight, sems.at[0]),
         pltpu.make_async_copy(listed_hbm, listed, sems.at[1]),
         pltpu.make_async_copy(target_hbm, target, sems.at[2]),
+        pltpu.make_async_copy(row_taps_hbm, row_taps, sems.at[7]),
+        pltpu.make_async_copy(col_taps_hbm, col_taps, sems.at[8]),
+        pltpu.make_async_copy(weights_hbm, weights, sems.at[9]),
     ]
+    slow = len(fetch)
     parts = 4
     rows = s.rows // parts
     for q in range(parts):
@@ -133,13 +164,23 @@
     left = flat.T.astype(BF16)
     for k in range(s.steps):
         if k % (s.steps // parts) == 0:
-            fetch[3 + k // (s.steps // parts)].wait()
+            fetch[slow + k // (s.steps // parts)].wait()
         block = features[:, k * ROWS : (k + 1) * ROWS, :].reshape(s.channels * ROWS, s.cols)
         sums = dot(left, block)
         for b in range(3):
             acc[b, k * ROWS : k * ROWS + WIN, :] += sums[b * WIN : (b + 1) * WIN]
-    fetch[1].wait()
-    fetch[2].wait()
+    for copy in fetch[1:slow]:
+        copy.wait()
+    for k in range(s.filters // 2):
+        weights_out[k : k + 1, :] = jnp.broadcast_to(weights[k], (1, 128))
+    across, down = s.cols // BLOCK, s.rows // BLOCK
+    row, col = iota((8, s.width), 0), iota((8, s.width), 1) - s.mask_halo
+    inside = (col >= 0) & (col < s.cols) & (row < down)
+    number = jnp.where(inside, row * across + (col + BLOCK) // BLOCK - 1, -1)
+    used = jnp.zeros((8, s.width), F32)
+    for n in range(listed.shape[2]):
+        used = jnp.where(number == listed[0, 0, n], 1.0, used)
+    own[...] = used
     whole = jnp.zeros((s.grad_pad, s.width), F32)
     blank = jnp.zeros((s.grad_pad, s.width - s.cols), F32)
     for b in range(3):
@@ -150,7 +191,6 @@
     place, row = iota((s.grad_pad, 128), 1), iota((s.grad_pad, 128), 0)
     aim = jnp.concatenate([target[...], jnp.zeros((s.grad_pad - s.rows, s.cols), F32)], 0)
     aim = jnp.concatenate([aim, jnp.zeros((s.grad_pad, s.width - s.cols), F32)], 1)
-    across = s.cols // BLOCK
     strips = []
     for first, first_aim, block_col in (
         (s.base, 0, 0),
@@ -181,7 +221,7 @@
     )
 
 
-def middle_kernel(s, listed, partial, target, first, second, band, logits, aim, occupied, first_out, second_out):
+def middle_kernel(s, own_used, partial, target, first, second, band, logits, aim, occupied, first_out, second_out):
     extra = jnp.zeros((s.grad_pad, s.width - 128), F32)
     lane = iota((s.grad_pad, 128), 1)
     has_left, has_right, odd = neighbours("col")
@@ -203,13 +243,9 @@
     aims += placed(east, s.strip, s.field_halo, s.cols + s.field_halo)[: s.rows]
     aim[...] = aims
 
-    across, down = s.cols // BLOCK, s.rows // BLOCK
+    down = s.rows // BLOCK
     row, col = iota((8, s.width), 0), iota((8, s.width), 1) - s.mask_halo
-    inside = (col >= 0) & (col < s.cols) & (row < down)
-    number = jnp.where(inside, row * across + (col + BLOCK) // BLOCK - 1, -1)
-    used = jnp.zeros((8, s.width), F32)
-    for n in range(listed.shape[2]):
-        used = jnp.where(number == listed[0, 0, n], 1.0, used)
+    used = own_used[...]
     flag = s.strip + s.field_halo
     for r in range(down):
         here = row == r
@@ -240,10 +276,14 @@
         fill(second_out, False)
 
 
+def overlapped(s, value):
+    return jnp.concatenate([value[:, : s.main], pltpu.roll(value, s.reach, 1)[:, s.main :]], 1)
+
+
 def optics_kernel(
-    s, weights, logits, aim, occupied, first, second, row_band, col_fwd, col_adj, adj_high, adj_low,
+    s, weights, logits, aim, occupied, first, second, row_band, fwd_main, fwd_last, adj_main, adj_last, adj_high, adj_low,
     features, shifted, terms,
-    ext, aims, masks, field, pulled_high, pulled_low, total,
+    ext, aims, masks, field, pulled, total,
 ):
 
     has_left, has_right, _ = neighbours("col")
@@ -271,83 +311,66 @@
     used = jnp.where(below, south[s.strip : s.strip + 1], used)
     sigma = jax.nn.sigmoid(ext[...])
     mask = used * sigma
-    high, low = split(mask)
-    masks[: s.depth, :] = high
-    masks[s.depth : 2 * s.depth, :] = low
-    masks[2 * s.depth :, :] = high
+    high, low = split(overlapped(s, mask))
+    for here in (slice(0, s.depth), slice(s.depth, 2 * s.depth)):
+        masks[here, : s.width] = high
+        masks[here, s.width :] = low
     slope = (mask * (1.0 - sigma))[s.base : s.base + s.grad_pad]
     slope = pltpu.roll(slope, s.width - s.base, 1)
 
-    blocks = -(-s.field_cols // 128)
     total[...] = jnp.zeros_like(total)
     group = 4
     tall = group * s.field_pad
-    gap = jnp.zeros((s.field_pad, 128), BF16)
-
-    def windows(high, low, count):
-        rows = []
-        for n in range(count):
-            line = []
-            for part in (high, low):
-                line.append(part[:, 128 * n : min(128 * n + 256, s.width)])
-                if 128 * n + 256 > s.width:
-                    line.append(gap)
-            rows.append(jnp.concatenate(line, 1))
-        return jnp.concatenate(rows, 0)
-
-    def doubled(band):
-        return jnp.concatenate([band, band], 0)
-
-    def forward(g, carry):
-        start = pl.multiple_of(g * tall, 16)
-        band = row_band[pl.ds(start, tall), :]
-        stack = jnp.concatenate([band[:, : s.depth], band[:, : s.depth], band[:, s.depth :]], 1)
-        rowed = dot(stack, masks[...])
+    late = iota((s.field_pad, 128), 1) >= 128 - s.reach
+
+    def banded(high, low, main, last):
+        ends = jnp.concatenate([high[:, s.main :], low[:, s.main :]], 1)
+        both = dot(ends, jnp.concatenate([last, last], 0))
+        tail = both[:, :128] + both[:, 128:]
+        high, low = high[:, : s.main], low[:, : s.main]
+        stack = jnp.concatenate([main[0], main[0], main[1]], 0)
+        head = dot(jnp.concatenate([high, low, high], 1), stack)
+        seam = head[:, s.main - 128 :] + jnp.where(late, tail, 0.0)
+        pieces = [seam, tail]
+        if s.main > 128:
+            pieces.insert(0, head[:, : s.main - 128])
+        return jnp.concatenate(pieces, 1)
+
+    for g in range(s.filters // group):
+        band = row_band[g * tall : (g + 1) * tall, :]
+        one = dot(band, masks[:, : s.width + 128])
+        two = dot(band[:, : s.depth], masks[: s.depth, s.width + 128 :])
+        rowed = one[:, : s.width] + jnp.concatenate([one[:, s.width :], two], 1)
         for i in range(0, group, 2):
             squares = 0.0
-            for f in (i, i + 1):
-                high, low = split(rowed[f * s.field_pad : (f + 1) * s.field_pad])
-                both = dot(windows(high, low, blocks), doubled(col_fwd[g * group + f]))
-                value = both[:, :128] + both[:, 128:]
-                for n in range(blocks):
-                    here = slice(n * s.field_pad, (n + 1) * s.field_pad)
-                    field[g * group + f, :, 128 * n : 128 * (n + 1)] = value[here]
+            for j in (i, i + 1):
+                f = g * group + j
+                high, low = split(rowed[j * s.field_pad : (j + 1) * s.field_pad])
+                value = banded(high, low, fwd_main[f], fwd_last[f])
+                field[f] = value
                 squares += value * value
-            squares *= weights[(g * group + i) // 2]
-            for n in range(blocks):
-                total[:, 128 * n : 128 * (n + 1)] += squares[n * s.field_pad : (n + 1) * s.field_pad]
-        return carry
-
-    lax.fori_loop(0, s.filters // group, forward, 0)
-
-    row, col = iota((s.field_pad, s.width), 0) - s.field_halo, iota((s.field_pad, s.width), 1) - s.field_halo
+            k = (g * group + i) // 2
+            total[...] += squares * weights[k : k + 1, :1]
+
+    row, lane = iota((s.field_pad, s.width), 0) - s.field_halo, iota((s.field_pad, s.width), 1)
+    col = jnp.where(lane < s.main, lane, lane - s.reach) - s.field_halo
     inside = ((row >= 0) | has_up) & ((row < s.rows) | has_down) & (row < s.rows + s.field_halo)
     inside &= ((col >= 0) | has_left) & ((col < s.cols) | has_right) & (col < s.cols + s.field_halo)
-    total[...] = jnp.where(inside, total[...] - aims[...], 0.0)
-    out_blocks = -(-(s.cols + 2) // 128)
-    if blocks * 128 < s.width:
-        field[:, :, blocks * 128 :] = jnp.zeros_like(field[:, :, blocks * 128 :])
-
-    def backward(g, carry):
-        for i in range(group):
-            f = g * group + i
-            high, low = split(total[...] * field[f])
-            start = pl.multiple_of(f * s.field_pad, 16)
-            both = dot(windows(high, low, out_blocks), doubled(col_adj[f]))
-            high, low = split(both[:, :128] + both[:, 128:])
-            for n in range(out_blocks):
-                here = slice(n * s.field_pad, (n + 1) * s.field_pad)
-                pulled_high[pl.ds(start, s.field_pad), 128 * n : 128 * (n + 1)] = high[here]
-                pulled_low[pl.ds(start, s.field_pad), 128 * n : 128 * (n + 1)] = low[here]
-        return carry
-
-    lax.fori_loop(0, s.filters // group, backward, 0)
-    if out_blocks * 128 < s.width:
-        pulled_high[:, out_blocks * 128 :] = jnp.zeros_like(pulled_high[:, out_blocks * 128 :])
-        pulled_low[:, out_blocks * 128 :] = jnp.zeros_like(pulled_low[:, out_blocks * 128 :])
-    both = dot(jnp.concatenate([adj_high[...], adj_low[...]], 0), pulled_high[...])
-    grad = both[: s.grad_pad] + both[s.grad_pad :] + dot(adj_high[...], pulled_low[...])
-    grad = grad * slope
+    total[...] = jnp.where(inside, total[...] - overlapped(s, aims[...]), 0.0)
+
+    for f in range(s.filters):
+        high, low = split(total[...] * field[f])
+        high, low = split(banded(high, low, adj_main[f], adj_last[f]))
+        rows = slice(f * s.field_pad, (f + 1) * s.field_pad)
+        pulled[rows, : s.width] = high
+        pulled[rows, s.width : s.width + 128] = low[:, s.main :]
+        pulled[rows, s.width + 128 :] = low[:, : s.main]
+
+    both = dot(jnp.concatenate([adj_high[...], adj_low[...]], 0), pulled[:, : s.width + 128])
+    rest = both[: s.grad_pad, s.width :]
+    both = both[: s.grad_pad, : s.width] + both[s.grad_pad :, : s.width]
+    low = dot(adj_high[...], pulled[:, s.width + 128 :])
+    grad = jnp.concatenate([both[:, : s.main] + low, both[:, s.main :] + rest], 1) * slope
 
     for b in range(3):
         moved = grad if b == 2 else pltpu.roll(grad, s.width - (2 - b), 1)
@@ -417,7 +440,7 @@
     channels, tile_rows, tile_cols = features.shape
     s = Sizes(channels, tile_rows, tile_cols, row_taps.shape[2], row_taps.shape[0] * 2)
     shape = jax.ShapeDtypeStruct
-    smem, hbm = spec(pltpu.SMEM), spec(pltpu.HBM)
+    hbm = spec(pltpu.HBM)
 
     def call(body, outs, ins, scratch=(), limit=24, out_space=pltpu.VMEM):
         return pl.pallas_call(
@@ -430,32 +453,45 @@
         )
 
     half_strip = shape((s.fold, 128), F32)
-    table, partial, first, second = call(
+    table, partial, first, second, features_here, target_here, row_here, col_here, weights, own = call(
         edge_kernel,
         (
             shape((channels * ROWS, 9 * WIN), BF16),
             shape((s.grad_pad, s.width), F32),
             half_strip,
             half_strip,
+            shape(features.shape, BF16),
+            shape(target.shape, F32),
+            shape(row_taps.shape, F32),
+            shape(col_taps.shape, F32),
+            shape((8 * -(-s.filters // 16), 128), F32),
+            shape((8, s.width), F32),
         ),
-        [hbm] * 4,
+        [hbm] * 7,
         [
             pltpu.VMEM((3, s.rows + WIN, s.cols), F32),
             pltpu.SMEM(block_list.shape, jnp.int32),
-            pltpu.VMEM(features.shape, BF16),
             pltpu.VMEM((3, 3, channels), BF16),
-            pltpu.VMEM(target.shape, F32),
-            pltpu.SemaphoreType.DMA((7,)),
+            pltpu.SMEM(kernel_weight.shape, F32),
+            pltpu.SemaphoreType.DMA((10,)),
         ],
-    )(*(pltpu.with_memory_space_constraint(x, pltpu.HBM) for x in (block_list, features, conv_weight.transpose(1, 2, 0), target)))
+    )(
+        *(
+            pltpu.with_memory_space_constraint(x, pltpu.HBM)
+            for x in (
+                block_list, features, conv_weight.transpose(1, 2, 0), target, row_taps, col_taps,
+                kernel_weight,
+            )
+        )
+    )
     first, second = exchanged(first, second, "col")
 
     filters = s.filters
     col_bands = call(
         col_band_kernel,
-        (shape((filters, 256, 256), BF16), shape((filters, 256, 256), BF16)),
+        (shape((filters, 2, s.main, s.main), BF16), shape((filters, 128, 256), BF16)) * 2,
         [spec()],
-    )(col_taps)
+    )(col_here)
     row_bands = call(
         row_band_kernel,
         (
@@ -463,9 +499,9 @@
             shape((s.grad_pad, filters * s.field_pad), BF16),
             shape((s.grad_pad, filters * s.field_pad), BF16),
         ),
-        [spec(), smem],
+        [spec(), spec()],
         [pltpu.VMEM((filters * s.field_pad, s.depth), F32)],
-    )(row_taps, kernel_weight)
+    )(row_here, weights)
 
     row_strip = shape((s.strip_rows, s.width), F32)
     logits, aim, occupied, first, second = call(
@@ -477,25 +513,24 @@
             row_strip,
             row_strip,
         ),
-        [smem, spec(), spec(), spec(), spec(), spec()],
-    )(block_list, partial, target, first, second, col_bands[0])
+        [spec()] * 6,
+    )(own, partial, target_here, first, second, col_bands[1])
     first, second = exchanged(first, second, "row")
 
     shifted, terms = call(
         optics_kernel,
         (shape((9, s.grad_pad, s.cols), BF16), shape((16, channels), F32)),
-        [smem] + [spec()] * 11,
+        [spec()] * 14,
         [
             pltpu.VMEM((s.depth, s.width), F32),
             pltpu.VMEM((s.field_pad, s.width), F32),
-            pltpu.VMEM((3 * s.depth, s.width), BF16),
+            pltpu.VMEM((2 * s.depth, 2 * s.width), BF16),
             pltpu.VMEM((filters, s.field_pad, s.width), F32),
-            pltpu.VMEM((filters * s.field_pad, s.width), BF16),
-            pltpu.VMEM((filters * s.field_pad, s.width), BF16),
+            pltpu.VMEM((filters * s.field_pad, 2 * s.width), BF16),
             pltpu.VMEM((s.field_pad, s.width), F32),
         ],
         32,
-    )(kernel_weight, logits, aim, occupied, first, second, *row_bands[:1], *col_bands, *row_bands[1:], features)
+    )(weights, logits, aim, occupied, first, second, *row_bands[:1], *col_bands, *row_bands[1:], features_here)
 
     by_row = summed(terms, "row")
     grad_features = call(

time: 40.4 us -> 37.9 us (0.938)
  Pallas kernels: 21.3 us -> 19.7 us
  waiting for transfers between devices: 4.99 us -> 4.04 us
    pallas_call x1, Pallas kernels: 12 us -> 9.44 us  [on_device(): call(optics_kernel, (shape((9, s.grad_pad, s.cols), BF16), shape((16, cha...]
    ppermute x2, waiting for transfers between devices: 2.15 us -> 0.73 us  [exchanged(): return (one, lax.ppermute(second, ('grp', axis), pairs))]
    pallas_call x1, Pallas kernels: 1.01 us -> 1.84 us  [on_device(): call(col_band_kernel, (shape((filters, 2, s.main, s.main), BF16), shape((...]
    pallas_call x1, Pallas kernels: 2.2 us -> 2.81 us  [on_device(): call(row_band_kernel, (shape((filters * s.field_pad, 2 * s.depth), BF16),...]
    ppermute x6, waiting for transfers between devices: 2.84 us -> 3.31 us  [summed(): lax.ppermute(value, axis, [(i, i ^ step) for i in range(size)])]
  transfers between devices with their start and end apart: 10 -> 10, of which waited for: 5 -> 5; matrix products, arithmetic and copies ran while one was open for 0% -> 0% of each run, Pallas kernels for 13% -> 18%
where the time goes in v2:
time: 37.9 us; the launch traced here: 37.7 us
  Pallas kernels  19.7 us (52%)
  starting transfers between devices  12.6 us (33%)
  waiting for transfers between devices  4.04 us (11%)
  between operations  0.71 us (2%)
  local copies, waits for them, and re-layouts  0.6 us (2%)
    pallas_call x1, Pallas kernels, on_device(): call(optics_kernel, (shape((9, s.grad_pad, s.cols), BF16), shape((16, cha...  9.44 us
    ppermute x6, starting transfers between devices, summed(): lax.ppermute(value, axis, [(i, i ^ step) for i in range(size)])  6.37 us
    ppermute x6, waiting for transfers between devices, summed(): lax.ppermute(value, axis, [(i, i ^ step) for i in range(size)])  3.31 us
    ppermute x2, starting transfers between devices, exchanged(): one = lax.ppermute(first, axis, [(i, i ^ 1) for i in range(size)])  3.16 us
    ppermute x2, starting transfers between devices, exchanged(): return (one, lax.ppermute(second, ('grp', axis), pairs))  3.11 us
    pallas_call x1, Pallas kernels, on_device(): call(edge_kernel, (shape((channels * ROWS, 9 * WIN), BF16), shape((s.grad...  3.01 us
    pallas_call x1, Pallas kernels, on_device(): call(row_band_kernel, (shape((filters * s.field_pad, 2 * s.depth), BF16),...  2.81 us
    pallas_call x1, Pallas kernels, on_device(): call(feature_kernel, shape(features.shape, BF16), [spec(), spec()], [pltp...  2.19 us
  transfers between devices with their start and end apart: 10, of which 5 were waited for; matrix products, arithmetic and copies ran while one was open for 0% of the time, Pallas kernels for 18%

profile of v2, /device:TPU:0, one launch (start us, length us, event | category | flops | bytes accessed | tf_op | source)
XLA Modules:
  0.0 37.7 jit_solution(3750983572461727371)
XLA Ops:
  0.6 3.0 %shard_map.86 = (bf16[512,288]{1,0:T(8,128)(2,1)S(1)}, f32[144,384]{1,0:T(8,128)S(1)}, f32[72,128]{1,0:T(8,128)S(1)}, f32[72,128]{1,0:T(8,128)S(1)}, bf16[32,128...) custom-call(s32[1,1,8]{2,1,0:T(1,128)} %listed_hbm.1, ...), custom_call_target="tpu_custom_call" | custom-call | tf_op jit(solution)/shard_map/pallas_call | solution.py:456
  3.7 3.1 %collective-permute-start = (f32[72,128]{1,0:T(8,128)S(1)}, f32[72,128]{1,0:T(8,128)S(1)}, u32[]{:S(2)}, u32[]{:S(2)}) collective-permute-start(f32[72,128]{1,0:T(8,128)S(1)} %get-tuple-element.30), channel_id=1, source_target_pairs={{0,1},{1,0},{2,3},{3,2},{4,5},{5,4},{6,7},{7,6},{8,9},{9,8},{10,11... | collective-permute-start | bytes 110600 | tf_op jit(solution)/shard_map/ppermute | solution.py:417
  6.7 1.5 %collective-permute-start.1 = (f32[72,128]{1,0:T(8,128)S(1)}, f32[72,128]{1,0:T(8,128)S(1)}, u32[]{:S(2)}, u32[]{:S(2)}) collective-permute-start(f32[72,128]{1,0:T(8,128)S(1)} %get-tuple-element.31), channel_id=1, source_target_pairs={{0,16},{1,2},{2,1},{3,19},{16,0},{17,18},{18,17},{19,3},{4,20},{5,... | collective-permute-start | bytes 110600 | tf_op jit(solution)/shard_map/ppermute | solution.py:428
  8.3 1.8 %shard_map.87 = (bf16[16,2,256,256]{3,2,1,0:T(8,128)(2,1)S(1)}, bf16[16,128,256]{2,1,0:T(8,128)(2,1)S(1)}, bf16[16,2,256,256]{3,2,1,0:T(8,128)(2,1)S(1)}, bf16[16,128,256]{2,1,0:T(8,128)(2,1)S(1)}) custom-call(f32[8,2,33]{2,1,0:T(2,128)S(1)} %get-tuple-element.32.col_taps), custom_call_target="tpu_custom_call" | custom-call | tf_op jit(solution)/shard_map/pallas_call | solution.py:490
  10.1 0.0 collective-permute-done.first
  10.1 0.6 %collective-permute-done.1.second = f32[72,128]{1,0:T(8,128)S(1)} collective-permute-done((f32[72,128]{1,0:T(8,128)S(1)}, f32[72,128]{1,0:T(8,128)S(1)}, u32[]{:S(2)}, u32[]{:S(2)}) %collective-permute-start.1) | collective-permute-done | bytes 36896 | tf_op jit(solution)/shard_map/ppermute | solution.py:428
  10.7 0.4 %shard_map.88 = (f32[144,384]{1,0:T(8,128)S(1)}, f32[128,384]{1,0:T(8,128)S(1)}, f32[8,384]{1,0:T(8,128)S(1)}, f32[56,384]{1,0:T(8,128)S(1)}, f32[56,384]{1,0:T(8,128)S(1)}) custom-call(f32[8,384]{1,0:T(8,128)S(1)} %get-tuple-element.27.own_used, f32[144,384]{1,0:T(8,128)S(1)} %get-tuple-element.28.partial, f32[128,256]{1,0:T(8,128)S(1)} %get-tuple-element.29.target, ...), custom_call_target="tpu_custom_call" | custom-call | tf_op jit(solution)/shard_map/pallas_call | solution.py:507
  11.1 0.1 collective-permute-start.2
  11.2 1.6 %collective-permute-start.3 = (f32[56,384]{1,0:T(8,128)S(1)}, f32[56,384]{1,0:T(8,128)S(1)}, u32[]{:S(2)}, u32[]{:S(2)}) collective-permute-start(f32[56,384]{1,0:T(8,128)S(1)} %get-tuple-element.38), channel_id=1, source_target_pairs={{0,16},{4,8},{8,4},{12,28},{16,0},{20,24},{24,20},{28,12},{1,17},{... | collective-permute-start | bytes 258056 | tf_op jit(solution)/shard_map/ppermute | solution.py:428
  12.8 2.8 %shard_map.89 = (bf16[2816,512]{1,0:T(8,128)(2,1)S(1)}, bf16[144,2816]{1,0:T(8,128)(2,1)S(1)}, bf16[144,2816]{1,0:T(8,128)(2,1)S(1)}) custom-call(f32[8,2,33]{2,1,0:T(2,128)S(1)} %get-tuple-element.39.row_taps, f32[8,128]{1,0:T(8,128)S(1)} %get-tuple-element.26.weights), custom_call_target="tpu_custom_call" | custom-call | tf_op jit(solution)/shard_map/pallas_call | solution.py:495
  15.6 0.0 collective-permute-done.2.first
  15.6 0.1 collective-permute-done.3.second
  15.8 9.4 %shard_map.90 = (bf16[9,144,256]{2,1,0:T(8,128)(2,1)S(1)}, f32[16,32]{1,0:T(8,128)S(1)}) custom-call(f32[8,128]{1,0:T(8,128)S(1)} %get-tuple-element.26.weights, f32[144,384]{1,0:T(8,128)S(1)} %get-tuple-element.34.logits, f32[128,384]{1,0:T(8,128)S(1)} %get-tuple-element.35.aim, f32[8,384]{1,0:T(8,128)S(1)} %get-tuple-element.36.occupied, ...), custom_call_target="tpu_custom_call" | custom-call | tf_op jit(solution)/shard_map/pallas_call | solution.py:520
  25.2 1.1 %collective-permute-start.6 = (f32[16,32]{1,0:T(8,128)S(1)}, f32[16,32]{1,0:T(8,128)S(1)}, u32[]{:S(2)}, u32[]{:S(2)}) collective-permute-start(f32[16,32]{1,0:T(8,128)S(1)} %get-tuple-element.47), channel_id=1, source_target_pairs={{0,12},{4,8},{8,4},{12,0},{1,13},{5,9},{9,5},{13,1},{2,14},{6,10},... | collective-permute-start | bytes 6152 | tf_op jit(solution)/shard_map/ppermute | solution.py:434
  26.3 0.6 %collective-permute-start.5 = (f32[16,32]{1,0:T(8,128)S(1)}, f32[16,32]{1,0:T(8,128)S(1)}, u32[]{:S(2)}, u32[]{:S(2)}) collective-permute-start(f32[16,32]{1,0:T(8,128)S(1)} %get-tuple-element.47), channel_id=1, source_target_pairs={{0,8},{4,12},{8,0},{12,4},{1,9},{5,13},{9,1},{13,5},{2,10},{6,14},... | collective-permute-start | bytes 6152 | tf_op jit(solution)/shard_map/ppermute | solution.py:434
  27.0 0.1 collective-permute-start.4
  27.1 1.2 %collective-permute-done.6 = f32[16,32]{1,0:T(8,128)S(1)} collective-permute-done((f32[16,32]{1,0:T(8,128)S(1)}, f32[16,32]{1,0:T(8,128)S(1)}, u32[]{:S(2)}, u32[]{:S(2)}) %collective-permute-start.6) | collective-permute-done | bytes 2080 | tf_op jit(solution)/shard_map/ppermute | solution.py:434
  28.3 1.7 %collective-permute-done.5 = f32[16,32]{1,0:T(8,128)S(1)} collective-permute-done((f32[16,32]{1,0:T(8,128)S(1)}, f32[16,32]{1,0:T(8,128)S(1)}, u32[]{:S(2)}, u32[]{:S(2)}) %collective-permute-start.5) | collective-permute-done | bytes 2080 | tf_op jit(solution)/shard_map/ppermute | solution.py:434
  30.0 2.5 %collective-permute-start.9 = (f32[16,32]{1,0:T(8,128)S(1)}, f32[16,32]{1,0:T(8,128)S(1)}, u32[]{:S(2)}, u32[]{:S(2)}) collective-permute-start(f32[16,32]{1,0:T(8,128)S(1)} %add_add_fusion), channel_id=1, source_target_pairs={{0,3},{1,2},{2,1},{3,0},{4,7},{5,6},{6,5},{7,4},{8,11},{9,10},{10,... | collective-permute-start | bytes 6152 | tf_op jit(solution)/shard_map/ppermute | solution.py:434
  32.5 0.2 collective-permute-start.8
  32.7 1.7 %collective-permute-start.7 = (f32[16,32]{1,0:T(8,128)S(1)}, f32[16,32]{1,0:T(8,128)S(1)}, u32[]{:S(2)}, u32[]{:S(2)}) collective-permute-start(f32[16,32]{1,0:T(8,128)S(1)} %add_add_fusion), channel_id=1, source_target_pairs={{0,1},{1,0},{2,3},{3,2},{4,5},{5,4},{6,7},{7,6},{8,9},{9,8},{10,11... | collective-permute-start | bytes 6152 | tf_op jit(solution)/shard_map/ppermute | solution.py:434
  34.5 2.2 %shard_map.91 = bf16[32,128,256]{2,1,0:T(8,128)(2,1)} custom-call(bf16[512,288]{1,0:T(8,128)(2,1)S(1)} %get-tuple-element.48.table, bf16[9,144,256]{2,1,0:T(8,128)(2,1)S(1)} %get-tuple-element.49.shifted), custom_call_target="tpu_custom_call" | custom-call | tf_op jit(solution)/shard_map/pallas_call | solution.py:536
  36.7 0.4 %collective-permute-done.8 = f32[16,32]{1,0:T(8,128)S(1)} collective-permute-done((f32[16,32]{1,0:T(8,128)S(1)}, f32[16,32]{1,0:T(8,128)S(1)}, u32[]{:S(2)}, u32[]{:S(2)}) %collective-permute-start.8) | collective-permute-done | bytes 2080 | tf_op jit(solution)/shard_map/ppermute | solution.py:434
  37.1 0.6 %reshape.7 = f32[32,3,3]{0,2,1:T(4,128)} reshape(f32[32,9]{0,1:T(8,128)S(1)} %fusion.1) | data formatting | bytes 2304 | tf_op jit(solution)/shard_map/reshape | solution.py:546
  (5 shorter events, 0.0 us)
Async XLA Ops:
  3.7 6.5 %collective-permute-start = (f32[72,128]{1,0:T(8,128)S(1)}, f32[72,128]{1,0:T(8,128)S(1)}, u32[]{:S(2)}, u32[]{:S(2)}) collective-permute-start(f32[72,128]{1,0:T(8,128)S(1)} %get-tuple-element.30), channel_id=1, source_target_pairs={{0,1},{1,0},{2,3},{3,2},{4,5},{5,4},{6,7},{7,6},{8,9},{9,8},{10,11... | collective-permute-start | bytes 110600 | tf_op jit(solution)/shard_map/ppermute | solution.py:417
  6.7 4.0 %collective-permute-start.1 = (f32[72,128]{1,0:T(8,128)S(1)}, f32[72,128]{1,0:T(8,128)S(1)}, u32[]{:S(2)}, u32[]{:S(2)}) collective-permute-start(f32[72,128]{1,0:T(8,128)S(1)} %get-tuple-element.31), channel_id=1, source_target_pairs={{0,16},{1,2},{2,1},{3,19},{16,0},{17,18},{18,17},{19,3},{4,20},{5,... | collective-permute-start | bytes 110600 | tf_op jit(solution)/shard_map/ppermute | solution.py:428
  11.1 4.5 %collective-permute-start.2 = (f32[56,384]{1,0:T(8,128)S(1)}, f32[56,384]{1,0:T(8,128)S(1)}, u32[]{:S(2)}, u32[]{:S(2)}) collective-permute-start(f32[56,384]{1,0:T(8,128)S(1)} %get-tuple-element.37), channel_id=1, source_target_pairs={{0,4},{4,0},{8,12},{12,8},{1,5},{5,1},{9,13},{13,9},{2,6},{6,2},{1... | collective-permute-start | bytes 258056 | tf_op jit(solution)/shard_map/ppermute | solution.py:417
  11.2 4.6 %collective-permute-start.3 = (f32[56,384]{1,0:T(8,128)S(1)}, f32[56,384]{1,0:T(8,128)S(1)}, u32[]{:S(2)}, u32[]{:S(2)}) collective-permute-start(f32[56,384]{1,0:T(8,128)S(1)} %get-tuple-element.38), channel_id=1, source_target_pairs={{0,16},{4,8},{8,4},{12,28},{16,0},{20,24},{24,20},{28,12},{1,17},{... | collective-permute-start | bytes 258056 | tf_op jit(solution)/shard_map/ppermute | solution.py:428
  25.2 3.1 %collective-permute-start.6 = (f32[16,32]{1,0:T(8,128)S(1)}, f32[16,32]{1,0:T(8,128)S(1)}, u32[]{:S(2)}, u32[]{:S(2)}) collective-permute-start(f32[16,32]{1,0:T(8,128)S(1)} %get-tuple-element.47), channel_id=1, source_target_pairs={{0,12},{4,8},{8,4},{12,0},{1,13},{5,9},{9,5},{13,1},{2,14},{6,10},... | collective-permute-start | bytes 6152 | tf_op jit(solution)/shard_map/ppermute | solution.py:434
  26.3 3.7 %collective-permute-start.5 = (f32[16,32]{1,0:T(8,128)S(1)}, f32[16,32]{1,0:T(8,128)S(1)}, u32[]{:S(2)}, u32[]{:S(2)}) collective-permute-start(f32[16,32]{1,0:T(8,128)S(1)} %get-tuple-element.47), channel_id=1, source_target_pairs={{0,8},{4,12},{8,0},{12,4},{1,9},{5,13},{9,1},{13,5},{2,10},{6,14},... | collective-permute-start | bytes 6152 | tf_op jit(solution)/shard_map/ppermute | solution.py:434
  27.0 3.0 %collective-permute-start.4 = (f32[16,32]{1,0:T(8,128)S(1)}, f32[16,32]{1,0:T(8,128)S(1)}, u32[]{:S(2)}, u32[]{:S(2)}) collective-permute-start(f32[16,32]{1,0:T(8,128)S(1)} %get-tuple-element.47), channel_id=1, source_target_pairs={{0,4},{4,0},{8,12},{12,8},{1,5},{5,1},{9,13},{13,9},{2,6},{6,2},{1... | collective-permute-start | bytes 6152 | tf_op jit(solution)/shard_map/ppermute | solution.py:434
  30.0 6.7 %collective-permute-start.9 = (f32[16,32]{1,0:T(8,128)S(1)}, f32[16,32]{1,0:T(8,128)S(1)}, u32[]{:S(2)}, u32[]{:S(2)}) collective-permute-start(f32[16,32]{1,0:T(8,128)S(1)} %add_add_fusion), channel_id=1, source_target_pairs={{0,3},{1,2},{2,1},{3,0},{4,7},{5,6},{6,5},{7,4},{8,11},{9,10},{10,... | collective-permute-start | bytes 6152 | tf_op jit(solution)/shard_map/ppermute | solution.py:434
  32.5 4.5 %collective-permute-start.8 = (f32[16,32]{1,0:T(8,128)S(1)}, f32[16,32]{1,0:T(8,128)S(1)}, u32[]{:S(2)}, u32[]{:S(2)}) collective-permute-start(f32[16,32]{1,0:T(8,128)S(1)} %add_add_fusion), channel_id=1, source_target_pairs={{0,2},{1,3},{2,0},{3,1},{4,6},{5,7},{6,4},{7,5},{8,10},{9,11},{10,... | collective-permute-start | bytes 6152 | tf_op jit(solution)/shard_map/ppermute | solution.py:434
  32.7 4.4 %collective-permute-start.7 = (f32[16,32]{1,0:T(8,128)S(1)}, f32[16,32]{1,0:T(8,128)S(1)}, u32[]{:S(2)}, u32[]{:S(2)}) collective-permute-start(f32[16,32]{1,0:T(8,128)S(1)} %add_add_fusion), channel_id=1, source_target_pairs={{0,1},{1,0},{2,3},{3,2},{4,5},{5,4},{6,7},{7,6},{8,9},{9,8},{10,11... | collective-permute-start | bytes 6152 | tf_op jit(solution)/shard_map/ppermute | solution.py:434

commit v3 on v2

--- a/solution.py
+++ b/solution.py
@@ -58,6 +58,7 @@
         self.field_pad = up(self.field_rows, 16)
         self.grad_pad = tile_rows + ROWS
         mask_rows = tile_rows + 2 * self.mask_halo
+        self.mask_pad = up(mask_rows, 16)
         self.depth = up(max(mask_rows, self.field_pad + taps), 128)
         self.steps = tile_rows // ROWS
         self.reach = taps - 1
@@ -122,6 +123,13 @@
             jnp.broadcast_to(wide[:, :128], (128, 128)), 128 - 2 * s.reach, 1, stride=1, stride_axis=0
         )
         adj_last[f, :, :128], adj_last[f, :, 128:] = split(corner)
+
+
+def pulled_tile(value, start, lane):
+    first = start // 128 * 128
+    tile = value[:, first : first + 128]
+    shift = (lane - start) % 128
+    return pltpu.roll(tile, shift, 1) if shift else tile
 
 
 def edge_kernel(
@@ -148,7 +156,7 @@
     for copy in fetch:
         copy.start()
     acc[...] = jnp.zeros_like(acc)
-    lanes = 3 * WIN
+    lanes = 128
     u, lane = iota((s.channels * ROWS, lanes), 0) % ROWS, iota((s.channels * ROWS, lanes), 1)
     h = lane % WIN
     owner = jnp.where(
@@ -160,15 +168,16 @@
     for row_shift in range(3):
         spread = dot(conv_weight[row_shift].astype(F32), pick, ((0,), (0,))).astype(BF16)
         flat = jnp.where(h == u - row_shift + 2, dot(owner, spread), flat)
-    table[...] = jnp.concatenate([flat.astype(BF16)] * 3, 1)
-    left = flat.T.astype(BF16)
+    table[...] = flat.astype(BF16)
+    left = flat.T[: 3 * WIN].astype(BF16)
     for k in range(s.steps):
         if k % (s.steps // parts) == 0:
             fetch[slow + k // (s.steps // parts)].wait()
         block = features[:, k * ROWS : (k + 1) * ROWS, :].reshape(s.channels * ROWS, s.cols)
-        sums = dot(left, block)
-        for b in range(3):
-            acc[b, k * ROWS : k * ROWS + WIN, :] += sums[b * WIN : (b + 1) * WIN]
+        for n in range(0, s.cols, 128):
+            sums = dot(left, block[:, n : n + 128])
+            for b in range(3):
+                acc[b, k * ROWS : k * ROWS + WIN, n : n + 128] += sums[b * WIN : (b + 1) * WIN]
     for copy in fetch[1:slow]:
         copy.wait()
     for k in range(s.filters // 2):
@@ -189,15 +198,14 @@
     partial[...] = whole
 
     place, row = iota((s.grad_pad, 128), 1), iota((s.grad_pad, 128), 0)
-    aim = jnp.concatenate([target[...], jnp.zeros((s.grad_pad - s.rows, s.cols), F32)], 0)
-    aim = jnp.concatenate([aim, jnp.zeros((s.grad_pad, s.width - s.cols), F32)], 1)
+    filler = jnp.zeros((s.grad_pad - s.rows, 128), F32)
     strips = []
     for first, first_aim, block_col in (
         (s.base, 0, 0),
         (s.cols, s.cols - s.field_halo, across - 1),
     ):
-        logits = pltpu.roll(whole, (s.width - first) % s.width, 1)[:, :128]
-        wanted = pltpu.roll(aim, (s.width - first_aim + s.strip) % s.width, 1)[:, :128]
+        logits, wanted = pulled_tile(whole, first, 0), pulled_tile(target[...], first_aim, s.strip)
+        wanted = jnp.concatenate([wanted, filler], 0)
         number = (row // BLOCK) * across + block_col
         used = jnp.zeros((s.grad_pad, 128), F32)
         for n in range(listed.shape[2]):
@@ -222,7 +230,6 @@
 
 
 def middle_kernel(s, own_used, partial, target, first, second, band, logits, aim, occupied, first_out, second_out):
-    extra = jnp.zeros((s.grad_pad, s.width - 128), F32)
     lane = iota((s.grad_pad, 128), 1)
     has_left, has_right, odd = neighbours("col")
     one, two = first[...], second[...]
@@ -231,8 +238,10 @@
 
     def placed(value, keep_from, keep, offset):
         kept = jnp.where((lane >= keep_from) & (lane < keep_from + keep), value, 0.0)
-        wide = jnp.concatenate([kept, extra], 1)
-        return pltpu.roll(wide, (offset - keep_from) % s.width, 1)
+        shift = (offset - keep_from) % 128
+        kept = pltpu.roll(kept, shift, 1) if shift else kept
+        blank = jnp.zeros((s.grad_pad, 128), F32)
+        return jnp.concatenate([kept if n == offset // 128 else blank for n in range(s.width // 128)], 1)
 
     whole = partial[...] + placed(west, 0, s.strip, 0)
     whole += placed(east, 0, s.strip, s.cols + s.base)
@@ -303,7 +312,7 @@
     aims[s.field_halo : s.field_halo + s.rows, :] = aim[...]
     aims[s.field_halo + s.rows : s.field_rows, :] = south[s.strip + 1 : s.strip + 1 + s.field_halo]
 
-    place = iota((s.depth, s.width), 0) - s.mask_halo
+    place = iota((s.mask_pad, s.width), 0) - s.mask_halo
     used = jnp.where(place < 0, north[s.strip : s.strip + 1], 0.0)
     for r in range(s.rows // BLOCK):
         used = jnp.where((place >= r * BLOCK) & (place < (r + 1) * BLOCK), occupied[r : r + 1, :], used)
@@ -312,14 +321,19 @@
     sigma = jax.nn.sigmoid(ext[...])
     mask = used * sigma
     high, low = split(overlapped(s, mask))
-    for here in (slice(0, s.depth), slice(s.depth, 2 * s.depth)):
+    for first_row in (0, s.depth):
+        here = slice(first_row, first_row + s.mask_pad)
         masks[here, : s.width] = high
         masks[here, s.width :] = low
+        if s.mask_pad < s.depth:
+            masks[first_row + s.mask_pad : first_row + s.depth, :] = jnp.zeros(
+                (s.depth - s.mask_pad, 2 * s.width), BF16
+            )
     slope = (mask * (1.0 - sigma))[s.base : s.base + s.grad_pad]
     slope = pltpu.roll(slope, s.width - s.base, 1)
 
     total[...] = jnp.zeros_like(total)
-    group = 4
+    group = 2
     tall = group * s.field_pad
     late = iota((s.field_pad, 128), 1) >= 128 - s.reach
 
@@ -328,8 +342,9 @@
         both = dot(ends, jnp.concatenate([last, last], 0))
         tail = both[:, :128] + both[:, 128:]
         high, low = high[:, : s.main], low[:, : s.main]
-        stack = jnp.concatenate([main[0], main[0], main[1]], 0)
-        head = dot(jnp.concatenate([high, low, high], 1), stack)
+        rows = high.shape[0]
+        both = dot(jnp.concatenate([high, low], 0), main[0])
+        head = both[:rows] + both[rows:] + dot(high, main[1])
         seam = head[:, s.main - 128 :] + jnp.where(late, tail, 0.0)
         pieces = [seam, tail]
         if s.main > 128:
@@ -338,9 +353,10 @@
 
     for g in range(s.filters // group):
         band = row_band[g * tall : (g + 1) * tall, :]
-        one = dot(band, masks[:, : s.width + 128])
-        two = dot(band[:, : s.depth], masks[: s.depth, s.width + 128 :])
-        rowed = one[:, : s.width] + jnp.concatenate([one[:, s.width :], two], 1)
+        top, bottom = band[:, : s.depth], band[:, s.depth :]
+        one = dot(top, masks[: s.depth, :])
+        two = dot(bottom, masks[: s.depth, : s.width])
+        rowed = one[:, : s.width] + one[:, s.width :] + two
         for i in range(0, group, 2):
             squares = 0.0
             for j in (i, i + 1):
@@ -397,9 +413,14 @@
 
 def feature_kernel(s, table, shifted, out, blocks, sems):
     copies = []
+    wide = jnp.concatenate([table[...]] * 3, 1)
+    blank = jnp.zeros((WIN, s.cols), BF16)
     for k in range(s.steps):
-        window = jnp.concatenate([shifted[q, k * ROWS : k * ROWS + WIN, :] for q in range(9)], 0)
-        value = dot(table[...], window)
+        rows = slice(k * ROWS, k * ROWS + WIN)
+        parts = []
+        for part in range(3):
+            parts += [shifted[3 * part + b, rows, :] for b in range(3)] + [blank]
+        value = dot(wide, jnp.concatenate(parts, 0))
         here = pl.ds(k * ROWS, ROWS)
         blocks[:, here, :] = value.astype(BF16).reshape(s.channels, ROWS, s.cols)
         copies.append(pltpu.make_async_copy(blocks.at[:, here, :], out.at[:, here, :], sems.at[k]))
@@ -456,7 +477,7 @@
     table, partial, first, second, features_here, target_here, row_here, col_here, weights, own = call(
         edge_kernel,
         (
-            shape((channels * ROWS, 9 * WIN), BF16),
+            shape((channels * ROWS, 128), BF16),
             shape((s.grad_pad, s.width), F32),
             half_strip,
             half_strip,
@@ -522,7 +543,7 @@
         (shape((9, s.grad_pad, s.cols), BF16), shape((16, channels), F32)),
         [spec()] * 14,
         [
-            pltpu.VMEM((s.depth, s.width), F32),
+            pltpu.VMEM((s.mask_pad, s.width), F32),
             pltpu.VMEM((s.field_pad, s.width), F32),
             pltpu.VMEM((2 * s.depth, 2 * s.width), BF16),
             pltpu.VMEM((filters, s.field_pad, s.width), F32),

time: 37.9 us -> 37.3 us (0.984)
  Pallas kernels: 19.7 us -> 19.1 us
    pallas_call x1, Pallas kernels: 9.44 us -> 9.02 us  [on_device(): call(optics_kernel, (shape((9, s.grad_pad, s.cols), BF16), shape((16, cha...]
where the time goes in v3:
time: 37.3 us; the launch traced here: 37.1 us
  Pallas kernels  19.1 us (51%)
  starting transfers between devices  12.6 us (34%)
  waiting for transfers between devices  4.09 us (11%)
  between operations  0.71 us (2%)
  local copies, waits for them, and re-layouts  0.6 us (2%)
    pallas_call x1, Pallas kernels, on_device(): call(optics_kernel, (shape((9, s.grad_pad, s.cols), BF16), shape((16, cha...  9.02 us
    ppermute x6, starting transfers between devices, summed(): lax.ppermute(value, axis, [(i, i ^ step) for i in range(size)])  6.33 us
    ppermute x6, waiting for transfers between devices, summed(): lax.ppermute(value, axis, [(i, i ^ step) for i in range(size)])  3.35 us
    ppermute x2, starting transfers between devices, exchanged(): one = lax.ppermute(first, axis, [(i, i ^ 1) for i in range(size)])  3.16 us
    ppermute x2, starting transfers between devices, exchanged(): return (one, lax.ppermute(second, ('grp', axis), pairs))  3.1 us
    pallas_call x1, Pallas kernels, on_device(): call(edge_kernel, (shape((channels * ROWS, 128), BF16), shape((s.grad_pad...  2.84 us
    pallas_call x1, Pallas kernels, on_device(): call(row_band_kernel, (shape((filters * s.field_pad, 2 * s.depth), BF16),...  2.81 us
    pallas_call x1, Pallas kernels, on_device(): call(feature_kernel, shape(features.shape, BF16), [spec(), spec()], [pltp...  2.18 us
  transfers between devices with their start and end apart: 10, of which 5 were waited for; matrix products, arithmetic and copies ran while one was open for 0% of the time, Pallas kernels for 18%

profile of v3, /device:TPU:0, one launch (start us, length us, event | category | flops | bytes accessed | tf_op | source)
XLA Modules:
  0.0 37.1 jit_solution(12134121356943757357)
XLA Ops:
  0.6 2.8 %shard_map.86 = (bf16[512,128]{1,0:T(8,128)(2,1)S(1)}, f32[144,384]{1,0:T(8,128)S(1)}, f32[72,128]{1,0:T(8,128)S(1)}, f32[72,128]{1,0:T(8,128)S(1)}, bf16[32,128...) custom-call(s32[1,1,8]{2,1,0:T(1,128)} %listed_hbm.1, ...), custom_call_target="tpu_custom_call" | custom-call | tf_op jit(solution)/shard_map/pallas_call | solution.py:477
  3.5 3.1 %collective-permute-start = (f32[72,128]{1,0:T(8,128)S(1)}, f32[72,128]{1,0:T(8,128)S(1)}, u32[]{:S(2)}, u32[]{:S(2)}) collective-permute-start(f32[72,128]{1,0:T(8,128)S(1)} %get-tuple-element.30), channel_id=1, source_target_pairs={{0,1},{1,0},{2,3},{3,2},{4,5},{5,4},{6,7},{7,6},{8,9},{9,8},{10,11... | collective-permute-start | bytes 110600 | tf_op jit(solution)/shard_map/ppermute | solution.py:438
  6.6 1.5 %collective-permute-start.1 = (f32[72,128]{1,0:T(8,128)S(1)}, f32[72,128]{1,0:T(8,128)S(1)}, u32[]{:S(2)}, u32[]{:S(2)}) collective-permute-start(f32[72,128]{1,0:T(8,128)S(1)} %get-tuple-element.31), channel_id=1, source_target_pairs={{0,16},{1,2},{2,1},{3,19},{16,0},{17,18},{18,17},{19,3},{4,20},{5,... | collective-permute-start | bytes 110600 | tf_op jit(solution)/shard_map/ppermute | solution.py:449
  8.1 1.8 %shard_map.87 = (bf16[16,2,256,256]{3,2,1,0:T(8,128)(2,1)S(1)}, bf16[16,128,256]{2,1,0:T(8,128)(2,1)S(1)}, bf16[16,2,256,256]{3,2,1,0:T(8,128)(2,1)S(1)}, bf16[16,128,256]{2,1,0:T(8,128)(2,1)S(1)}) custom-call(f32[8,2,33]{2,1,0:T(2,128)S(1)} %get-tuple-element.32.col_taps), custom_call_target="tpu_custom_call" | custom-call | tf_op jit(solution)/shard_map/pallas_call | solution.py:511
  9.9 0.0 collective-permute-done.first
  9.9 0.6 %collective-permute-done.1.second = f32[72,128]{1,0:T(8,128)S(1)} collective-permute-done((f32[72,128]{1,0:T(8,128)S(1)}, f32[72,128]{1,0:T(8,128)S(1)}, u32[]{:S(2)}, u32[]{:S(2)}) %collective-permute-start.1) | collective-permute-done | bytes 36896 | tf_op jit(solution)/shard_map/ppermute | solution.py:449
  10.5 0.4 %shard_map.88 = (f32[144,384]{1,0:T(8,128)S(1)}, f32[128,384]{1,0:T(8,128)S(1)}, f32[8,384]{1,0:T(8,128)S(1)}, f32[56,384]{1,0:T(8,128)S(1)}, f32[56,384]{1,0:T(8,128)S(1)}) custom-call(f32[8,384]{1,0:T(8,128)S(1)} %get-tuple-element.27.own_used, f32[144,384]{1,0:T(8,128)S(1)} %get-tuple-element.28.partial, f32[128,256]{1,0:T(8,128)S(1)} %get-tuple-element.29.target, ...), custom_call_target="tpu_custom_call" | custom-call | tf_op jit(solution)/shard_map/pallas_call | solution.py:528
  10.9 0.1 collective-permute-start.2
  11.0 1.6 %collective-permute-start.3 = (f32[56,384]{1,0:T(8,128)S(1)}, f32[56,384]{1,0:T(8,128)S(1)}, u32[]{:S(2)}, u32[]{:S(2)}) collective-permute-start(f32[56,384]{1,0:T(8,128)S(1)} %get-tuple-element.38), channel_id=1, source_target_pairs={{0,16},{4,8},{8,4},{12,28},{16,0},{20,24},{24,20},{28,12},{1,17},{... | collective-permute-start | bytes 258056 | tf_op jit(solution)/shard_map/ppermute | solution.py:449
  12.6 2.8 %shard_map.89 = (bf16[2816,512]{1,0:T(8,128)(2,1)S(1)}, bf16[144,2816]{1,0:T(8,128)(2,1)S(1)}, bf16[144,2816]{1,0:T(8,128)(2,1)S(1)}) custom-call(f32[8,2,33]{2,1,0:T(2,128)S(1)} %get-tuple-element.39.row_taps, f32[8,128]{1,0:T(8,128)S(1)} %get-tuple-element.26.weights), custom_call_target="tpu_custom_call" | custom-call | tf_op jit(solution)/shard_map/pallas_call | solution.py:516
  15.4 0.1 collective-permute-done.3.second
  15.6 9.0 %shard_map.90 = (bf16[9,144,256]{2,1,0:T(8,128)(2,1)S(1)}, f32[16,32]{1,0:T(8,128)S(1)}) custom-call(f32[8,128]{1,0:T(8,128)S(1)} %get-tuple-element.26.weights, f32[144,384]{1,0:T(8,128)S(1)} %get-tuple-element.34.logits, f32[128,384]{1,0:T(8,128)S(1)} %get-tuple-element.35.aim, f32[8,384]{1,0:T(8,128)S(1)} %get-tuple-element.36.occupied, ...), custom_call_target="tpu_custom_call" | custom-call | tf_op jit(solution)/shard_map/pallas_call | solution.py:541
  24.6 1.1 %collective-permute-start.6 = (f32[16,32]{1,0:T(8,128)S(1)}, f32[16,32]{1,0:T(8,128)S(1)}, u32[]{:S(2)}, u32[]{:S(2)}) collective-permute-start(f32[16,32]{1,0:T(8,128)S(1)} %get-tuple-element.47), channel_id=1, source_target_pairs={{0,12},{4,8},{8,4},{12,0},{1,13},{5,9},{9,5},{13,1},{2,14},{6,10},... | collective-permute-start | bytes 6152 | tf_op jit(solution)/shard_map/ppermute | solution.py:455
  25.7 0.7 %collective-permute-start.5 = (f32[16,32]{1,0:T(8,128)S(1)}, f32[16,32]{1,0:T(8,128)S(1)}, u32[]{:S(2)}, u32[]{:S(2)}) collective-permute-start(f32[16,32]{1,0:T(8,128)S(1)} %get-tuple-element.47), channel_id=1, source_target_pairs={{0,8},{4,12},{8,0},{12,4},{1,9},{5,13},{9,1},{13,5},{2,10},{6,14},... | collective-permute-start | bytes 6152 | tf_op jit(solution)/shard_map/ppermute | solution.py:455
  26.4 0.1 collective-permute-start.4
  26.5 1.2 %collective-permute-done.6 = f32[16,32]{1,0:T(8,128)S(1)} collective-permute-done((f32[16,32]{1,0:T(8,128)S(1)}, f32[16,32]{1,0:T(8,128)S(1)}, u32[]{:S(2)}, u32[]{:S(2)}) %collective-permute-start.6) | collective-permute-done | bytes 2080 | tf_op jit(solution)/shard_map/ppermute | solution.py:455
  27.7 1.7 %collective-permute-done.5 = f32[16,32]{1,0:T(8,128)S(1)} collective-permute-done((f32[16,32]{1,0:T(8,128)S(1)}, f32[16,32]{1,0:T(8,128)S(1)}, u32[]{:S(2)}, u32[]{:S(2)}) %collective-permute-start.5) | collective-permute-done | bytes 2080 | tf_op jit(solution)/shard_map/ppermute | solution.py:455
  29.4 0.0 collective-permute-done.4
  29.4 2.5 %collective-permute-start.9 = (f32[16,32]{1,0:T(8,128)S(1)}, f32[16,32]{1,0:T(8,128)S(1)}, u32[]{:S(2)}, u32[]{:S(2)}) collective-permute-start(f32[16,32]{1,0:T(8,128)S(1)} %add_add_fusion), channel_id=1, source_target_pairs={{0,3},{1,2},{2,1},{3,0},{4,7},{5,6},{6,5},{7,4},{8,11},{9,10},{10,... | collective-permute-start | bytes 6152 | tf_op jit(solution)/shard_map/ppermute | solution.py:455
  31.9 0.2 collective-permute-start.8
  32.1 1.7 %collective-permute-start.7 = (f32[16,32]{1,0:T(8,128)S(1)}, f32[16,32]{1,0:T(8,128)S(1)}, u32[]{:S(2)}, u32[]{:S(2)}) collective-permute-start(f32[16,32]{1,0:T(8,128)S(1)} %add_add_fusion), channel_id=1, source_target_pairs={{0,1},{1,0},{2,3},{3,2},{4,5},{5,4},{6,7},{7,6},{8,9},{9,8},{10,11... | collective-permute-start | bytes 6152 | tf_op jit(solution)/shard_map/ppermute | solution.py:455
  33.8 2.2 %shard_map.91 = bf16[32,128,256]{2,1,0:T(8,128)(2,1)} custom-call(bf16[512,128]{1,0:T(8,128)(2,1)S(1)} %get-tuple-element.48.table, bf16[9,144,256]{2,1,0:T(8,128)(2,1)S(1)} %get-tuple-element.49.shifted), custom_call_target="tpu_custom_call" | custom-call | tf_op jit(solution)/shard_map/pallas_call | solution.py:557
  36.0 0.4 %collective-permute-done.8 = f32[16,32]{1,0:T(8,128)S(1)} collective-permute-done((f32[16,32]{1,0:T(8,128)S(1)}, f32[16,32]{1,0:T(8,128)S(1)}, u32[]{:S(2)}, u32[]{:S(2)}) %collective-permute-start.8) | collective-permute-done | bytes 2080 | tf_op jit(solution)/shard_map/ppermute | solution.py:455
  36.5 0.6 %reshape.7 = f32[32,3,3]{0,2,1:T(4,128)} reshape(f32[32,9]{0,1:T(8,128)S(1)} %fusion.1) | data formatting | bytes 2304 | tf_op jit(solution)/shard_map/reshape | solution.py:567
  (5 shorter events, 0.0 us)
Async XLA Ops:
  3.5 6.5 %collective-permute-start = (f32[72,128]{1,0:T(8,128)S(1)}, f32[72,128]{1,0:T(8,128)S(1)}, u32[]{:S(2)}, u32[]{:S(2)}) collective-permute-start(f32[72,128]{1,0:T(8,128)S(1)} %get-tuple-element.30), channel_id=1, source_target_pairs={{0,1},{1,0},{2,3},{3,2},{4,5},{5,4},{6,7},{7,6},{8,9},{9,8},{10,11... | collective-permute-start | bytes 110600 | tf_op jit(solution)/shard_map/ppermute | solution.py:438
  6.6 4.0 %collective-permute-start.1 = (f32[72,128]{1,0:T(8,128)S(1)}, f32[72,128]{1,0:T(8,128)S(1)}, u32[]{:S(2)}, u32[]{:S(2)}) collective-permute-start(f32[72,128]{1,0:T(8,128)S(1)} %get-tuple-element.31), channel_id=1, source_target_pairs={{0,16},{1,2},{2,1},{3,19},{16,0},{17,18},{18,17},{19,3},{4,20},{5,... | collective-permute-start | bytes 110600 | tf_op jit(solution)/shard_map/ppermute | solution.py:449
  10.9 4.5 %collective-permute-start.2 = (f32[56,384]{1,0:T(8,128)S(1)}, f32[56,384]{1,0:T(8,128)S(1)}, u32[]{:S(2)}, u32[]{:S(2)}) collective-permute-start(f32[56,384]{1,0:T(8,128)S(1)} %get-tuple-element.37), channel_id=1, source_target_pairs={{0,4},{4,0},{8,12},{12,8},{1,5},{5,1},{9,13},{13,9},{2,6},{6,2},{1... | collective-permute-start | bytes 258056 | tf_op jit(solution)/shard_map/ppermute | solution.py:438
  11.0 4.6 %collective-permute-start.3 = (f32[56,384]{1,0:T(8,128)S(1)}, f32[56,384]{1,0:T(8,128)S(1)}, u32[]{:S(2)}, u32[]{:S(2)}) collective-permute-start(f32[56,384]{1,0:T(8,128)S(1)} %get-tuple-element.38), channel_id=1, source_target_pairs={{0,16},{4,8},{8,4},{12,28},{16,0},{20,24},{24,20},{28,12},{1,17},{... | collective-permute-start | bytes 258056 | tf_op jit(solution)/shard_map/ppermute | solution.py:449
  24.6 3.1 %collective-permute-start.6 = (f32[16,32]{1,0:T(8,128)S(1)}, f32[16,32]{1,0:T(8,128)S(1)}, u32[]{:S(2)}, u32[]{:S(2)}) collective-permute-start(f32[16,32]{1,0:T(8,128)S(1)} %get-tuple-element.47), channel_id=1, source_target_pairs={{0,12},{4,8},{8,4},{12,0},{1,13},{5,9},{9,5},{13,1},{2,14},{6,10},... | collective-permute-start | bytes 6152 | tf_op jit(solution)/shard_map/ppermute | solution.py:455
  25.7 3.7 %collective-permute-start.5 = (f32[16,32]{1,0:T(8,128)S(1)}, f32[16,32]{1,0:T(8,128)S(1)}, u32[]{:S(2)}, u32[]{:S(2)}) collective-permute-start(f32[16,32]{1,0:T(8,128)S(1)} %get-tuple-element.47), channel_id=1, source_target_pairs={{0,8},{4,12},{8,0},{12,4},{1,9},{5,13},{9,1},{13,5},{2,10},{6,14},... | collective-permute-start | bytes 6152 | tf_op jit(solution)/shard_map/ppermute | solution.py:455
  26.4 3.0 %collective-permute-start.4 = (f32[16,32]{1,0:T(8,128)S(1)}, f32[16,32]{1,0:T(8,128)S(1)}, u32[]{:S(2)}, u32[]{:S(2)}) collective-permute-start(f32[16,32]{1,0:T(8,128)S(1)} %get-tuple-element.47), channel_id=1, source_target_pairs={{0,4},{4,0},{8,12},{12,8},{1,5},{5,1},{9,13},{13,9},{2,6},{6,2},{1... | collective-permute-start | bytes 6152 | tf_op jit(solution)/shard_map/ppermute | solution.py:455
  29.4 6.6 %collective-permute-start.9 = (f32[16,32]{1,0:T(8,128)S(1)}, f32[16,32]{1,0:T(8,128)S(1)}, u32[]{:S(2)}, u32[]{:S(2)}) collective-permute-start(f32[16,32]{1,0:T(8,128)S(1)} %add_add_fusion), channel_id=1, source_target_pairs={{0,3},{1,2},{2,1},{3,0},{4,7},{5,6},{6,5},{7,4},{8,11},{9,10},{10,... | collective-permute-start | bytes 6152 | tf_op jit(solution)/shard_map/ppermute | solution.py:455
  31.9 4.5 %collective-permute-start.8 = (f32[16,32]{1,0:T(8,128)S(1)}, f32[16,32]{1,0:T(8,128)S(1)}, u32[]{:S(2)}, u32[]{:S(2)}) collective-permute-start(f32[16,32]{1,0:T(8,128)S(1)} %add_add_fusion), channel_id=1, source_target_pairs={{0,2},{1,3},{2,0},{3,1},{4,6},{5,7},{6,4},{7,5},{8,10},{9,11},{10,... | collective-permute-start | bytes 6152 | tf_op jit(solution)/shard_map/ppermute | solution.py:455
  32.1 4.4 %collective-permute-start.7 = (f32[16,32]{1,0:T(8,128)S(1)}, f32[16,32]{1,0:T(8,128)S(1)}, u32[]{:S(2)}, u32[]{:S(2)}) collective-permute-start(f32[16,32]{1,0:T(8,128)S(1)} %add_add_fusion), channel_id=1, source_target_pairs={{0,1},{1,0},{2,3},{3,2},{4,5},{5,4},{6,7},{7,6},{8,9},{9,8},{10,11... | collective-permute-start | bytes 6152 | tf_op jit(solution)/shard_map/ppermute | solution.py:455

commit v4 on v3

--- a/solution.py
+++ b/solution.py
@@ -134,8 +134,8 @@
 
 def edge_kernel(
     s, listed_hbm, features_hbm, conv_weight_hbm, target_hbm, row_taps_hbm, col_taps_hbm, weights_hbm,
-    table, partial, first_out, second_out, features, target, row_taps, col_taps, weights_out, own,
-    acc, listed, conv_weight, weights, sems,
+    table, acc, first_out, second_out, features, target, row_taps, col_taps, weights_out, own,
+    listed, conv_weight, weights, sems,
 ):
     fetch = [
         pltpu.make_async_copy(conv_weight_hbm, conv_weight, sems.at[0]),
@@ -190,21 +190,21 @@
     for n in range(listed.shape[2]):
         used = jnp.where(number == listed[0, 0, n], 1.0, used)
     own[...] = used
-    whole = jnp.zeros((s.grad_pad, s.width), F32)
-    blank = jnp.zeros((s.grad_pad, s.width - s.cols), F32)
-    for b in range(3):
-        part = jnp.concatenate([acc[b, : s.grad_pad], blank], 1)
-        whole += pltpu.roll(part, s.base + 2 - b, 1)
-    partial[...] = whole
-
     place, row = iota((s.grad_pad, 128), 1), iota((s.grad_pad, 128), 0)
     filler = jnp.zeros((s.grad_pad - s.rows, 128), F32)
     strips = []
-    for first, first_aim, block_col in (
-        (s.base, 0, 0),
-        (s.cols, s.cols - s.field_halo, across - 1),
-    ):
-        logits, wanted = pulled_tile(whole, first, 0), pulled_tile(target[...], first_aim, s.strip)
+    for first_aim, block_col in ((0, 0), (s.cols - s.field_halo, across - 1)):
+        logits = jnp.zeros((s.grad_pad, 128), F32)
+        for b in range(3):
+            if block_col == 0:
+                part = acc[b, : s.grad_pad, :128]
+                shift, kept = 2 - b, place >= 2 - b
+            else:
+                part = acc[b, : s.grad_pad, s.cols - 128 :]
+                shift, kept = s.strip - b, place < s.strip - b
+            part = pltpu.roll(part, shift, 1) if shift else part
+            logits += jnp.where(kept, part, 0.0)
+        wanted = pulled_tile(target[...], first_aim, s.strip)
         wanted = jnp.concatenate([wanted, filler], 0)
         number = (row // BLOCK) * across + block_col
         used = jnp.zeros((s.grad_pad, 128), F32)
@@ -220,6 +220,15 @@
     odd = neighbours("col")[2]
     first_out[...] = jnp.where(odd, strips[0], strips[1])
     second_out[...] = jnp.where(odd, strips[1], strips[0])
+
+
+def partial_kernel(s, acc, partial):
+    whole = jnp.zeros((s.grad_pad, s.width), F32)
+    blank = jnp.zeros((s.grad_pad, s.width - s.cols), F32)
+    for b in range(3):
+        part = jnp.concatenate([acc[b, : s.grad_pad], blank], 1)
+        whole += pltpu.roll(part, s.base + 2 - b, 1)
+    partial[...] = whole
 
 
 def unfolded(s, value):
@@ -474,11 +483,11 @@
         )
 
     half_strip = shape((s.fold, 128), F32)
-    table, partial, first, second, features_here, target_here, row_here, col_here, weights, own = call(
+    table, sums, first, second, features_here, target_here, row_here, col_here, weights, own = call(
         edge_kernel,
         (
             shape((channels * ROWS, 128), BF16),
-            shape((s.grad_pad, s.width), F32),
+            shape((3, s.rows + WIN, s.cols), F32),
             half_strip,
             half_strip,
             shape(features.shape, BF16),
@@ -490,7 +499,6 @@
         ),
         [hbm] * 7,
         [
-            pltpu.VMEM((3, s.rows + WIN, s.cols), F32),
             pltpu.SMEM(block_list.shape, jnp.int32),
             pltpu.VMEM((3, 3, channels), BF16),
             pltpu.SMEM(kernel_weight.shape, F32),
@@ -506,6 +514,7 @@
         )
     )
     first, second = exchanged(first, second, "col")
+    partial = call(partial_kernel, shape((s.grad_pad, s.width), F32), [spec()])(sums)
 
     filters = s.filters
     col_bands = call(

time: 37.3 us -> 37.2 us (level)
    pallas_call x1 -> x2, Pallas kernels: 2.84 us -> 3 us  [the longest x1 2.81 us: on_device(): call(edge_kernel, (shape((channels * ROWS, 128), BF16), shape((3, s.rows...]
  transfers between devices with their start and end apart: 10 -> 10, of which waited for: 5 -> 5; matrix products, arithmetic and copies ran while one was open for 0% -> 0% of each run, Pallas kernels for 18% -> 19%
where the time goes in v4:
time: 37.2 us; the launch traced here: 37.1 us
  Pallas kernels  19.2 us (52%)
  starting transfers between devices  12.6 us (34%)
  waiting for transfers between devices  3.87 us (10%)
  between operations  0.72 us (2%)
  local copies, waits for them, and re-layouts  0.6 us (2%)
    pallas_call x1, Pallas kernels, on_device(): call(optics_kernel, (shape((9, s.grad_pad, s.cols), BF16), shape((16, cha...  9.02 us
    ppermute x6, starting transfers between devices, summed(): lax.ppermute(value, axis, [(i, i ^ step) for i in range(size)])  6.33 us
    ppermute x6, waiting for transfers between devices, summed(): lax.ppermute(value, axis, [(i, i ^ step) for i in range(size)])  3.35 us
    ppermute x2, starting transfers between devices, exchanged(): one = lax.ppermute(first, axis, [(i, i ^ 1) for i in range(size)])  3.16 us
    ppermute x2, starting transfers between devices, exchanged(): return (one, lax.ppermute(second, ('grp', axis), pairs))  3.11 us
    pallas_call x1, Pallas kernels, on_device(): call(edge_kernel, (shape((channels * ROWS, 128), BF16), shape((3, s.rows...  2.81 us
    pallas_call x1, Pallas kernels, on_device(): call(row_band_kernel, (shape((filters * s.field_pad, 2 * s.depth), BF16),...  2.81 us
    pallas_call x1, Pallas kernels, on_device(): call(feature_kernel, shape(features.shape, BF16), [spec(), spec()], [pltp...  2.18 us
  transfers between devices with their start and end apart: 10, of which 5 were waited for; matrix products, arithmetic and copies ran while one was open for 0% of the time, Pallas kernels for 19%

profile of v4, /device:TPU:0, one launch (start us, length us, event | category | flops | bytes accessed | tf_op | source)
XLA Modules:
  0.0 37.1 jit_solution(16136897203731532971)
XLA Ops:
  0.6 2.8 %shard_map.86 = (bf16[512,128]{1,0:T(8,128)(2,1)S(1)}, f32[3,160,256]{2,1,0:T(8,128)S(1)}, f32[72,128]{1,0:T(8,128)S(1)}, f32[72,128]{1,0:T(8,128)S(1)}, bf16[32...) custom-call(s32[1,1,8]{2,1,0:T(1,128)} %listed_hbm.1, ...), custom_call_target="tpu_custom_call" | custom-call | tf_op jit(solution)/shard_map/pallas_call | solution.py:486
  3.4 3.1 %collective-permute-start = (f32[72,128]{1,0:T(8,128)S(1)}, f32[72,128]{1,0:T(8,128)S(1)}, u32[]{:S(2)}, u32[]{:S(2)}) collective-permute-start(f32[72,128]{1,0:T(8,128)S(1)} %get-tuple-element.30), channel_id=1, source_target_pairs={{0,1},{1,0},{2,3},{3,2},{4,5},{5,4},{6,7},{7,6},{8,9},{9,8},{10,11... | collective-permute-start | bytes 110600 | tf_op jit(solution)/shard_map/ppermute | solution.py:447
  6.5 1.5 %collective-permute-start.1 = (f32[72,128]{1,0:T(8,128)S(1)}, f32[72,128]{1,0:T(8,128)S(1)}, u32[]{:S(2)}, u32[]{:S(2)}) collective-permute-start(f32[72,128]{1,0:T(8,128)S(1)} %get-tuple-element.31), channel_id=1, source_target_pairs={{0,16},{1,2},{2,1},{3,19},{16,0},{17,18},{18,17},{19,3},{4,20},{5,... | collective-permute-start | bytes 110600 | tf_op jit(solution)/shard_map/ppermute | solution.py:458
  8.1 0.2 shard_map.87.partial
  8.3 1.8 %shard_map.88 = (bf16[16,2,256,256]{3,2,1,0:T(8,128)(2,1)S(1)}, bf16[16,128,256]{2,1,0:T(8,128)(2,1)S(1)}, bf16[16,2,256,256]{3,2,1,0:T(8,128)(2,1)S(1)}, bf16[16,128,256]{2,1,0:T(8,128)(2,1)S(1)}) custom-call(f32[8,2,33]{2,1,0:T(2,128)S(1)} %get-tuple-element.32.col_taps), custom_call_target="tpu_custom_call" | custom-call | tf_op jit(solution)/shard_map/pallas_call | solution.py:520
  10.1 0.4 %collective-permute-done.1.second = f32[72,128]{1,0:T(8,128)S(1)} collective-permute-done((f32[72,128]{1,0:T(8,128)S(1)}, f32[72,128]{1,0:T(8,128)S(1)}, u32[]{:S(2)}, u32[]{:S(2)}) %collective-permute-start.1) | collective-permute-done | bytes 36896 | tf_op jit(solution)/shard_map/ppermute | solution.py:458
  10.5 0.4 %shard_map.89 = (f32[144,384]{1,0:T(8,128)S(1)}, f32[128,384]{1,0:T(8,128)S(1)}, f32[8,384]{1,0:T(8,128)S(1)}, f32[56,384]{1,0:T(8,128)S(1)}, f32[56,384]{1,0:T(8,128)S(1)}) custom-call(f32[8,384]{1,0:T(8,128)S(1)} %get-tuple-element.27.own_used, f32[144,384]{1,0:T(8,128)S(1)} %shard_map.87.partial, f32[128,256]{1,0:T(8,128)S(1)} %get-tuple-element.29.target, ...), custom_call_target="tpu_custom_call" | custom-call | tf_op jit(solution)/shard_map/pallas_call | solution.py:537
  10.9 0.1 collective-permute-start.2
  11.0 1.6 %collective-permute-start.3 = (f32[56,384]{1,0:T(8,128)S(1)}, f32[56,384]{1,0:T(8,128)S(1)}, u32[]{:S(2)}, u32[]{:S(2)}) collective-permute-start(f32[56,384]{1,0:T(8,128)S(1)} %get-tuple-element.38), channel_id=1, source_target_pairs={{0,16},{4,8},{8,4},{12,28},{16,0},{20,24},{24,20},{28,12},{1,17},{... | collective-permute-start | bytes 258056 | tf_op jit(solution)/shard_map/ppermute | solution.py:458
  12.6 2.8 %shard_map.90 = (bf16[2816,512]{1,0:T(8,128)(2,1)S(1)}, bf16[144,2816]{1,0:T(8,128)(2,1)S(1)}, bf16[144,2816]{1,0:T(8,128)(2,1)S(1)}) custom-call(f32[8,2,33]{2,1,0:T(2,128)S(1)} %get-tuple-element.39.row_taps, f32[8,128]{1,0:T(8,128)S(1)} %get-tuple-element.26.weights), custom_call_target="tpu_custom_call" | custom-call | tf_op jit(solution)/shard_map/pallas_call | solution.py:525
  15.4 0.1 collective-permute-done.3.second
  15.5 9.0 %shard_map.91 = (bf16[9,144,256]{2,1,0:T(8,128)(2,1)S(1)}, f32[16,32]{1,0:T(8,128)S(1)}) custom-call(f32[8,128]{1,0:T(8,128)S(1)} %get-tuple-element.26.weights, f32[144,384]{1,0:T(8,128)S(1)} %get-tuple-element.34.logits, f32[128,384]{1,0:T(8,128)S(1)} %get-tuple-element.35.aim, f32[8,384]{1,0:T(8,128)S(1)} %get-tuple-element.36.occupied, ...), custom_call_target="tpu_custom_call" | custom-call | tf_op jit(solution)/shard_map/pallas_call | solution.py:550
  24.5 1.1 %collective-permute-start.6 = (f32[16,32]{1,0:T(8,128)S(1)}, f32[16,32]{1,0:T(8,128)S(1)}, u32[]{:S(2)}, u32[]{:S(2)}) collective-permute-start(f32[16,32]{1,0:T(8,128)S(1)} %get-tuple-element.47), channel_id=1, source_target_pairs={{0,12},{4,8},{8,4},{12,0},{1,13},{5,9},{9,5},{13,1},{2,14},{6,10},... | collective-permute-start | bytes 6152 | tf_op jit(solution)/shard_map/ppermute | solution.py:464
  25.7 0.7 %collective-permute-start.5 = (f32[16,32]{1,0:T(8,128)S(1)}, f32[16,32]{1,0:T(8,128)S(1)}, u32[]{:S(2)}, u32[]{:S(2)}) collective-permute-start(f32[16,32]{1,0:T(8,128)S(1)} %get-tuple-element.47), channel_id=1, source_target_pairs={{0,8},{4,12},{8,0},{12,4},{1,9},{5,13},{9,1},{13,5},{2,10},{6,14},... | collective-permute-start | bytes 6152 | tf_op jit(solution)/shard_map/ppermute | solution.py:464
  26.3 0.1 collective-permute-start.4
  26.4 1.2 %collective-permute-done.6 = f32[16,32]{1,0:T(8,128)S(1)} collective-permute-done((f32[16,32]{1,0:T(8,128)S(1)}, f32[16,32]{1,0:T(8,128)S(1)}, u32[]{:S(2)}, u32[]{:S(2)}) %collective-permute-start.6) | collective-permute-done | bytes 2080 | tf_op jit(solution)/shard_map/ppermute | solution.py:464
  27.6 1.7 %collective-permute-done.5 = f32[16,32]{1,0:T(8,128)S(1)} collective-permute-done((f32[16,32]{1,0:T(8,128)S(1)}, f32[16,32]{1,0:T(8,128)S(1)}, u32[]{:S(2)}, u32[]{:S(2)}) %collective-permute-start.5) | collective-permute-done | bytes 2080 | tf_op jit(solution)/shard_map/ppermute | solution.py:464
  29.3 0.0 collective-permute-done.4
  29.3 2.5 %collective-permute-start.9 = (f32[16,32]{1,0:T(8,128)S(1)}, f32[16,32]{1,0:T(8,128)S(1)}, u32[]{:S(2)}, u32[]{:S(2)}) collective-permute-start(f32[16,32]{1,0:T(8,128)S(1)} %add_add_fusion), channel_id=1, source_target_pairs={{0,3},{1,2},{2,1},{3,0},{4,7},{5,6},{6,5},{7,4},{8,11},{9,10},{10,... | collective-permute-start | bytes 6152 | tf_op jit(solution)/shard_map/ppermute | solution.py:464
  31.9 0.3 collective-permute-start.8
  32.2 1.6 %collective-permute-start.7 = (f32[16,32]{1,0:T(8,128)S(1)}, f32[16,32]{1,0:T(8,128)S(1)}, u32[]{:S(2)}, u32[]{:S(2)}) collective-permute-start(f32[16,32]{1,0:T(8,128)S(1)} %add_add_fusion), channel_id=1, source_target_pairs={{0,1},{1,0},{2,3},{3,2},{4,5},{5,4},{6,7},{7,6},{8,9},{9,8},{10,11... | collective-permute-start | bytes 6152 | tf_op jit(solution)/shard_map/ppermute | solution.py:464
  33.8 2.2 %shard_map.92 = bf16[32,128,256]{2,1,0:T(8,128)(2,1)} custom-call(bf16[512,128]{1,0:T(8,128)(2,1)S(1)} %get-tuple-element.48.table, bf16[9,144,256]{2,1,0:T(8,128)(2,1)S(1)} %get-tuple-element.49.shifted), custom_call_target="tpu_custom_call" | custom-call | tf_op jit(solution)/shard_map/pallas_call | solution.py:566
  36.0 0.4 %collective-permute-done.8 = f32[16,32]{1,0:T(8,128)S(1)} collective-permute-done((f32[16,32]{1,0:T(8,128)S(1)}, f32[16,32]{1,0:T(8,128)S(1)}, u32[]{:S(2)}, u32[]{:S(2)}) %collective-permute-start.8) | collective-permute-done | bytes 2080 | tf_op jit(solution)/shard_map/ppermute | solution.py:464
  36.5 0.6 %reshape.7 = f32[32,3,3]{0,2,1:T(4,128)} reshape(f32[32,9]{0,1:T(8,128)S(1)} %fusion.1) | data formatting | bytes 2304 | tf_op jit(solution)/shard_map/reshape | solution.py:576
  (6 shorter events, 0.0 us)
Async XLA Ops:
  3.4 6.7 %collective-permute-start = (f32[72,128]{1,0:T(8,128)S(1)}, f32[72,128]{1,0:T(8,128)S(1)}, u32[]{:S(2)}, u32[]{:S(2)}) collective-permute-start(f32[72,128]{1,0:T(8,128)S(1)} %get-tuple-element.30), channel_id=1, source_target_pairs={{0,1},{1,0},{2,3},{3,2},{4,5},{5,4},{6,7},{7,6},{8,9},{9,8},{10,11... | collective-permute-start | bytes 110600 | tf_op jit(solution)/shard_map/ppermute | solution.py:447
  6.5 4.0 %collective-permute-start.1 = (f32[72,128]{1,0:T(8,128)S(1)}, f32[72,128]{1,0:T(8,128)S(1)}, u32[]{:S(2)}, u32[]{:S(2)}) collective-permute-start(f32[72,128]{1,0:T(8,128)S(1)} %get-tuple-element.31), channel_id=1, source_target_pairs={{0,16},{1,2},{2,1},{3,19},{16,0},{17,18},{18,17},{19,3},{4,20},{5,... | collective-permute-start | bytes 110600 | tf_op jit(solution)/shard_map/ppermute | solution.py:458
  10.9 4.5 %collective-permute-start.2 = (f32[56,384]{1,0:T(8,128)S(1)}, f32[56,384]{1,0:T(8,128)S(1)}, u32[]{:S(2)}, u32[]{:S(2)}) collective-permute-start(f32[56,384]{1,0:T(8,128)S(1)} %get-tuple-element.37), channel_id=1, source_target_pairs={{0,4},{4,0},{8,12},{12,8},{1,5},{5,1},{9,13},{13,9},{2,6},{6,2},{1... | collective-permute-start | bytes 258056 | tf_op jit(solution)/shard_map/ppermute | solution.py:447
  11.0 4.6 %collective-permute-start.3 = (f32[56,384]{1,0:T(8,128)S(1)}, f32[56,384]{1,0:T(8,128)S(1)}, u32[]{:S(2)}, u32[]{:S(2)}) collective-permute-start(f32[56,384]{1,0:T(8,128)S(1)} %get-tuple-element.38), channel_id=1, source_target_pairs={{0,16},{4,8},{8,4},{12,28},{16,0},{20,24},{24,20},{28,12},{1,17},{... | collective-permute-start | bytes 258056 | tf_op jit(solution)/shard_map/ppermute | solution.py:458
  24.5 3.1 %collective-permute-start.6 = (f32[16,32]{1,0:T(8,128)S(1)}, f32[16,32]{1,0:T(8,128)S(1)}, u32[]{:S(2)}, u32[]{:S(2)}) collective-permute-start(f32[16,32]{1,0:T(8,128)S(1)} %get-tuple-element.47), channel_id=1, source_target_pairs={{0,12},{4,8},{8,4},{12,0},{1,13},{5,9},{9,5},{13,1},{2,14},{6,10},... | collective-permute-start | bytes 6152 | tf_op jit(solution)/shard_map/ppermute | solution.py:464
  25.7 3.7 %collective-permute-start.5 = (f32[16,32]{1,0:T(8,128)S(1)}, f32[16,32]{1,0:T(8,128)S(1)}, u32[]{:S(2)}, u32[]{:S(2)}) collective-permute-start(f32[16,32]{1,0:T(8,128)S(1)} %get-tuple-element.47), channel_id=1, source_target_pairs={{0,8},{4,12},{8,0},{12,4},{1,9},{5,13},{9,1},{13,5},{2,10},{6,14},... | collective-permute-start | bytes 6152 | tf_op jit(solution)/shard_map/ppermute | solution.py:464
  26.3 3.0 %collective-permute-start.4 = (f32[16,32]{1,0:T(8,128)S(1)}, f32[16,32]{1,0:T(8,128)S(1)}, u32[]{:S(2)}, u32[]{:S(2)}) collective-permute-start(f32[16,32]{1,0:T(8,128)S(1)} %get-tuple-element.47), channel_id=1, source_target_pairs={{0,4},{4,0},{8,12},{12,8},{1,5},{5,1},{9,13},{13,9},{2,6},{6,2},{1... | collective-permute-start | bytes 6152 | tf_op jit(solution)/shard_map/ppermute | solution.py:464
  29.3 6.6 %collective-permute-start.9 = (f32[16,32]{1,0:T(8,128)S(1)}, f32[16,32]{1,0:T(8,128)S(1)}, u32[]{:S(2)}, u32[]{:S(2)}) collective-permute-start(f32[16,32]{1,0:T(8,128)S(1)} %add_add_fusion), channel_id=1, source_target_pairs={{0,3},{1,2},{2,1},{3,0},{4,7},{5,6},{6,5},{7,4},{8,11},{9,10},{10,... | collective-permute-start | bytes 6152 | tf_op jit(solution)/shard_map/ppermute | solution.py:464
  31.9 4.5 %collective-permute-start.8 = (f32[16,32]{1,0:T(8,128)S(1)}, f32[16,32]{1,0:T(8,128)S(1)}, u32[]{:S(2)}, u32[]{:S(2)}) collective-permute-start(f32[16,32]{1,0:T(8,128)S(1)} %add_add_fusion), channel_id=1, source_target_pairs={{0,2},{1,3},{2,0},{3,1},{4,6},{5,7},{6,4},{7,5},{8,10},{9,11},{10,... | collective-permute-start | bytes 6152 | tf_op jit(solution)/shard_map/ppermute | solution.py:464
  32.2 4.3 %collective-permute-start.7 = (f32[16,32]{1,0:T(8,128)S(1)}, f32[16,32]{1,0:T(8,128)S(1)}, u32[]{:S(2)}, u32[]{:S(2)}) collective-permute-start(f32[16,32]{1,0:T(8,128)S(1)} %add_add_fusion), channel_id=1, source_target_pairs={{0,1},{1,0},{2,3},{3,2},{4,5},{5,4},{6,7},{7,6},{8,9},{9,8},{10,11... | collective-permute-start | bytes 6152 | tf_op jit(solution)/shard_map/ppermute | solution.py:464

commit v5 on v4

--- a/solution.py
+++ b/solution.py
@@ -300,7 +300,7 @@
 
 def optics_kernel(
     s, weights, logits, aim, occupied, first, second, row_band, fwd_main, fwd_last, adj_main, adj_last, adj_high, adj_low,
-    features, shifted, terms,
+    features, shifted, exact, terms,
     ext, aims, masks, field, pulled, total,
 ):
 
@@ -399,10 +399,8 @@
 
     for b in range(3):
         moved = grad if b == 2 else pltpu.roll(grad, s.width - (2 - b), 1)
-        moved = moved[:, : s.cols]
-        shifted[b], shifted[3 + b] = split(moved)
-        rest = moved - shifted[b].astype(F32) - shifted[3 + b].astype(F32)
-        shifted[6 + b] = rest.astype(BF16)
+        shifted[b], shifted[3 + b] = split(moved[:, : s.cols])
+    exact[...] = grad
     sums = jnp.zeros((s.channels * ROWS, 6 * WIN), F32)
     for k in range(s.steps):
         block = features[:, k * ROWS : (k + 1) * ROWS, :].reshape(s.channels * ROWS, s.cols)
@@ -420,15 +418,19 @@
     terms[...] = result
 
 
-def feature_kernel(s, table, shifted, out, blocks, sems):
+def feature_kernel(s, table, shifted, exact, out, blocks, third, sems):
     copies = []
+    for b in range(3):
+        moved = exact[...] if b == 2 else pltpu.roll(exact[...], s.width - (2 - b), 1)
+        rest = moved[:, : s.cols] - shifted[b].astype(F32) - shifted[3 + b].astype(F32)
+        third[b] = rest.astype(BF16)
     wide = jnp.concatenate([table[...]] * 3, 1)
     blank = jnp.zeros((WIN, s.cols), BF16)
     for k in range(s.steps):
         rows = slice(k * ROWS, k * ROWS + WIN)
         parts = []
         for part in range(3):
-            parts += [shifted[3 * part + b, rows, :] for b in range(3)] + [blank]
+            parts += [(third[b, rows, :] if part == 2 else shifted[3 * part + b, rows, :]) for b in range(3)] + [blank]
         value = dot(wide, jnp.concatenate(parts, 0))
         here = pl.ds(k * ROWS, ROWS)
         blocks[:, here, :] = value.astype(BF16).reshape(s.channels, ROWS, s.cols)
@@ -547,9 +549,9 @@
     )(own, partial, target_here, first, second, col_bands[1])
     first, second = exchanged(first, second, "row")
 
-    shifted, terms = call(
+    shifted, exact, terms = call(
         optics_kernel,
-        (shape((9, s.grad_pad, s.cols), BF16), shape((16, channels), F32)),
+        (shape((6, s.grad_pad, s.cols), BF16), shape((s.grad_pad, s.width), F32), shape((16, channels), F32)),
         [spec()] * 14,
         [
             pltpu.VMEM((s.mask_pad, s.width), F32),
@@ -566,10 +568,14 @@
     grad_features = call(
         feature_kernel,
         shape(features.shape, BF16),
-        [spec(), spec()],
-        [pltpu.VMEM(features.shape, BF16), pltpu.SemaphoreType.DMA((s.steps,))],
+        [spec()] * 3,
+        [
+            pltpu.VMEM(features.shape, BF16),
+            pltpu.VMEM((3, s.grad_pad, s.cols), BF16),
+            pltpu.SemaphoreType.DMA((s.steps,)),
+        ],
         out_space=pltpu.HBM,
-    )(table, shifted)
+    )(table, shifted, exact)
     whole = summed(by_row, "col")
     height = tile_rows * lax.axis_size("row")
     width = tile_cols * lax.axis_size("col")

time: 37.2 us -> 37.2 us (level)
  no operation moved by 1% of the time
where the time goes in v5:
time: 37.2 us; the launch traced here: 37.1 us
  Pallas kernels  19.2 us (52%)
  starting transfers between devices  12.6 us (34%)
  waiting for transfers between devices  3.88 us (10%)
  between operations  0.72 us (2%)
  local copies, waits for them, and re-layouts  0.6 us (2%)
    pallas_call x1, Pallas kernels, on_device(): call(optics_kernel, (shape((6, s.grad_pad, s.cols), BF16), shape((s.grad_...  9.02 us
    ppermute x6, starting transfers between devices, summed(): lax.ppermute(value, axis, [(i, i ^ step) for i in range(size)])  6.33 us
    ppermute x6, waiting for transfers between devices, summed(): lax.ppermute(value, axis, [(i, i ^ step) for i in range(size)])  3.36 us
    ppermute x2, starting transfers between devices, exchanged(): one = lax.ppermute(first, axis, [(i, i ^ 1) for i in range(size)])  3.16 us
    ppermute x2, starting transfers between devices, exchanged(): return (one, lax.ppermute(second, ('grp', axis), pairs))  3.11 us
    pallas_call x1, Pallas kernels, on_device(): call(edge_kernel, (shape((channels * ROWS, 128), BF16), shape((3, s.rows...  2.81 us
    pallas_call x1, Pallas kernels, on_device(): call(row_band_kernel, (shape((filters * s.field_pad, 2 * s.depth), BF16),...  2.81 us
    pallas_call x1, Pallas kernels, on_device(): call(feature_kernel, shape(features.shape, BF16), [spec()] * 3, [pltpu.VM...  2.18 us
  transfers between devices with their start and end apart: 10, of which 5 were waited for; matrix products, arithmetic and copies ran while one was open for 0% of the time, Pallas kernels for 19%

profile of v5, /device:TPU:0, one launch (start us, length us, event | category | flops | bytes accessed | tf_op | source)
XLA Modules:
  0.0 37.1 jit_solution(8508407595509893846)
XLA Ops:
  0.6 2.8 %shard_map.86 = (bf16[512,128]{1,0:T(8,128)(2,1)S(1)}, f32[3,160,256]{2,1,0:T(8,128)S(1)}, f32[72,128]{1,0:T(8,128)S(1)}, f32[72,128]{1,0:T(8,128)S(1)}, bf16[32...) custom-call(s32[1,1,8]{2,1,0:T(1,128)} %listed_hbm.1, ...), custom_call_target="tpu_custom_call" | custom-call | tf_op jit(solution)/shard_map/pallas_call | solution.py:488
  3.4 3.1 %collective-permute-start = (f32[72,128]{1,0:T(8,128)S(1)}, f32[72,128]{1,0:T(8,128)S(1)}, u32[]{:S(2)}, u32[]{:S(2)}) collective-permute-start(f32[72,128]{1,0:T(8,128)S(1)} %get-tuple-element.31), channel_id=1, source_target_pairs={{0,1},{1,0},{2,3},{3,2},{4,5},{5,4},{6,7},{7,6},{8,9},{9,8},{10,11... | collective-permute-start | bytes 110600 | tf_op jit(solution)/shard_map/ppermute | solution.py:449
  6.5 1.5 %collective-permute-start.1 = (f32[72,128]{1,0:T(8,128)S(1)}, f32[72,128]{1,0:T(8,128)S(1)}, u32[]{:S(2)}, u32[]{:S(2)}) collective-permute-start(f32[72,128]{1,0:T(8,128)S(1)} %get-tuple-element.32), channel_id=1, source_target_pairs={{0,16},{1,2},{2,1},{3,19},{16,0},{17,18},{18,17},{19,3},{4,20},{5,... | collective-permute-start | bytes 110600 | tf_op jit(solution)/shard_map/ppermute | solution.py:460
  8.1 0.2 shard_map.87.partial
  8.3 1.8 %shard_map.88 = (bf16[16,2,256,256]{3,2,1,0:T(8,128)(2,1)S(1)}, bf16[16,128,256]{2,1,0:T(8,128)(2,1)S(1)}, bf16[16,2,256,256]{3,2,1,0:T(8,128)(2,1)S(1)}, bf16[16,128,256]{2,1,0:T(8,128)(2,1)S(1)}) custom-call(f32[8,2,33]{2,1,0:T(2,128)S(1)} %get-tuple-element.33.col_taps), custom_call_target="tpu_custom_call" | custom-call | tf_op jit(solution)/shard_map/pallas_call | solution.py:522
  10.1 0.4 %collective-permute-done.1.second = f32[72,128]{1,0:T(8,128)S(1)} collective-permute-done((f32[72,128]{1,0:T(8,128)S(1)}, f32[72,128]{1,0:T(8,128)S(1)}, u32[]{:S(2)}, u32[]{:S(2)}) %collective-permute-start.1) | collective-permute-done | bytes 36896 | tf_op jit(solution)/shard_map/ppermute | solution.py:460
  10.5 0.4 %shard_map.89 = (f32[144,384]{1,0:T(8,128)S(1)}, f32[128,384]{1,0:T(8,128)S(1)}, f32[8,384]{1,0:T(8,128)S(1)}, f32[56,384]{1,0:T(8,128)S(1)}, f32[56,384]{1,0:T(8,128)S(1)}) custom-call(f32[8,384]{1,0:T(8,128)S(1)} %get-tuple-element.28.own_used, f32[144,384]{1,0:T(8,128)S(1)} %shard_map.87.partial, f32[128,256]{1,0:T(8,128)S(1)} %get-tuple-element.30.target, ...), custom_call_target="tpu_custom_call" | custom-call | tf_op jit(solution)/shard_map/pallas_call | solution.py:539
  10.9 0.1 collective-permute-start.2
  11.0 1.6 %collective-permute-start.3 = (f32[56,384]{1,0:T(8,128)S(1)}, f32[56,384]{1,0:T(8,128)S(1)}, u32[]{:S(2)}, u32[]{:S(2)}) collective-permute-start(f32[56,384]{1,0:T(8,128)S(1)} %get-tuple-element.39), channel_id=1, source_target_pairs={{0,16},{4,8},{8,4},{12,28},{16,0},{20,24},{24,20},{28,12},{1,17},{... | collective-permute-start | bytes 258056 | tf_op jit(solution)/shard_map/ppermute | solution.py:460
  12.6 2.8 %shard_map.90 = (bf16[2816,512]{1,0:T(8,128)(2,1)S(1)}, bf16[144,2816]{1,0:T(8,128)(2,1)S(1)}, bf16[144,2816]{1,0:T(8,128)(2,1)S(1)}) custom-call(f32[8,2,33]{2,1,0:T(2,128)S(1)} %get-tuple-element.40.row_taps, f32[8,128]{1,0:T(8,128)S(1)} %get-tuple-element.27.weights), custom_call_target="tpu_custom_call" | custom-call | tf_op jit(solution)/shard_map/pallas_call | solution.py:527
  15.4 0.1 collective-permute-done.3.second
  15.5 9.0 %shard_map.91 = (bf16[6,144,256]{2,1,0:T(8,128)(2,1)S(1)}, f32[144,384]{1,0:T(8,128)S(1)}, f32[16,32]{1,0:T(8,128)S(1)}) custom-call(f32[8,128]{1,0:T(8,128)S(1)} %get-tuple-element.27.weights, f32[144,384]{1,0:T(8,128)S(1)} %get-tuple-element.35.logits, f32[128,384]{1,0:T(8,128)S(1)} %get-tuple-element.36.aim, f32[8,384]{1,0:T(8,128)S(1)} %get-tuple-element.37.occupied, ...), custom_call_target="tpu_custom_call" | custom-call | tf_op jit(solution)/shard_map/pallas_call | solution.py:552
  24.5 1.1 %collective-permute-start.6 = (f32[16,32]{1,0:T(8,128)S(1)}, f32[16,32]{1,0:T(8,128)S(1)}, u32[]{:S(2)}, u32[]{:S(2)}) collective-permute-start(f32[16,32]{1,0:T(8,128)S(1)} %get-tuple-element.48), channel_id=1, source_target_pairs={{0,12},{4,8},{8,4},{12,0},{1,13},{5,9},{9,5},{13,1},{2,14},{6,10},... | collective-permute-start | bytes 6152 | tf_op jit(solution)/shard_map/ppermute | solution.py:466
  25.7 0.7 %collective-permute-start.5 = (f32[16,32]{1,0:T(8,128)S(1)}, f32[16,32]{1,0:T(8,128)S(1)}, u32[]{:S(2)}, u32[]{:S(2)}) collective-permute-start(f32[16,32]{1,0:T(8,128)S(1)} %get-tuple-element.48), channel_id=1, source_target_pairs={{0,8},{4,12},{8,0},{12,4},{1,9},{5,13},{9,1},{13,5},{2,10},{6,14},... | collective-permute-start | bytes 6152 | tf_op jit(solution)/shard_map/ppermute | solution.py:466
  26.3 0.1 collective-permute-start.4
  26.4 1.2 %collective-permute-done.6 = f32[16,32]{1,0:T(8,128)S(1)} collective-permute-done((f32[16,32]{1,0:T(8,128)S(1)}, f32[16,32]{1,0:T(8,128)S(1)}, u32[]{:S(2)}, u32[]{:S(2)}) %collective-permute-start.6) | collective-permute-done | bytes 2080 | tf_op jit(solution)/shard_map/ppermute | solution.py:466
  27.6 1.7 %collective-permute-done.5 = f32[16,32]{1,0:T(8,128)S(1)} collective-permute-done((f32[16,32]{1,0:T(8,128)S(1)}, f32[16,32]{1,0:T(8,128)S(1)}, u32[]{:S(2)}, u32[]{:S(2)}) %collective-permute-start.5) | collective-permute-done | bytes 2080 | tf_op jit(solution)/shard_map/ppermute | solution.py:466
  29.4 2.5 %collective-permute-start.9 = (f32[16,32]{1,0:T(8,128)S(1)}, f32[16,32]{1,0:T(8,128)S(1)}, u32[]{:S(2)}, u32[]{:S(2)}) collective-permute-start(f32[16,32]{1,0:T(8,128)S(1)} %add_add_fusion), channel_id=1, source_target_pairs={{0,3},{1,2},{2,1},{3,0},{4,7},{5,6},{6,5},{7,4},{8,11},{9,10},{10,... | collective-permute-start | bytes 6152 | tf_op jit(solution)/shard_map/ppermute | solution.py:466
  31.9 0.3 collective-permute-start.8
  32.2 1.7 %collective-permute-start.7 = (f32[16,32]{1,0:T(8,128)S(1)}, f32[16,32]{1,0:T(8,128)S(1)}, u32[]{:S(2)}, u32[]{:S(2)}) collective-permute-start(f32[16,32]{1,0:T(8,128)S(1)} %add_add_fusion), channel_id=1, source_target_pairs={{0,1},{1,0},{2,3},{3,2},{4,5},{5,4},{6,7},{7,6},{8,9},{9,8},{10,11... | collective-permute-start | bytes 6152 | tf_op jit(solution)/shard_map/ppermute | solution.py:466
  33.8 2.2 %shard_map.92 = bf16[32,128,256]{2,1,0:T(8,128)(2,1)} custom-call(bf16[512,128]{1,0:T(8,128)(2,1)S(1)} %get-tuple-element.49.table, bf16[6,144,256]{2,1,0:T(8,128)(2,1)S(1)} %get-tuple-element.50.shifted, f32[144,384]{1,0:T(8,128)S(1)} %get-tuple-element.51.exact), custom_call_target="tpu_custom_call" | custom-call | tf_op jit(solution)/shard_map/pallas_call | solution.py:568
  36.0 0.4 %collective-permute-done.8 = f32[16,32]{1,0:T(8,128)S(1)} collective-permute-done((f32[16,32]{1,0:T(8,128)S(1)}, f32[16,32]{1,0:T(8,128)S(1)}, u32[]{:S(2)}, u32[]{:S(2)}) %collective-permute-start.8) | collective-permute-done | bytes 2080 | tf_op jit(solution)/shard_map/ppermute | solution.py:466
  36.4 0.0 collective-permute-done.7
  36.5 0.6 %reshape.7 = f32[32,3,3]{0,2,1:T(4,128)} reshape(f32[32,9]{0,1:T(8,128)S(1)} %fusion.1) | data formatting | bytes 2304 | tf_op jit(solution)/shard_map/reshape | solution.py:582
  (6 shorter events, 0.0 us)
Async XLA Ops:
  3.4 6.7 %collective-permute-start = (f32[72,128]{1,0:T(8,128)S(1)}, f32[72,128]{1,0:T(8,128)S(1)}, u32[]{:S(2)}, u32[]{:S(2)}) collective-permute-start(f32[72,128]{1,0:T(8,128)S(1)} %get-tuple-element.31), channel_id=1, source_target_pairs={{0,1},{1,0},{2,3},{3,2},{4,5},{5,4},{6,7},{7,6},{8,9},{9,8},{10,11... | collective-permute-start | bytes 110600 | tf_op jit(solution)/shard_map/ppermute | solution.py:449
  6.5 4.0 %collective-permute-start.1 = (f32[72,128]{1,0:T(8,128)S(1)}, f32[72,128]{1,0:T(8,128)S(1)}, u32[]{:S(2)}, u32[]{:S(2)}) collective-permute-start(f32[72,128]{1,0:T(8,128)S(1)} %get-tuple-element.32), channel_id=1, source_target_pairs={{0,16},{1,2},{2,1},{3,19},{16,0},{17,18},{18,17},{19,3},{4,20},{5,... | collective-permute-start | bytes 110600 | tf_op jit(solution)/shard_map/ppermute | solution.py:460
  10.9 4.5 %collective-permute-start.2 = (f32[56,384]{1,0:T(8,128)S(1)}, f32[56,384]{1,0:T(8,128)S(1)}, u32[]{:S(2)}, u32[]{:S(2)}) collective-permute-start(f32[56,384]{1,0:T(8,128)S(1)} %get-tuple-element.38), channel_id=1, source_target_pairs={{0,4},{4,0},{8,12},{12,8},{1,5},{5,1},{9,13},{13,9},{2,6},{6,2},{1... | collective-permute-start | bytes 258056 | tf_op jit(solution)/shard_map/ppermute | solution.py:449
  11.0 4.6 %collective-permute-start.3 = (f32[56,384]{1,0:T(8,128)S(1)}, f32[56,384]{1,0:T(8,128)S(1)}, u32[]{:S(2)}, u32[]{:S(2)}) collective-permute-start(f32[56,384]{1,0:T(8,128)S(1)} %get-tuple-element.39), channel_id=1, source_target_pairs={{0,16},{4,8},{8,4},{12,28},{16,0},{20,24},{24,20},{28,12},{1,17},{... | collective-permute-start | bytes 258056 | tf_op jit(solution)/shard_map/ppermute | solution.py:460
  24.5 3.1 %collective-permute-start.6 = (f32[16,32]{1,0:T(8,128)S(1)}, f32[16,32]{1,0:T(8,128)S(1)}, u32[]{:S(2)}, u32[]{:S(2)}) collective-permute-start(f32[16,32]{1,0:T(8,128)S(1)} %get-tuple-element.48), channel_id=1, source_target_pairs={{0,12},{4,8},{8,4},{12,0},{1,13},{5,9},{9,5},{13,1},{2,14},{6,10},... | collective-permute-start | bytes 6152 | tf_op jit(solution)/shard_map/ppermute | solution.py:466
  25.7 3.7 %collective-permute-start.5 = (f32[16,32]{1,0:T(8,128)S(1)}, f32[16,32]{1,0:T(8,128)S(1)}, u32[]{:S(2)}, u32[]{:S(2)}) collective-permute-start(f32[16,32]{1,0:T(8,128)S(1)} %get-tuple-element.48), channel_id=1, source_target_pairs={{0,8},{4,12},{8,0},{12,4},{1,9},{5,13},{9,1},{13,5},{2,10},{6,14},... | collective-permute-start | bytes 6152 | tf_op jit(solution)/shard_map/ppermute | solution.py:466
  26.3 3.0 %collective-permute-start.4 = (f32[16,32]{1,0:T(8,128)S(1)}, f32[16,32]{1,0:T(8,128)S(1)}, u32[]{:S(2)}, u32[]{:S(2)}) collective-permute-start(f32[16,32]{1,0:T(8,128)S(1)} %get-tuple-element.48), channel_id=1, source_target_pairs={{0,4},{4,0},{8,12},{12,8},{1,5},{5,1},{9,13},{13,9},{2,6},{6,2},{1... | collective-permute-start | bytes 6152 | tf_op jit(solution)/shard_map/ppermute | solution.py:466
  29.4 6.6 %collective-permute-start.9 = (f32[16,32]{1,0:T(8,128)S(1)}, f32[16,32]{1,0:T(8,128)S(1)}, u32[]{:S(2)}, u32[]{:S(2)}) collective-permute-start(f32[16,32]{1,0:T(8,128)S(1)} %add_add_fusion), channel_id=1, source_target_pairs={{0,3},{1,2},{2,1},{3,0},{4,7},{5,6},{6,5},{7,4},{8,11},{9,10},{10,... | collective-permute-start | bytes 6152 | tf_op jit(solution)/shard_map/ppermute | solution.py:466
  31.9 4.5 %collective-permute-start.8 = (f32[16,32]{1,0:T(8,128)S(1)}, f32[16,32]{1,0:T(8,128)S(1)}, u32[]{:S(2)}, u32[]{:S(2)}) collective-permute-start(f32[16,32]{1,0:T(8,128)S(1)} %add_add_fusion), channel_id=1, source_target_pairs={{0,2},{1,3},{2,0},{3,1},{4,6},{5,7},{6,4},{7,5},{8,10},{9,11},{10,... | collective-permute-start | bytes 6152 | tf_op jit(solution)/shard_map/ppermute | solution.py:466
  32.2 4.3 %collective-permute-start.7 = (f32[16,32]{1,0:T(8,128)S(1)}, f32[16,32]{1,0:T(8,128)S(1)}, u32[]{:S(2)}, u32[]{:S(2)}) collective-permute-start(f32[16,32]{1,0:T(8,128)S(1)} %add_add_fusion), channel_id=1, source_target_pairs={{0,1},{1,0},{2,3},{3,2},{4,5},{5,4},{6,7},{7,6},{8,9},{9,8},{10,11... | collective-permute-start | bytes 6152 | tf_op jit(solution)/shard_map/ppermute | solution.py:466
